TPU v7x, 128 devices: a whole 4x4x4 slice. The times are simulated.
128 devices in a mesh: lon: 16 (over x, y_hi, core), lat: 8 (over y_lo, z).
Axes of the slice: x: 4, y: 4 (y_hi: 2, y_lo: 2; y = y_hi * 2 + y_lo), z: 4, core: 2. Of those that a mesh axis runs over, the one named last changes fastest.
Arguments:
- air_state: bfloat16 [4, 48, 384, 192], P(None, 'lat', 'lon'), may hold values from -6 to 6
- upstream: bfloat16 [4, 48, 384, 192], P(None, 'lat', 'lon'), may hold values from -6 to 6
- norm_gain: float32 [192], replicated, may hold values from 0.25 to 1.75
- w_qkv: bfloat16 [192, 576], replicated, may hold values from -0.4375 to 0.4375
- w_proj: bfloat16 [192, 192], replicated, may hold values from -0.4375 to 0.4375
- bias_table: float32 [8, 2, 6, 3312], P('lat'), may hold values from -5 to 260
Outputs:
- block_out: bfloat16 [4, 48, 384, 192], P(None, 'lat', 'lon')
- d_state: bfloat16 [4, 48, 384, 192], P(None, 'lat', 'lon')
- d_gain: float32 [192], replicated
- d_wqkv: float32 [192, 576], replicated
- d_wproj: float32 [192, 192], replicated
- d_table: float32 [8, 2, 6, 3312], P('lat')
All inputs are finite; a program needn't handle non-finite values.
Results may differ from a plain program's by a relative error of at most 0.019.
Values may be sent and summed in bfloat16 or wider, within the bound.
No kernel may reach another device: no remote copies, remote signals or barrier semaphores. Data moves between devices by JAX's collectives and lax.ppermute only.
A program may use at most 128 MiB of HBM per device.

v0:
```python
import functools

import jax
import jax.numpy as jnp
from jax import lax
from jax.experimental import pallas as pl
from jax.experimental.pallas import tpu as pltpu
from jax.sharding import PartitionSpec as P

HEADS = 6
HEAD = 32
WLEV = 2
WLAT = 6
WLON = 12
WIN = 144
POS = WLEV * WLAT
REL = 2 * WLON - 1
C = 192
TOK = 576
WROWS = 80
TROWS = 32
CHUNK = WROWS + TROWS

epsilon = 1e-05
masked_score = -1000000000.0
f32 = jnp.float32
bf16 = jnp.bfloat16

NN = (((1,), (0,)), ((), ()))
NT = (((1,), (1,)), ((), ()))
TN = (((0,), (0,)), ((), ()))


def dot(a, b, dims):
    return lax.dot_general(a, b, dims, preferred_element_type=f32)


def window_parts():
    for a in range(2):
        for s in range(WLEV):
            for lat in range(WLAT):
                p = s * WLAT + lat
                yield (2 * a + s + 1) % 4, lat, a * 2 * WIN + p, (a * 2 + 1) * WIN + p


def put(dst, start, rows):
    n = rows.shape[0]
    dst[pl.ds(start, n, stride=POS), :] = rows[:, :128]
    high = jnp.concatenate([rows[:, 128:], jnp.zeros((n, 64), f32)], axis=1)
    dst[pl.ds(TOK + start, n, stride=POS), :] = high


def get(src, start):
    low = src[pl.ds(start, WLON, stride=POS), :]
    high = src[pl.ds(TOK + start, WLON, stride=POS), :]
    return jnp.concatenate([low, high[:, :64]], axis=1).astype(bf16)


def whole_rows(src):
    return jnp.concatenate([src[:TOK], src[TOK:][:, :64]], axis=1)


def hold(dst, rows):
    dst[:TOK] = rows[:, :128]
    dst[TOK:, :64] = rows[:, 128:]


def main_kernel(
    last_ref, air_ref, up_ref, lonh_ref, lath_ref, corh_ref, gain_ref, wqkv_ref, wproj_ref, tab_ref,
    own_ref, lono_ref, lato_ref, coro_ref, grad_ref,
    xt, ut, bias, dbias, q_s, k_s, v_s, dm_s, mix_s, dq_s, dk_s, dv_s, gw, gt,
):
    for i, (src, dst) in enumerate(((air_ref, xt), (up_ref, ut))):
        for lev, lat, w0, w1 in window_parts():
            if lat < 3:
                row = src[lev, lat + 3].astype(f32)
                first, second = row[6:18], row[18:24]
                third = lonh_ref[i, lev, lat].astype(f32)
            else:
                row = lath_ref[i, lev, lat - 3].astype(f32)
                first, second = row[0:12], row[12:18]
                third = corh_ref[i, lev, lat - 3].astype(f32)
            put(dst, w0, first)
            put(dst, w1, second)
            put(dst, w1 + 72, third)

    for a in range(2):
        for h in range(HEADS):
            rows = pl.ds((a * HEADS + h) * POS, POS)
            for lon in range(WLON):
                bias[a, lon * POS : (lon + 1) * POS, h * WIN : (h + 1) * WIN] = tab_ref[
                    rows, (11 - lon) * POS : (11 - lon) * POS + WIN
                ]
    is_last = last_ref[0]
    for a in range(2):
        pj = lax.broadcasted_iota(jnp.int32, (WIN, 1), 0) % POS
        pi = lax.broadcasted_iota(jnp.int32, (1, HEADS * WIN), 1) % POS

        def region(p):
            lev_part = jnp.where(p >= WLAT, 2 * a, 0)
            lat_part = jnp.where((p % WLAT) >= WLAT // 2, is_last, 0)
            return lev_part + lat_part

        bias[a] = jnp.where(region(pj) == region(pi), bias[a], masked_score)
    dbias[...] = jnp.zeros_like(dbias)

    x = whole_rows(xt)
    mean = jnp.sum(x, axis=1, keepdims=True) * (1.0 / C)
    centred = x - mean
    var = jnp.sum(centred * centred, axis=1, keepdims=True) * (1.0 / C)
    rstd = lax.rsqrt(var + epsilon)
    gain = gain_ref[...]
    normed = (centred * rstd * gain).astype(bf16)
    for part, dst in enumerate((q_s, k_s, v_s)):
        dst[...] = dot(normed, wqkv_ref[:, part * C : (part + 1) * C], NN).astype(bf16)
    up = whole_rows(ut).astype(bf16)
    dm_s[...] = dot(up, wproj_ref[...], NT).astype(bf16)

    scale = HEAD**-0.5
    lane_head = lax.broadcasted_iota(jnp.int32, (1, C), 1) // HEAD

    def spread(rows):
        zero = jnp.zeros_like(rows)
        return jnp.concatenate([jnp.where(lane_head == h, rows, zero) for h in range(HEADS)], axis=0)

    def gathered(stacked):
        total = stacked[0:WIN]
        for h in range(1, HEADS):
            total = jnp.where(lane_head == h, stacked[h * WIN : (h + 1) * WIN], total)
        return total

    def window(w, carry):
        a = w // 2
        rows = pl.ds(pl.multiple_of(w * WIN, 16), WIN)
        k, v = k_s[rows, :], v_s[rows, :]
        qs = spread(q_s[rows, :])
        scores = dot(k, qs, NT) * scale + bias[a]
        top = jnp.max(scores, axis=0, keepdims=True)
        weights = jnp.exp(scores - top)
        probs = weights * (1.0 / jnp.sum(weights, axis=0, keepdims=True))
        soft = probs.astype(bf16)
        mix_s[rows, :] = gathered(dot(soft, v, TN)).astype(bf16)
        ds = spread(dm_s[rows, :])
        dprobs = dot(v, ds, NT)
        dv_s[rows, :] = dot(soft, ds, NN).astype(bf16)
        inner = jnp.sum(probs * dprobs, axis=0, keepdims=True)
        dscores = probs * (dprobs - inner)
        dbias[a] += dscores
        dsc = dscores.astype(bf16)
        dk_s[rows, :] = (dot(dsc, qs, NN) * scale).astype(bf16)
        dq_s[rows, :] = (gathered(dot(dsc, k, TN)) * scale).astype(bf16)
        return carry

    lax.fori_loop(0, 4, window, 0)

    mix = mix_s[...]
    dq, dk, dv = dq_s[...], dk_s[...], dv_s[...]
    mats = [dot(normed, d, TN) for d in (dq, dk, dv)] + [dot(mix, up, TN)]
    for t, m in enumerate(mats):
        gw[t * C : (t + 1) * C, :] = m[:, 0:128].astype(bf16)
    for t in range(2):
        both = jnp.concatenate([mats[2 * t][:, 128:192], mats[2 * t + 1][:, 128:192]], axis=1)
        gw[(4 + t) * C : (5 + t) * C, :] = both.astype(bf16)

    branch = dot(mix, wproj_ref[...], NN).astype(bf16).astype(f32)
    dnorm = (
        dot(dq, wqkv_ref[:, 0:C], NT)
        + dot(dk, wqkv_ref[:, C : 2 * C], NT)
        + dot(dv, wqkv_ref[:, 2 * C : 3 * C], NT)
    )
    xhat = centred * rstd
    dgain = jnp.sum(dnorm * xhat, axis=0, keepdims=True)
    dhat = dnorm * gain
    m1 = jnp.sum(dhat, axis=1, keepdims=True) * (1.0 / C)
    m2 = jnp.sum(dhat * xhat, axis=1, keepdims=True) * (1.0 / C)
    dx = rstd * (dhat - m1 - xhat * m2)
    gw[6 * C :, :] = jnp.zeros((16 * WROWS - 6 * C, 128), bf16)
    row_of = lax.broadcasted_iota(jnp.int32, (16, 128), 0)
    dg0 = dgain[:, 0:128]
    dg1 = jnp.concatenate([dgain[:, 128:192], jnp.zeros((1, 64), f32)], axis=1)
    gw[6 * C : 6 * C + 16, :] = jnp.where(
        row_of == 0, dg0, jnp.where(row_of == 1, dg1, jnp.zeros((16, 128), f32))
    ).astype(bf16)

    hold(xt, branch)
    hold(ut, dx)
    for i, src in enumerate((xt, ut)):
        for lev, lat, w0, w1 in window_parts():
            first = get(src, w0)
            rest = get(src, w1)
            if lat < 3:
                own_ref[i, lev, lat, 0:12] = first
                own_ref[i, lev, lat, 12:18] = rest[0:6]
                lono_ref[i, lev, lat] = rest[6:12]
            else:
                lato_ref[i, lev, lat - 3, 0:12] = first
                lato_ref[i, lev, lat - 3, 12:18] = rest[0:6]
                coro_ref[i, lev, lat - 3] = rest[6:12]

    gt[...] = jnp.zeros_like(gt)
    for a in range(2):
        for h in range(HEADS):
            rows = pl.ds((a * HEADS + h) * POS, POS)
            for lon in range(WLON):
                gt[rows, (11 - lon) * POS : (11 - lon) * POS + WIN] += dbias[
                    a, lon * POS : (lon + 1) * POS, h * WIN : (h + 1) * WIN
                ]
    gtb = gt[...].astype(bf16)
    table_rows = jnp.concatenate(
        [gtb[:, 0:128], gtb[:, 128:256], gtb[:, 256:384], jnp.zeros((80, 128), bf16)], axis=0
    )
    for i in range(16):
        grad_ref[i, 0:WROWS] = gw[i * WROWS : (i + 1) * WROWS, :]
        grad_ref[i, WROWS:CHUNK] = table_rows[i * TROWS : (i + 1) * TROWS]


def run_main(last, air, up, lonh, lath, corh, gain, wqkv, wproj, tab):
    vmem = pl.BlockSpec(memory_space=pltpu.VMEM)
    smem = pl.BlockSpec(memory_space=pltpu.SMEM)
    tok = lambda dt: pltpu.VMEM((TOK, C), dt)
    return pl.pallas_call(
        main_kernel,
        in_specs=[smem] + [vmem] * 9,
        out_specs=[vmem] * 5,
        out_shape=[
            jax.ShapeDtypeStruct((2, 4, 3, 18, C), bf16),
            jax.ShapeDtypeStruct((2, 4, 3, 6, C), bf16),
            jax.ShapeDtypeStruct((2, 4, 3, 18, C), bf16),
            jax.ShapeDtypeStruct((2, 4, 3, 6, C), bf16),
            jax.ShapeDtypeStruct((16, CHUNK, 128), bf16),
        ],
        scratch_shapes=[
            pltpu.VMEM((2 * TOK, 128), f32),
            pltpu.VMEM((2 * TOK, 128), f32),
            pltpu.VMEM((2, WIN, HEADS * WIN), f32),
            pltpu.VMEM((2, WIN, HEADS * WIN), f32),
        ]
        + [tok(bf16)] * 8
        + [pltpu.VMEM((16 * WROWS, 128), bf16), pltpu.VMEM((WIN, 384), f32)],
        compiler_params=pltpu.CompilerParams(vmem_limit_bytes=48 << 20),
        name="sublayer",
    )(last, air, up, lonh, lath, corh, gain, wqkv, wproj, tab)


def neighbour(array, lon_by, lat_by):
    lons, lats = lax.axis_size("lon"), lax.axis_size("lat")
    if lat_by == 0:
        return lax.ppermute(array, "lon", [(i, (i + lon_by) % lons) for i in range(lons)])
    if lon_by == 0:
        return lax.ppermute(array, "lat", [(i, (i + lat_by) % lats) for i in range(lats)])
    pairs = [
        (i * lats + j, ((i + lon_by) % lons) * lats + (j + lat_by) % lats)
        for i in range(lons)
        for j in range(lats)
    ]
    return lax.ppermute(array, ("lon", "lat"), pairs)


def each(array, axis):
    copies = jnp.broadcast_to(array, (lax.axis_size(axis), *array.shape))
    return lax.all_to_all(copies, axis, split_axis=0, concat_axis=0, tiled=True)


def summed(array):
    return jnp.sum(array.astype(f32), axis=0).astype(bf16)


def on_device(air, up, gain, wqkv, wproj, table):
    both = jnp.stack([air, up])
    lonh = neighbour(both[:, :, 3:6, 0:6], -1, 0)
    lath = neighbour(both[:, :, 0:3, 6:24], 0, -1)
    corh = neighbour(both[:, :, 0:3, 0:6], -1, -1)
    last = (lax.axis_index("lat") == lax.axis_size("lat") - 1).astype(jnp.int32).reshape(1)
    tab = table.reshape(12, POS, POS, REL)[:, :, :, ::-1].transpose(0, 2, 3, 1)
    tab = tab.reshape(12 * POS, REL * POS)
    own, lono, lato, coro, grads = run_main(
        last, air, up, lonh, lath, corh, gain.reshape(1, C), wqkv, wproj, tab
    )
    lonr = neighbour(lono, 1, 0)
    latr = neighbour(lato, 0, 1)
    corr = neighbour(coro, 1, 1)

    part = summed(lax.all_to_all(grads, "lon", split_axis=0, concat_axis=0, tiled=True))
    weights = summed(each(part[:WROWS], "lat"))
    whole = each(jnp.concatenate([weights, part[WROWS:]], axis=0), "lon")

    top = jnp.concatenate([corr, latr], axis=3)
    low = jnp.concatenate([lonr, own], axis=3)
    add = jnp.concatenate([top, low], axis=2).astype(f32)
    block_out = (air.astype(f32) + add[0]).astype(bf16)
    d_state = (up.astype(f32) + add[1]).astype(bf16)

    gw = whole[:, :WROWS].reshape(16 * WROWS, 128).astype(f32)
    tiles = [gw[t * C : (t + 1) * C] for t in range(6)]
    dwq = jnp.concatenate([tiles[0], tiles[4][:, :64]], axis=1)
    dwk = jnp.concatenate([tiles[1], tiles[4][:, 64:]], axis=1)
    dwv = jnp.concatenate([tiles[2], tiles[5][:, :64]], axis=1)
    d_wproj = jnp.concatenate([tiles[3], tiles[5][:, 64:]], axis=1)
    d_wqkv = jnp.concatenate([dwq, dwk, dwv], axis=1)
    d_gain = jnp.concatenate([gw[6 * C], gw[6 * C + 1, :64]])
    gt = whole[:, WROWS:].reshape(16 * TROWS, 128)[: 3 * WIN].reshape(3, WIN, 128)
    gt = gt.transpose(1, 0, 2).reshape(WIN, 384)[:, : REL * POS].astype(f32)
    gt = gt.reshape(12, POS, REL, POS).transpose(0, 3, 1, 2)[:, :, :, ::-1]
    d_table = gt.reshape(1, 2, HEADS, POS * POS * REL)
    return (block_out, d_state, d_gain, d_wqkv, d_wproj, d_table)


def solution(mesh):
    grid = P(None, "lat", "lon", None)
    return jax.shard_map(
        on_device,
        mesh=mesh,
        in_specs=(grid, grid, P(), P(), P(), P("lat", None, None, None)),
        out_specs=(grid, grid, P(), P(), P(), P("lat", None, None, None)),
        check_vma=False,
    )
```

profile of v0, /device:TPU:8, one launch (start us, length us, event | category | flops | bytes accessed | tf_op | source)
XLA Modules:
  0.0 79.0 jit_solution(16661411777977527504)
XLA Ops:
  0.6 1.1 %fusion.4 = bf16[2,4,3,18,192]{4,3,2,1,0:T(8,128)(2,1)S(1)} fusion(bf16[1,4,6,24,192]{4,3,2,1,0:T(8,128)(2,1)} %bitcast.33, bf16[1,4,6,24,192]{4,3,2,1,0:T(8,128)(2,1)} %bitcast.35), kind=kLoop, calls=%fused_computation.10 | loop fusion | flops 82944 | bytes 608256 | tf_op jit(solution)/shard_map/stack | solution.py:269
  1.8 4.0 %collective-permute-start.1 = (bf16[2,4,3,18,192]{4,3,2,1,0:T(8,128)(2,1)S(1)}, bf16[2,4,3,18,192]{4,3,2,1,0:T(8,128)(2,1)S(1)}, u32[]{:S(2)}, u32[]{:S(2)}) collective-permute-start(bf16[2,4,3,18,192]{4,3,2,1,0:T(8,128)(2,1)S(1)} %fusion.4), channel_id=1, source_target_pairs={{0,7},{1,0},{2,1},{3,2},{4,3},{5,4},{6,5},{7,6},{8,15},{9,8},{10,9... | collective-permute-start | bytes 497672 | tf_op jit(solution)/shard_map/ppermute | solution.py:250
  5.8 0.9 %pad_maximum_fusion.1 = (bf16[2,4,3,6,192]{4,3,2,1,0:T(8,128)(2,1)S(1)}, bf16[2,4,3,6,192]{4,3,2,1,0:T(8,128)(2,1)S(1)}) fusion(bf16[1,4,6,24,192]{4,3,2,1,0:T(8,128)(2,1)} %bitcast.36, bf16[1,4,6,24,192]{4,3,2,1,0:T(8,128)(2,1)} %bitcast.34), kind=kLoop, calls=%fused_computation.14 | loop fusion | flops 221184 | bytes 552960 | tf_op jit(solution)/shard_map/stack | solution.py:269
  6.7 3.0 %collective-permute-start.2 = (bf16[2,4,3,6,192]{4,3,2,1,0:T(8,128)(2,1)S(1)}, bf16[2,4,3,6,192]{4,3,2,1,0:T(8,128)(2,1)S(1)}, u32[]{:S(2)}, u32[]{:S(2)}) collective-permute-start(bf16[2,4,3,6,192]{4,3,2,1,0:T(8,128)(2,1)S(1)} %get-tuple-element.44), channel_id=1, source_target_pairs={{0,127},{1,120},{2,121},{3,122},{4,123},{5,124},{6,125},{7,126},{8... | collective-permute-start | bytes 165896 | tf_op jit(solution)/shard_map/ppermute | solution.py:256
  9.6 2.0 %collective-permute-start = (bf16[2,4,3,6,192]{4,3,2,1,0:T(8,128)(2,1)S(1)}, bf16[2,4,3,6,192]{4,3,2,1,0:T(8,128)(2,1)S(1)}, u32[]{:S(2)}, u32[]{:S(2)}) collective-permute-start(bf16[2,4,3,6,192]{4,3,2,1,0:T(8,128)(2,1)S(1)} %get-tuple-element.45), channel_id=1, source_target_pairs={{0,120},{8,0},{16,8},{24,16},{32,24},{40,32},{48,40},{56,48},{64,5... | collective-permute-start | bytes 165896 | tf_op jit(solution)/shard_map/ppermute | solution.py:248
  11.7 0.7 reshape.48
  12.4 0.9 %rev.6 = f32[12,12,12,23]{3,2,1,0:T(8,128)S(1)} reverse(f32[12,12,12,23]{3,2,1,0:T(8,128)S(1)} %reshape.48), dimensions={3} | reverse | bytes 317952 | tf_op jit(solution)/shard_map/rev | solution.py:274
  13.4 2.2 %copy.22 = f32[12,12,23,12]{3,2,1,0:T(8,128)} copy(f32[12,12,23,12]{2,1,3,0:T(8,128)S(1)} %bitcast.39) | data formatting | bytes 317952 | tf_op jit(solution)/shard_map/transpose | solution.py:274
  15.6 2.0 %reshape.49.tab_ref = f32[144,276]{1,0:T(8,128)S(1)} reshape(f32[12,12,23,12]{3,2,1,0:T(8,128)} %copy.22) | data formatting | bytes 317952 | tf_op jit(solution)/shard_map/reshape | solution.py:275
  17.7 7.4 %sublayer.1 = (bf16[2,4,3,18,192]{4,3,2,1,0:T(8,128)(2,1)S(1)}, bf16[2,4,3,6,192]{4,3,2,1,0:T(8,128)(2,1)S(1)}, bf16[2,4,3,18,192]{4,3,2,1,0:T(8,128)(2,1)S(1)},...) custom-call(s32[1]{0:T(128)} %bitcast.last_ref, bf16[4,6,24,192]{3,2,1,0:T(8,128)(2,1)S(1)} %copy-done, ...), custom_call_target="tpu_custom_call" | custom-call | tf_op jit(solution)/shard_map/sublayer/pallas_call | solution.py:221
  25.1 15.8 %all_to_all.15 = bf16[16,112,128]{2,1,0:T(8,128)(2,1)S(1)} all-to-all(bf16[16,112,128]{2,1,0:T(8,128)(2,1)S(1)} %get-tuple-element.15), channel_id=1, replica_groups=mesh['lon'=16,'lat'=8] {'lon'}, dimensions={0} | all-to-all | bytes 917504 | tf_op jit(solution)/shard_map/all_to_all | solution.py:283
  40.9 0.1 reduce_sum.24
  41.0 0.7 broadcast_in_dim.6
  41.7 5.7 %all-to-all-start.1 = ((bf16[8,80,128]{2,1,0:T(8,128)(2,1)}), bf16[8,80,128]{2,1,0:T(8,128)(2,1)S(1)}, u32[]{:S(2)}, u32[]{:S(2)}) async-start(bf16[8,80,128]{2,1,0:T(8,128)(2,1)} %broadcast_in_dim.6), calls=%async_computation.1 | async-start | bytes 327680 | tf_op jit(solution)/shard_map/all_to_all | solution.py:261
  47.4 1.5 %collective-permute-start.4 = (bf16[2,4,3,18,192]{4,3,2,1,0:T(8,128)(2,1)S(1)}, bf16[2,4,3,18,192]{4,3,2,1,0:T(8,128)(2,1)S(1)}, u32[]{:S(2)}, u32[]{:S(2)}) collective-permute-start(bf16[2,4,3,18,192]{4,3,2,1,0:T(8,128)(2,1)S(1)} %get-tuple-element.12), channel_id=1, source_target_pairs={{0,1},{1,2},{2,3},{3,4},{4,5},{5,6},{6,7},{7,0},{8,9},{9,10},{10,1... | collective-permute-start | bytes 497672 | tf_op jit(solution)/shard_map/ppermute | solution.py:250
  48.8 1.4 %collective-permute-start.5 = (bf16[2,4,3,6,192]{4,3,2,1,0:T(8,128)(2,1)S(1)}, bf16[2,4,3,6,192]{4,3,2,1,0:T(8,128)(2,1)S(1)}, u32[]{:S(2)}, u32[]{:S(2)}) collective-permute-start(bf16[2,4,3,6,192]{4,3,2,1,0:T(8,128)(2,1)S(1)} %get-tuple-element.13), channel_id=1, source_target_pairs={{0,8},{8,16},{16,24},{24,32},{32,40},{40,48},{48,56},{56,64},{64,7... | collective-permute-start | bytes 165896 | tf_op jit(solution)/shard_map/ppermute | solution.py:248
  50.2 3.1 %all-to-all-done.1 = bf16[8,80,128]{2,1,0:T(8,128)(2,1)S(1)} async-done(((bf16[8,80,128]{2,1,0:T(8,128)(2,1)}), bf16[8,80,128]{2,1,0:T(8,128)(2,1)S(1)}, u32[]{:S(2)}, u32[]{:S(2)}) %all-to-all-start.1) | async-done | bytes 163872 | tf_op jit(solution)/shard_map/all_to_all | solution.py:261
  53.3 0.8 %broadcast_in_dim.7 = bf16[16,112,128]{2,1,0:T(8,128)(2,1)} broadcast(bf16[112,128]{1,0:T(8,128)(2,1)S(1)} %pad_maximum_fusion.3), dimensions={1,2} | broadcast | bytes 487424 | tf_op jit(solution)/shard_map/broadcast_in_dim | solution.py:260
  54.2 5.2 %all-to-all-start.2 = ((bf16[16,112,128]{2,1,0:T(8,128)(2,1)}), bf16[16,112,128]{2,1,0:T(8,128)(2,1)S(1)}, u32[]{:S(2)}, u32[]{:S(2)}) async-start(bf16[16,112,128]{2,1,0:T(8,128)(2,1)} %broadcast_in_dim.7), calls=%async_computation.2 | async-start | bytes 917504 | tf_op jit(solution)/shard_map/all_to_all | solution.py:261
  59.4 0.2 maximum_convert_fusion
  59.7 1.0 %fusion.1 = (bf16[4,6,24,192]{3,2,1,0:T(8,128)(2,1)}, bf16[4,6,24,192]{3,2,1,0:T(8,128)(2,1)}) fusion(f32[2,4,6,24,192]{4,3,2,1,0:T(8,128)S(1)} %maximum_convert_fusion, bf16[4,6,24,192]{3,2,1,0:T(8,128)(2,1)S(1)} %copy-done.1, bf16[4,6,24,192]{3,2,1,0:T(8,128)(2,1)S(1)} %copy-done), kind=kLoop, calls=%fused_computation.2 | loop fusion | flops 663552 | bytes 1769472 | tf_op jit(solution)/shard_map/convert_element_type | solution.py:291
  60.6 10.5 %all-to-all-done.2 = bf16[16,112,128]{2,1,0:T(8,128)(2,1)S(1)} async-done(((bf16[16,112,128]{2,1,0:T(8,128)(2,1)}), bf16[16,112,128]{2,1,0:T(8,128)(2,1)S(1)}, u32[]{:S(2)}, u32[]{:S(2)}) %all-to-all-start.2) | async-done | bytes 458784 | tf_op jit(solution)/shard_map/all_to_all | solution.py:261
  71.2 0.8 %fusion.6 = (f32[192,64]{1,0:T(8,128)}, f32[192,64]{1,0:T(8,128)}, f32[192,64]{1,0:T(8,128)}, f32[192,64]{1,0:T(8,128)}) fusion(f32[1280,128]{1,0:T(8,128)S(1)} %bitcast_convert_fusion), kind=kLoop, calls=%fused_computation.21 | loop fusion | bytes 393216 | tf_op jit(solution)/shard_map/slice | solution.py:298
  72.0 0.7 fusion.5
  72.8 0.6 reshape.58
  73.4 0.7 rev.7
  74.1 1.4 %copy.24 = f32[12,12,12,23]{3,2,1,0:T(8,128)S(1)} copy(f32[12,12,12,23]{1,3,2,0:T(8,128)S(1)} %rev.7) | data formatting | bytes 317952 | tf_op jit(solution)/shard_map/rev | solution.py:303
  75.5 0.5 reshape.54
  76.0 0.7 copy.25
  76.8 0.6 pad_maximum_fusion.4
  77.3 0.7 pad_maximum_fusion
  78.1 0.9 %concatenate.26 = f32[192,576]{1,0:T(8,128)} concatenate(f32[192,128]{1,0:T(8,128)S(1)} %copy-done.10, f32[192,64]{1,0:T(8,128)S(1)} %copy-done.7, f32[192,128]{1,0:T(8,128)S(1)} %copy-done.9, f32[192,64]{1,0:T(8,128)S(1)} %copy-done.6, f32[192,128]{1,0:T(8,128)S(1)} %copy-done.8, f32[192,64]{1,0:T(8,128)S(1)} %copy-done.5), dimensions={1} | concatenate | bytes 884736 | tf_op jit(solution)/shard_map/concatenate | solution.py:299
  (48 shorter events, 0.3 us)
Async XLA Ops:
  0.6 11.0 %copy-start.13 = (f32[1,2,6,3312]{3,1,2,0:T(2,128)S(1)}, f32[1,2,6,3312]{3,1,2,0:T(2,128)}, u32[]{:S(2)}) copy-start(f32[1,2,6,3312]{3,1,2,0:T(2,128)} %param.11) | copy-start | bytes 476932
  1.8 15.9 %collective-permute-start.1 = (bf16[2,4,3,18,192]{4,3,2,1,0:T(8,128)(2,1)S(1)}, bf16[2,4,3,18,192]{4,3,2,1,0:T(8,128)(2,1)S(1)}, u32[]{:S(2)}, u32[]{:S(2)}) collective-permute-start(bf16[2,4,3,18,192]{4,3,2,1,0:T(8,128)(2,1)S(1)} %fusion.4), channel_id=1, source_target_pairs={{0,7},{1,0},{2,1},{3,2},{4,3},{5,4},{6,5},{7,6},{8,15},{9,8},{10,9... | collective-permute-start | bytes 497672 | tf_op jit(solution)/shard_map/ppermute | solution.py:250
  6.7 11.0 %collective-permute-start.2 = (bf16[2,4,3,6,192]{4,3,2,1,0:T(8,128)(2,1)S(1)}, bf16[2,4,3,6,192]{4,3,2,1,0:T(8,128)(2,1)S(1)}, u32[]{:S(2)}, u32[]{:S(2)}) collective-permute-start(bf16[2,4,3,6,192]{4,3,2,1,0:T(8,128)(2,1)S(1)} %get-tuple-element.44), channel_id=1, source_target_pairs={{0,127},{1,120},{2,121},{3,122},{4,123},{5,124},{6,125},{7,126},{8... | collective-permute-start | bytes 165896 | tf_op jit(solution)/shard_map/ppermute | solution.py:256
  9.6 8.0 %collective-permute-start = (bf16[2,4,3,6,192]{4,3,2,1,0:T(8,128)(2,1)S(1)}, bf16[2,4,3,6,192]{4,3,2,1,0:T(8,128)(2,1)S(1)}, u32[]{:S(2)}, u32[]{:S(2)}) collective-permute-start(bf16[2,4,3,6,192]{4,3,2,1,0:T(8,128)(2,1)S(1)} %get-tuple-element.45), channel_id=1, source_target_pairs={{0,120},{8,0},{16,8},{24,16},{32,24},{40,32},{48,40},{56,48},{64,5... | collective-permute-start | bytes 165896 | tf_op jit(solution)/shard_map/ppermute | solution.py:248
  15.6 2.1 %copy-start = (bf16[4,6,24,192]{3,2,1,0:T(8,128)(2,1)S(1)}, bf16[4,6,24,192]{3,2,1,0:T(8,128)(2,1)}, u32[]{:S(2)}) copy-start(bf16[4,6,24,192]{3,2,1,0:T(8,128)(2,1)} %air_ref.1) | copy-start | bytes 663556
  15.6 2.1 %copy-start.1 = (bf16[4,6,24,192]{3,2,1,0:T(8,128)(2,1)S(1)}, bf16[4,6,24,192]{3,2,1,0:T(8,128)(2,1)}, u32[]{:S(2)}) copy-start(bf16[4,6,24,192]{3,2,1,0:T(8,128)(2,1)} %up_ref.1) | copy-start | bytes 663556
  15.6 2.1 %copy-start.2 = (bf16[192,576]{1,0:T(8,128)(2,1)S(1)}, bf16[192,576]{1,0:T(8,128)(2,1)}, u32[]{:S(2)}) copy-start(bf16[192,576]{1,0:T(8,128)(2,1)} %wqkv_ref.1) | copy-start | bytes 663556
  15.6 2.1 %copy-start.3 = (bf16[192,192]{1,0:T(8,128)(2,1)S(1)}, bf16[192,192]{1,0:T(8,128)(2,1)}, u32[]{:S(2)}) copy-start(bf16[192,192]{1,0:T(8,128)(2,1)} %wproj_ref.1) | copy-start | bytes 221188
  15.6 2.1 %copy-start.4 = (f32[192]{0:T(256)S(1)}, f32[192]{0:T(256)}, u32[]{:S(2)}) copy-start(f32[192]{0:T(256)} %param.8) | copy-start | bytes 2308
  41.7 11.6 %all-to-all-start.1 = ((bf16[8,80,128]{2,1,0:T(8,128)(2,1)}), bf16[8,80,128]{2,1,0:T(8,128)(2,1)S(1)}, u32[]{:S(2)}, u32[]{:S(2)}) async-start(bf16[8,80,128]{2,1,0:T(8,128)(2,1)} %broadcast_in_dim.6), calls=%async_computation.1 | async-start | bytes 327680 | tf_op jit(solution)/shard_map/all_to_all | solution.py:261
  47.4 12.1 %collective-permute-start.4 = (bf16[2,4,3,18,192]{4,3,2,1,0:T(8,128)(2,1)S(1)}, bf16[2,4,3,18,192]{4,3,2,1,0:T(8,128)(2,1)S(1)}, u32[]{:S(2)}, u32[]{:S(2)}) collective-permute-start(bf16[2,4,3,18,192]{4,3,2,1,0:T(8,128)(2,1)S(1)} %get-tuple-element.12), channel_id=1, source_target_pairs={{0,1},{1,2},{2,3},{3,4},{4,5},{5,6},{6,7},{7,0},{8,9},{9,10},{10,1... | collective-permute-start | bytes 497672 | tf_op jit(solution)/shard_map/ppermute | solution.py:250
  48.8 10.6 %collective-permute-start.3 = (bf16[2,4,3,6,192]{4,3,2,1,0:T(8,128)(2,1)S(1)}, bf16[2,4,3,6,192]{4,3,2,1,0:T(8,128)(2,1)S(1)}, u32[]{:S(2)}, u32[]{:S(2)}) collective-permute-start(bf16[2,4,3,6,192]{4,3,2,1,0:T(8,128)(2,1)S(1)} %get-tuple-element.11), channel_id=1, source_target_pairs={{0,9},{1,10},{2,11},{3,12},{4,13},{5,14},{6,15},{7,8},{8,17},{9,18... | collective-permute-start | bytes 165896 | tf_op jit(solution)/shard_map/ppermute | solution.py:256
  48.8 10.6 %collective-permute-start.5 = (bf16[2,4,3,6,192]{4,3,2,1,0:T(8,128)(2,1)S(1)}, bf16[2,4,3,6,192]{4,3,2,1,0:T(8,128)(2,1)S(1)}, u32[]{:S(2)}, u32[]{:S(2)}) collective-permute-start(bf16[2,4,3,6,192]{4,3,2,1,0:T(8,128)(2,1)S(1)} %get-tuple-element.13), channel_id=1, source_target_pairs={{0,8},{8,16},{16,24},{24,32},{32,40},{40,48},{48,56},{56,64},{64,7... | collective-permute-start | bytes 165896 | tf_op jit(solution)/shard_map/ppermute | solution.py:248
  54.2 16.9 %all-to-all-start.2 = ((bf16[16,112,128]{2,1,0:T(8,128)(2,1)}), bf16[16,112,128]{2,1,0:T(8,128)(2,1)S(1)}, u32[]{:S(2)}, u32[]{:S(2)}) async-start(bf16[16,112,128]{2,1,0:T(8,128)(2,1)} %broadcast_in_dim.7), calls=%async_computation.2 | async-start | bytes 917504 | tf_op jit(solution)/shard_map/all_to_all | solution.py:261
  75.4 1.9 %copy-start.11 = (f32[192,64]{1,0:T(8,128)S(1)}, f32[192,64]{1,0:T(8,128)}, u32[]{:S(2)}) copy-start(f32[192,64]{1,0:T(8,128)} %get-tuple-element.40) | copy-start | bytes 147460
  75.4 1.9 %copy-start.12 = (f32[192,128]{1,0:T(8,128)S(1)}, f32[192,128]{1,0:T(8,128)}, u32[]{:S(2)}) copy-start(f32[192,128]{1,0:T(8,128)} %get-tuple-element.36) | copy-start | bytes 294916
  75.5 2.6 %copy-start.5 = (f32[192,64]{1,0:T(8,128)S(1)}, f32[192,64]{1,0:T(8,128)}, u32[]{:S(2)}) copy-start(f32[192,64]{1,0:T(8,128)} %get-tuple-element.41) | copy-start | bytes 147460
  75.5 2.6 %copy-start.6 = (f32[192,64]{1,0:T(8,128)S(1)}, f32[192,64]{1,0:T(8,128)}, u32[]{:S(2)}) copy-start(f32[192,64]{1,0:T(8,128)} %get-tuple-element.42) | copy-start | bytes 147460
  75.5 2.6 %copy-start.7 = (f32[192,64]{1,0:T(8,128)S(1)}, f32[192,64]{1,0:T(8,128)}, u32[]{:S(2)}) copy-start(f32[192,64]{1,0:T(8,128)} %get-tuple-element.43) | copy-start | bytes 147460
  75.5 2.6 %copy-start.8 = (f32[192,128]{1,0:T(8,128)S(1)}, f32[192,128]{1,0:T(8,128)}, u32[]{:S(2)}) copy-start(f32[192,128]{1,0:T(8,128)} %get-tuple-element.37) | copy-start | bytes 294916
  75.5 2.5 %copy-start.9 = (f32[192,128]{1,0:T(8,128)S(1)}, f32[192,128]{1,0:T(8,128)}, u32[]{:S(2)}) copy-start(f32[192,128]{1,0:T(8,128)} %get-tuple-element.38) | copy-start | bytes 294916
  75.5 2.5 %copy-start.10 = (f32[192,128]{1,0:T(8,128)S(1)}, f32[192,128]{1,0:T(8,128)}, u32[]{:S(2)}) copy-start(f32[192,128]{1,0:T(8,128)} %get-tuple-element.39) | copy-start | bytes 294916
where the time goes:
time: 79.4 us; the launch traced here: 79 us
  starting transfers between devices  22.8 us (29%)
  blocking collectives  15.8 us (20%)
  local copies, waits for them, and re-layouts  13.9 us (18%)
  waiting for transfers between devices  13.6 us (17%)
  Pallas kernels  7.37 us (9%)
  other arithmetic  4.63 us (6%)
  between operations  0.97 us (1%)
    all_to_all x1, blocking collectives, on_device(): lax.all_to_all(grads, 'lon', split_axis=0, concat_axis=0, tiled=True)  15.8 us
    all_to_all x2, waiting for transfers between devices, each(): return lax.all_to_all(copies, axis, split_axis=0, concat_axis=0, tiled=True)  13.5 us
    all_to_all x2, starting transfers between devices, each(): return lax.all_to_all(copies, axis, split_axis=0, concat_axis=0, tiled=True)  10.9 us
    pallas_call x1, Pallas kernels, run_main(): pl.pallas_call(main_kernel, in_specs=[smem] + [vmem] * 9, out_specs=[vmem...  7.37 us
    ppermute x2, starting transfers between devices, neighbour(): lax.ppermute(array, 'lat', [(i, (i + lat_by) % lats) for i in range(lats)])  5.46 us
    ppermute x2, starting transfers between devices, neighbour(): lax.ppermute(array, 'lon', [(i, (i + lon_by) % lons) for i in range(lons)])  3.41 us
    ppermute x2, starting transfers between devices, neighbour(): return lax.ppermute(array, ('lon', 'lat'), pairs)  2.95 us
    transpose x1, local copies, waits for them, and re-layouts, on_device(): tab = table.reshape(12, POS, POS, REL)[:, :, :, ::-1].transpose(0, 2, 3, 1)  2.2 us
  transfers between devices with their start and end apart: 8, of which 2 were waited for; matrix products, arithmetic and copies ran while one was open for 11% of the time, Pallas kernels for 0%

commit v1 on v0

v1 whole, which is shorter than its diff:
```python
import functools

import jax
import jax.numpy as jnp
from jax import lax
from jax.experimental import pallas as pl
from jax.experimental.pallas import tpu as pltpu
from jax.sharding import PartitionSpec as P

HEADS = 6
HEAD = 32
WLEV = 2
WLAT = 6
WLON = 12
WIN = 144
POS = WLEV * WLAT
REL = 2 * WLON - 1
C = 192
TOK = 576
SHARES = 16
WROWS = 72
GROW = 72
TROW = 76
TROWS = 20
CHUNK = 96
MID = 80
LANES = REL * POS

epsilon = 1e-05
masked_score = -1000000000.0
f32 = jnp.float32
bf16 = jnp.bfloat16

NN = (((1,), (0,)), ((), ()))
NT = (((1,), (1,)), ((), ()))
TN = (((0,), (0,)), ((), ()))


def dot(a, b, dims):
    return lax.dot_general(a, b, dims, preferred_element_type=f32)


def window_parts():
    for a in range(2):
        for s in range(WLEV):
            for lat in range(WLAT):
                p = s * WLAT + lat
                yield (2 * a + s + 1) % 4, lat, a * 2 * WIN + p, (a * 2 + 1) * WIN + p


def put(dst, start, rows):
    n = rows.shape[0]
    dst[pl.ds(start, n, stride=POS), :] = rows[:, :128]
    high = jnp.concatenate([rows[:, 128:], jnp.zeros((n, 64), f32)], axis=1)
    dst[pl.ds(TOK + start, n, stride=POS), :] = high


def get(src, start):
    low = src[pl.ds(start, WLON, stride=POS), :]
    high = src[pl.ds(TOK + start, WLON, stride=POS), :]
    return jnp.concatenate([low, high[:, :64]], axis=1)


def whole_rows(src):
    return jnp.concatenate([src[:TOK], src[TOK:][:, :64]], axis=1)


def hold(dst, rows):
    dst[:TOK] = rows[:, :128]
    dst[TOK:, :64] = rows[:, 128:]


def joined(state, up):
    return jnp.concatenate([state[:, :128], up[:, :128], state[:, 128:], up[:, 128:]], axis=1)


def parted(rows):
    state = jnp.concatenate([rows[:, 0:128], rows[:, 256:320]], axis=1)
    return state, jnp.concatenate([rows[:, 128:256], rows[:, 320:384]], axis=1)


def pack_kernel(air_ref, up_ref, lonh_ref, lath_ref, corh_ref):
    for lev in range(4):
        for r in range(3):
            at = lev * 3 + r
            row = joined(air_ref[lev, r].astype(f32), up_ref[lev, r].astype(f32)).astype(bf16)
            corh_ref[at * 6 : (at + 1) * 6] = row[0:6]
            lath_ref[at * 18 : (at + 1) * 18] = row[6:24]
            row = joined(
                air_ref[lev, r + 3][0:6].astype(f32), up_ref[lev, r + 3][0:6].astype(f32)
            )
            lonh_ref[at * 6 : (at + 1) * 6] = row.astype(bf16)


HALOS = [
    jax.ShapeDtypeStruct((72, 2 * C), bf16),
    jax.ShapeDtypeStruct((216, 2 * C), bf16),
    jax.ShapeDtypeStruct((72, 2 * C), bf16),
]


def pack(air, up):
    vmem = pl.BlockSpec(memory_space=pltpu.VMEM)
    return pl.pallas_call(
        pack_kernel,
        in_specs=[vmem] * 2,
        out_specs=[vmem] * 3,
        out_shape=HALOS,
        name="pack",
    )(air, up)


def normalised(x):
    mean = jnp.sum(x, axis=1, keepdims=True) * (1.0 / C)
    centred = x - mean
    var = jnp.sum(centred * centred, axis=1, keepdims=True) * (1.0 / C)
    rstd = lax.rsqrt(var + epsilon)
    return centred * rstd, rstd


def onehots():
    src = lax.broadcasted_iota(jnp.int32, (384, 384), 0)
    dst = lax.broadcasted_iota(jnp.int32, (384, 384), 1)
    wanted = (dst % POS) * REL + (REL - 1 - dst // POS)
    lanes = ((src == wanted) & (dst < LANES)).astype(f32).astype(bf16)
    to = lax.broadcasted_iota(jnp.int32, (WIN, 192), 0)
    at = lax.broadcasted_iota(jnp.int32, (WIN, 192), 1)
    ah = to // POS
    rows = (at == (to % POS) * 16 + (ah % HEADS) * 2 + ah // HEADS).astype(f32).astype(bf16)
    return lanes, rows


def prep_kernel(last_ref, table_ref, bias, apart, held):
    entries = jnp.concatenate([table_ref[h] for h in range(HEADS)], axis=0)
    apart[...] = jnp.zeros_like(apart)
    for pj in range(POS):
        for pi in range(POS):
            at = (pi * POS + pj) * REL
            apart[pj * 16 : pj * 16 + POS, pi * REL : (pi + 1) * REL] = entries[:, at : at + REL]
    lanes, rows = onehots()
    left = apart[...]
    total = None
    for _ in range(3):
        piece = left.astype(bf16)
        left = left - piece.astype(f32)
        moved = dot(rows, dot(piece, lanes, NN).astype(bf16), NN)
        total = moved if total is None else total + moved
    held[...] = total
    for a in range(2):
        for h in range(HEADS):
            at = (a * HEADS + h) * POS
            for lon in range(WLON):
                bias[a, lon * POS : (lon + 1) * POS, h * WIN : (h + 1) * WIN] = held[
                    at : at + POS, (11 - lon) * POS : (11 - lon) * POS + WIN
                ]
    is_last = last_ref[0]
    for a in range(2):
        pj = lax.broadcasted_iota(jnp.int32, (WIN, 1), 0) % POS
        pi = lax.broadcasted_iota(jnp.int32, (1, HEADS * WIN), 1) % POS

        def region(p):
            lev_part = jnp.where(p >= WLAT, 2 * a, 0)
            lat_part = jnp.where((p % WLAT) >= WLAT // 2, is_last, 0)
            return lev_part + lat_part

        bias[a] = jnp.where(region(pj) == region(pi), bias[a], masked_score)


def prep(last, table):
    vmem = pl.BlockSpec(memory_space=pltpu.VMEM)
    smem = pl.BlockSpec(memory_space=pltpu.SMEM)
    return pl.pallas_call(
        prep_kernel,
        in_specs=[smem, vmem],
        out_specs=vmem,
        out_shape=jax.ShapeDtypeStruct((2, WIN, HEADS * WIN), f32),
        scratch_shapes=[pltpu.VMEM((192, 384), f32), pltpu.VMEM((WIN, 384), f32)],
        compiler_params=pltpu.CompilerParams(vmem_limit_bytes=16 << 20),
        cost_estimate=pl.CostEstimate(flops=10**8, bytes_accessed=2 << 20, transcendentals=0),
        name="prep",
    )(last, table)


def main_kernel(
    air_ref, up_ref, lonh_ref, lath_ref, corh_ref, gain_ref, wqkv_ref, wproj_ref, bias,
    own_ref, lono_ref, lato_ref, coro_ref, grad_ref,
    xt, ut, dbias, q_s, k_s, v_s, dm_s, mix_s, dq_s, dk_s, dv_s, gw, gt, tr, one,
):
    for lev, lat, w0, w1 in window_parts():
        at = lev * 3 + lat % 3
        if lat < 3:
            rows = [src[lev, lat + 3].astype(f32) for src in (air_ref, up_ref)]
            far = parted(lonh_ref[at * 6 : (at + 1) * 6].astype(f32))
            shift = 6
        else:
            rows = parted(lath_ref[at * 18 : (at + 1) * 18].astype(f32))
            far = parted(corh_ref[at * 6 : (at + 1) * 6].astype(f32))
            shift = 0
        for dst, row, edge in zip((xt, ut), rows, far):
            put(dst, w0, row[shift : shift + 12])
            put(dst, w1, row[shift + 12 : shift + 18])
            put(dst, w1 + 72, edge)

    dbias[...] = jnp.zeros_like(dbias)

    x = whole_rows(xt)
    xhat, rstd = normalised(x)
    normed = (xhat * gain_ref[...]).astype(bf16)
    for part, dst in enumerate((q_s, k_s, v_s)):
        dst[...] = dot(normed, wqkv_ref[:, part * C : (part + 1) * C], NN).astype(bf16)
    up = whole_rows(ut).astype(bf16)
    dm_s[...] = dot(up, wproj_ref[...], NT).astype(bf16)

    scale = HEAD**-0.5
    lane_head = lax.broadcasted_iota(jnp.int32, (1, C), 1) // HEAD

    def spread(rows):
        zero = jnp.zeros_like(rows)
        return jnp.concatenate([jnp.where(lane_head == h, rows, zero) for h in range(HEADS)], axis=0)

    def gathered(stacked):
        total = stacked[0:WIN]
        for h in range(1, HEADS):
            total = jnp.where(lane_head == h, stacked[h * WIN : (h + 1) * WIN], total)
        return total

    def window(w, carry):
        a = w // 2
        rows = pl.ds(pl.multiple_of(w * WIN, 16), WIN)
        k, v = k_s[rows, :], v_s[rows, :]
        qs = spread(q_s[rows, :])
        scores = dot(k, qs, NT) * scale + bias[a]
        top = jnp.max(scores, axis=0, keepdims=True)
        weights = jnp.exp(scores - top)
        probs = weights * (1.0 / jnp.sum(weights, axis=0, keepdims=True))
        soft = probs.astype(bf16)
        mix_s[rows, :] = gathered(dot(soft, v, TN)).astype(bf16)
        ds = spread(dm_s[rows, :])
        dprobs = dot(v, ds, NT)
        dv_s[rows, :] = dot(soft, ds, NN).astype(bf16)
        inner = jnp.sum(probs * dprobs, axis=0, keepdims=True)
        dscores = probs * (dprobs - inner)
        dbias[a] += dscores
        dsc = dscores.astype(bf16)
        dk_s[rows, :] = (dot(dsc, qs, NN) * scale).astype(bf16)
        dq_s[rows, :] = (gathered(dot(dsc, k, TN)) * scale).astype(bf16)
        return carry

    lax.fori_loop(0, 4, window, 0)

    mix = mix_s[...]
    mq, mk, mv = (dot(normed, d[...], TN) for d in (dq_s, dk_s, dv_s))
    mp = dot(mix, up, TN)
    wide = lambda m, n: jnp.concatenate([m[:, 128:], n[:, :64]], axis=1)
    tiles = (mq[:, :128], wide(mq, mk), mk[:, 64:], mv[:, :128], wide(mv, mp), mp[:, 64:])
    for t, m in enumerate(tiles):
        gw[t * C : (t + 1) * C, :] = m
    dnorm = (
        dot(dq_s[...], wqkv_ref[:, 0:C], NT)
        + dot(dk_s[...], wqkv_ref[:, C : 2 * C], NT)
        + dot(dv_s[...], wqkv_ref[:, 2 * C : 3 * C], NT)
    )
    dgain = jnp.sum(dnorm * xhat, axis=0, keepdims=True)
    high = jnp.concatenate([dgain[:, 128:192], jnp.zeros((1, 64), f32)], axis=1)

    gt[...] = jnp.zeros_like(gt)
    for a in range(2):
        for h in range(HEADS):
            rows = pl.ds((a * HEADS + h) * POS, POS)
            for lon in range(WLON):
                gt[rows, (11 - lon) * POS : (11 - lon) * POS + WIN] += dbias[
                    a, lon * POS : (lon + 1) * POS, h * WIN : (h + 1) * WIN
                ]
    tr[0:WIN] = gt[:, 0:128]
    tr[WIN : 2 * WIN] = gt[:, 128:256]
    tr[2 * WIN :] = jnp.zeros((SHARES * TROWS - 2 * WIN, 128), f32)
    for g in range(6):
        tr[2 * WIN : 2 * WIN + 24, g * 20 : (g + 1) * 20] = gt[g * 24 : (g + 1) * 24, 256:LANES]

    one[GROW:TROW] = jnp.zeros((TROW - GROW, 128), f32)
    for i in range(SHARES):
        one[0:WROWS] = gw[i * WROWS : (i + 1) * WROWS]
        if i < 3:
            one[GROW : GROW + 1] = (dgain[:, :128], high, jnp.zeros((1, 128), f32))[i]
        one[TROW:CHUNK] = tr[i * TROWS : (i + 1) * TROWS]
        grad_ref[i] = one[...].astype(bf16)

    hold(xt, dot(mix, wproj_ref[...], NN).astype(bf16).astype(f32))
    dhat = dnorm * gain_ref[...]
    m1 = jnp.sum(dhat, axis=1, keepdims=True) * (1.0 / C)
    m2 = jnp.sum(dhat * xhat, axis=1, keepdims=True) * (1.0 / C)
    hold(ut, rstd * (dhat - m1 - xhat * m2))
    for lev, lat, w0, w1 in window_parts():
        at = lev * 3 + lat % 3
        first = joined(get(xt, w0), get(ut, w0)).astype(bf16)
        rest = joined(get(xt, w1), get(ut, w1)).astype(bf16)
        near, far = (own_ref, lono_ref) if lat < 3 else (lato_ref, coro_ref)
        near[at * 18 : at * 18 + 12] = first
        near[at * 18 + 12 : (at + 1) * 18] = rest[0:6]
        far[at * 6 : (at + 1) * 6] = rest[6:12]


def run_main(air, up, lonh, lath, corh, gain, wqkv, wproj, bias):
    vmem = pl.BlockSpec(memory_space=pltpu.VMEM)
    tok = lambda dt: pltpu.VMEM((TOK, C), dt)
    return pl.pallas_call(
        main_kernel,
        in_specs=[vmem] * 9,
        out_specs=[vmem] * 5,
        out_shape=[
            HALOS[1],
            *HALOS,
            jax.ShapeDtypeStruct((SHARES, CHUNK, 128), bf16),
        ],
        scratch_shapes=[
            pltpu.VMEM((2 * TOK, 128), f32),
            pltpu.VMEM((2 * TOK, 128), f32),
            pltpu.VMEM((2, WIN, HEADS * WIN), f32),
        ]
        + [tok(bf16)] * 8
        + [
            pltpu.VMEM((SHARES * WROWS, 128), f32),
            pltpu.VMEM((WIN, 384), f32),
            pltpu.VMEM((SHARES * TROWS, 128), f32),
            pltpu.VMEM((CHUNK, 128), f32),
        ],
        compiler_params=pltpu.CompilerParams(vmem_limit_bytes=40 << 20),
        cost_estimate=pl.CostEstimate(flops=10**9, bytes_accessed=4 << 20, transcendentals=0),
        name="sublayer",
    )(air, up, lonh, lath, corh, gain, wqkv, wproj, bias)


def combine_kernel(air_ref, up_ref, own_ref, lonr_ref, latr_ref, corr_ref, out_ref, grad_ref):
    for lev in range(4):
        for r in range(6):
            at = lev * 3 + r % 3
            far, near = (corr_ref, latr_ref) if r < 3 else (lonr_ref, own_ref)
            far = far[at * 6 : (at + 1) * 6].astype(f32)
            near = near[at * 18 : (at + 1) * 18].astype(f32)
            rows = parted(jnp.concatenate([far, near], axis=0))
            for src, dst, row in zip((air_ref, up_ref), (out_ref, grad_ref), rows):
                dst[lev, r] = (src[lev, r].astype(f32) + row).astype(bf16)


def combine(air, up, own, lonr, latr, corr):
    vmem = pl.BlockSpec(memory_space=pltpu.VMEM)
    return pl.pallas_call(
        combine_kernel,
        in_specs=[vmem] * 6,
        out_specs=[vmem] * 2,
        out_shape=[jax.ShapeDtypeStruct(air.shape, bf16)] * 2,
        compiler_params=pltpu.CompilerParams(vmem_limit_bytes=16 << 20),
        cost_estimate=pl.CostEstimate(flops=10**9, bytes_accessed=4 << 20, transcendentals=0),
        name="combine",
    )(air, up, own, lonr, latr, corr)


def unpack_kernel(whole_ref, dwqkv_ref, dwproj_ref, dgain_ref, dtable_ref, gw, tr, gt, flat):
    for i in range(SHARES):
        one = whole_ref[i].astype(f32)
        gw[i * WROWS : (i + 1) * WROWS] = one[0:WROWS]
        tr[i * TROWS : (i + 1) * TROWS] = one[TROW:CHUNK]
        if i == 0:
            dgain_ref[:, :128] = one[GROW : GROW + 1]
        if i == 1:
            dgain_ref[:, 128:] = one[GROW : GROW + 1, :64]
    tiles = [gw[t * C : (t + 1) * C] for t in range(6)]
    for t in range(4):
        dwqkv_ref[:, t * 128 : (t + 1) * 128] = tiles[t]
    dwqkv_ref[:, 512:576] = tiles[4][:, :64]
    dwproj_ref[...] = jnp.concatenate([tiles[4][:, 64:], tiles[5]], axis=1)

    gt[:, 0:128] = tr[0:WIN]
    gt[:, 128:256] = tr[WIN : 2 * WIN]
    gt[:, 256:384] = jnp.zeros((WIN, 128), f32)
    for g in range(6):
        gt[g * 24 : (g + 1) * 24, 256:LANES] = tr[2 * WIN : 2 * WIN + 24, g * 20 : (g + 1) * 20]
    lanes, rows = onehots()
    moved = dot(dot(rows, gt[...].astype(bf16), TN).astype(bf16), lanes, NT)
    for pj in range(POS):
        for pi in range(POS):
            at = (pi * POS + pj) * REL
            flat[:, at : at + REL] = moved[pj * 16 : (pj + 1) * 16, pi * REL : (pi + 1) * REL]
    for h in range(HEADS):
        dtable_ref[h] = flat[2 * h : 2 * h + 2, 0 : POS * POS * REL]


def unpack(whole):
    vmem = pl.BlockSpec(memory_space=pltpu.VMEM)
    return pl.pallas_call(
        unpack_kernel,
        in_specs=[vmem],
        out_specs=[vmem] * 4,
        out_shape=[
            jax.ShapeDtypeStruct((C, 3 * C), f32),
            jax.ShapeDtypeStruct((C, C), f32),
            jax.ShapeDtypeStruct((1, C), f32),
            jax.ShapeDtypeStruct((HEADS, 2, POS * POS * REL), f32),
        ],
        scratch_shapes=[
            pltpu.VMEM((SHARES * WROWS, 128), f32),
            pltpu.VMEM((SHARES * TROWS, 128), f32),
            pltpu.VMEM((WIN, 384), f32),
            pltpu.VMEM((16, 3328), f32),
        ],
        compiler_params=pltpu.CompilerParams(vmem_limit_bytes=16 << 20),
        name="unpack",
    )(whole)


def neighbour(array, lon_by, lat_by):
    lons, lats = lax.axis_size("lon"), lax.axis_size("lat")
    if lat_by == 0:
        return lax.ppermute(array, "lon", [(i, (i + lon_by) % lons) for i in range(lons)])
    if lon_by == 0:
        return lax.ppermute(array, "lat", [(i, (i + lat_by) % lats) for i in range(lats)])
    pairs = [
        (i * lats + j, ((i + lon_by) % lons) * lats + (j + lat_by) % lats)
        for i in range(lons)
        for j in range(lats)
    ]
    return lax.ppermute(array, ("lon", "lat"), pairs)


def each(array, axis):
    copies = jnp.broadcast_to(array, (lax.axis_size(axis), *array.shape))
    return lax.all_to_all(copies, axis, split_axis=0, concat_axis=0, tiled=True)


def summed(array):
    return jnp.sum(array.astype(f32), axis=0).astype(bf16)


def on_device(air, up, gain, wqkv, wproj, table):
    lonh, lath, corh = pack(air, up)
    lath = neighbour(lath, 0, -1)
    lonh = neighbour(lonh, -1, 0)
    corh = neighbour(corh, -1, -1)
    last = (lax.axis_index("lat") == lax.axis_size("lat") - 1).astype(jnp.int32).reshape(1)
    bias = prep(last, table.transpose(0, 2, 1, 3).reshape(HEADS, 2, POS * POS * REL))
    own, lono, lato, coro, grads = run_main(
        air, up, lonh, lath, corh, gain.reshape(1, C), wqkv, wproj, bias
    )
    latr = neighbour(lato, 0, 1)
    lonr = neighbour(lono, 1, 0)
    corr = neighbour(coro, 1, 1)
    part = summed(lax.all_to_all(grads, "lon", split_axis=0, concat_axis=0, tiled=True))
    part, latr, lonr, corr = lax.optimization_barrier((part, latr, lonr, corr))
    weights = summed(each(part[:MID], "lat"))
    share = jnp.concatenate([weights[:TROW], part[TROW:]], axis=0)
    whole = each(share, "lon")
    block_out, d_state = combine(air, up, own, lonr, latr, corr)
    d_wqkv, d_wproj, d_gain, d_table = unpack(whole)
    d_table = d_table.reshape(1, HEADS, 2, POS * POS * REL).transpose(0, 2, 1, 3)
    return (block_out, d_state, d_gain.reshape(C), d_wqkv, d_wproj, d_table)


def solution(mesh):
    grid = P(None, "lat", "lon", None)
    return jax.shard_map(
        on_device,
        mesh=mesh,
        in_specs=(grid, grid, P(), P(), P(), P("lat", None, None, None)),
        out_specs=(grid, grid, P(), P(), P(), P("lat", None, None, None)),
        check_vma=False,
    )
```

time: 79.4 us -> 74.7 us (0.941)
  the two profiles are of different devices: /device:TPU:8 before, /device:TPU:1 now
where the time goes in v1:
time: 74.7 us; the launch traced here: 74.3 us
  starting transfers between devices  32 us (43%)
  waiting for transfers between devices  25.8 us (35%)
  Pallas kernels  14 us (19%)
  local copies, waits for them, and re-layouts  1.53 us (2%)
  between operations  0.75 us (1%)
    all_to_all x2, waiting for transfers between devices, each(): return lax.all_to_all(copies, axis, split_axis=0, concat_axis=0, tiled=True)  14.6 us
    all_to_all x2, starting transfers between devices, each(): return lax.all_to_all(copies, axis, split_axis=0, concat_axis=0, tiled=True)  11.4 us
    pallas_call x1, Pallas kernels, run_main(): pl.pallas_call(main_kernel, in_specs=[vmem] * 9, out_specs=[vmem] * 5, ou...  7.34 us
    all_to_all x1, starting transfers between devices, on_device(): lax.all_to_all(grads, 'lon', split_axis=0, concat_axis=0, tiled=True)  7.23 us
    all_to_all x1, waiting for transfers between devices, on_device(): lax.all_to_all(grads, 'lon', split_axis=0, concat_axis=0, tiled=True)  6.87 us
    ppermute x2, starting transfers between devices, neighbour(): lax.ppermute(array, 'lat', [(i, (i + lat_by) % lats) for i in range(lats)])  5.6 us
    ppermute x2, starting transfers between devices, neighbour(): lax.ppermute(array, 'lon', [(i, (i + lon_by) % lons) for i in range(lons)])  4.16 us
    ppermute x2, starting transfers between devices, neighbour(): return lax.ppermute(array, ('lon', 'lat'), pairs)  3.66 us
  transfers between devices with their start and end apart: 9, of which 5 were waited for; matrix products, arithmetic and copies ran while one was open for 0% of the time, Pallas kernels for 4%

profile of v1, /device:TPU:1, one launch (start us, length us, event | category | flops | bytes accessed | tf_op | source)
XLA Modules:
  0.0 74.3 jit_solution(1524601283489747369)
XLA Ops:
  0.6 0.0 copy-start.2
  0.6 1.9 %pack.1 = (bf16[72,384]{1,0:T(8,128)(2,1)}, bf16[216,384]{1,0:T(8,128)(2,1)}, bf16[72,384]{1,0:T(8,128)(2,1)}) custom-call(bf16[4,6,24,192]{3,2,1,0:T(8,128)(2,1)} %air_ref.5, bf16[4,6,24,192]{3,2,1,0:T(8,128)(2,1)} %up_ref.5), custom_call_target="tpu_custom_call" | custom-call | tf_op jit(solution)/shard_map/pack/pallas_call | solution.py:104
  2.5 5.6 %collective-permute-start.1 = (bf16[216,384]{1,0:T(8,128)(2,1)}, bf16[216,384]{1,0:T(8,128)(2,1)S(1)}, u32[]{:S(2)}, u32[]{:S(2)}) collective-permute-start(bf16[216,384]{1,0:T(8,128)(2,1)} %get-tuple-element.25), channel_id=1, source_target_pairs={{0,7},{1,0},{2,1},{3,2},{4,3},{5,4},{6,5},{7,6},{8,15},{9,8},{10,9... | collective-permute-start | bytes 497672 | tf_op jit(solution)/shard_map/ppermute | solution.py:416
  8.1 1.0 %collective-permute-start = (bf16[72,384]{1,0:T(8,128)(2,1)}, bf16[72,384]{1,0:T(8,128)(2,1)S(1)}, u32[]{:S(2)}, u32[]{:S(2)}) collective-permute-start(bf16[72,384]{1,0:T(8,128)(2,1)} %get-tuple-element.24), channel_id=1, source_target_pairs={{0,120},{8,0},{16,8},{24,16},{32,24},{40,32},{48,40},{56,48},{64,5... | collective-permute-start | bytes 165896 | tf_op jit(solution)/shard_map/ppermute | solution.py:414
  9.1 3.7 %collective-permute-start.2 = (bf16[72,384]{1,0:T(8,128)(2,1)}, bf16[72,384]{1,0:T(8,128)(2,1)S(1)}, u32[]{:S(2)}, u32[]{:S(2)}) collective-permute-start(bf16[72,384]{1,0:T(8,128)(2,1)} %get-tuple-element.26), channel_id=1, source_target_pairs={{0,127},{1,120},{2,121},{3,122},{4,123},{5,124},{6,125},{7,126},{8... | collective-permute-start | bytes 165896 | tf_op jit(solution)/shard_map/ppermute | solution.py:422
  12.8 0.0 copy-done.2
  12.8 0.0 copy-start.4
  12.8 2.0 %prep.1.bias = f32[2,144,864]{2,1,0:T(8,128)S(1)} custom-call(s32[1]{0:T(128)} %bitcast.1.last_ref, f32[6,2,3312]{2,1,0:T(2,128)S(1)} %bitcast.10), custom_call_target="tpu_custom_call" | custom-call | flops 100000000 | bytes 2097152 | tf_op jit(solution)/shard_map/prep/pallas_call | solution.py:172
  14.8 0.0 copy-start.5
  14.8 1.8 %collective-permute-done.lonh_ref = bf16[72,384]{1,0:T(8,128)(2,1)S(1)} collective-permute-done((bf16[72,384]{1,0:T(8,128)(2,1)}, bf16[72,384]{1,0:T(8,128)(2,1)S(1)}, u32[]{:S(2)}, u32[]{:S(2)}) %collective-permute-start) | collective-permute-done | bytes 55328 | tf_op jit(solution)/shard_map/ppermute | solution.py:414
  16.7 0.0 collective-permute-done.2.corh_ref
  16.7 0.0 collective-permute-done.1.lath_ref
  16.7 0.0 copy-done
  16.7 0.0 copy-done.1
  16.7 7.3 %sublayer.1 = (bf16[216,384]{1,0:T(8,128)(2,1)S(1)}, bf16[72,384]{1,0:T(8,128)(2,1)S(1)}, bf16[216,384]{1,0:T(8,128)(2,1)S(1)}, bf16[72,384]{1,0:T(8,128)(2,1)S(1)}, bf16[16,96,128]{2,1,0:T(8,128)(2,1)}) custom-call(bf16[4,6,24,192]{3,2,1,0:T(8,128)(2,1)S(1)} %copy-done, bf16[4,6,24,192]{3,2,1,0:T(8,128)(2,1)S(1)} %copy-done.1, ...), custom_call_target="tpu_custom_call" | custom-call | flops 1000000000 | bytes 4194304 | tf_op jit(solution)/shard_map/sublayer/pallas_call | solution.py:306
  24.1 7.2 %all-to-all-start = ((bf16[16,96,128]{2,1,0:T(8,128)(2,1)}), bf16[16,96,128]{2,1,0:T(8,128)(2,1)S(1)}, u32[]{:S(2)}, u32[]{:S(2)}) async-start(bf16[16,96,128]{2,1,0:T(8,128)(2,1)} %get-tuple-element.28), calls=%async_computation | async-start | bytes 786432 | tf_op jit(solution)/shard_map/all_to_all | solution.py:447
  31.3 0.0 collective-permute-start.3
  31.3 3.2 %collective-permute-start.4 = (bf16[72,384]{1,0:T(8,128)(2,1)S(1)}, bf16[72,384]{1,0:T(8,128)(2,1)S(1)}, u32[]{:S(2)}, u32[]{:S(2)}) collective-permute-start(bf16[72,384]{1,0:T(8,128)(2,1)S(1)} %get-tuple-element.30), channel_id=1, source_target_pairs={{0,8},{8,16},{16,24},{24,32},{32,40},{40,48},{48,56},{56,64},{64,7... | collective-permute-start | bytes 165896 | tf_op jit(solution)/shard_map/ppermute | solution.py:414
  34.5 0.0 collective-permute-start.5
  34.5 6.9 %all-to-all-done = bf16[16,96,128]{2,1,0:T(8,128)(2,1)S(1)} async-done(((bf16[16,96,128]{2,1,0:T(8,128)(2,1)}), bf16[16,96,128]{2,1,0:T(8,128)(2,1)S(1)}, u32[]{:S(2)}, u32[]{:S(2)}) %all-to-all-start) | async-done | bytes 393248 | tf_op jit(solution)/shard_map/all_to_all | solution.py:447
  41.4 0.1 reduce_sum.24
  41.4 0.0 collective-permute-done.4.lonr_ref
  41.4 2.5 %collective-permute-done.5.corr_ref = bf16[72,384]{1,0:T(8,128)(2,1)S(1)} collective-permute-done((bf16[72,384]{1,0:T(8,128)(2,1)S(1)}, bf16[72,384]{1,0:T(8,128)(2,1)S(1)}, u32[]{:S(2)}, u32[]{:S(2)}) %collective-permute-start.5) | collective-permute-done | bytes 55328 | tf_op jit(solution)/shard_map/ppermute | solution.py:422
  44.0 0.0 collective-permute-done.3.latr_ref
  44.0 0.7 broadcast_in_dim.6
  44.7 3.4 %all-to-all-start.1 = ((bf16[8,80,128]{2,1,0:T(8,128)(2,1)}), bf16[8,80,128]{2,1,0:T(8,128)(2,1)S(1)}, u32[]{:S(2)}, u32[]{:S(2)}) async-start(bf16[8,80,128]{2,1,0:T(8,128)(2,1)} %broadcast_in_dim.6), calls=%async_computation.1 | async-start | bytes 327680 | tf_op jit(solution)/shard_map/all_to_all | solution.py:427
  48.1 5.5 %all-to-all-done.1 = bf16[8,80,128]{2,1,0:T(8,128)(2,1)S(1)} async-done(((bf16[8,80,128]{2,1,0:T(8,128)(2,1)}), bf16[8,80,128]{2,1,0:T(8,128)(2,1)S(1)}, u32[]{:S(2)}, u32[]{:S(2)}) %all-to-all-start.1) | async-done | bytes 163872 | tf_op jit(solution)/shard_map/all_to_all | solution.py:427
  53.7 0.8 %broadcast_in_dim.7 = bf16[16,96,128]{2,1,0:T(8,128)(2,1)} broadcast(bf16[96,128]{1,0:T(8,128)(2,1)S(1)} %pad_maximum_fusion), dimensions={1,2} | broadcast | bytes 417792 | tf_op jit(solution)/shard_map/broadcast_in_dim | solution.py:426
  54.5 8.0 %all-to-all-start.2 = ((bf16[16,96,128]{2,1,0:T(8,128)(2,1)}), bf16[16,96,128]{2,1,0:T(8,128)(2,1)S(1)}, u32[]{:S(2)}, u32[]{:S(2)}) async-start(bf16[16,96,128]{2,1,0:T(8,128)(2,1)} %broadcast_in_dim.7), calls=%async_computation.2 | async-start | bytes 786432 | tf_op jit(solution)/shard_map/all_to_all | solution.py:427
  62.5 1.0 %combine.1 = (bf16[4,6,24,192]{3,2,1,0:T(8,128)(2,1)}, bf16[4,6,24,192]{3,2,1,0:T(8,128)(2,1)}) custom-call(bf16[4,6,24,192]{3,2,1,0:T(8,128)(2,1)S(1)} %copy-done, bf16[4,6,24,192]{3,2,1,0:T(8,128)(2,1)S(1)} %copy-done.1, bf16[216,384]{1,0:T(8,128)(2,1)S(1)} %get-tuple-element.27.own_ref, bf16[72,384]{1,0:T(8,128)(2,1)S(1)} %collective-permute-done.4.lonr_ref, ...), custom_call_target="tpu_custom_call" | custom-call | flops 1000000000 | bytes 4194304 | tf_op jit(solution)/shard_map/combine/pallas_call | solution.py:347
  63.5 9.1 %all-to-all-done.2.whole_ref = bf16[16,96,128]{2,1,0:T(8,128)(2,1)S(1)} async-done(((bf16[16,96,128]{2,1,0:T(8,128)(2,1)}), bf16[16,96,128]{2,1,0:T(8,128)(2,1)S(1)}, u32[]{:S(2)}, u32[]{:S(2)}) %all-to-all-start.2) | async-done | bytes 393248 | tf_op jit(solution)/shard_map/all_to_all | solution.py:427
  72.6 1.7 %unpack.1 = (f32[192,576]{1,0:T(8,128)}, f32[192,192]{1,0:T(8,128)}, f32[1,192]{1,0:T(1,128)}, f32[6,2,3312]{2,1,0:T(2,128)}) custom-call(bf16[16,96,128]{2,1,0:T(8,128)(2,1)S(1)} %all-to-all-done.2.whole_ref), custom_call_target="tpu_custom_call" | custom-call | tf_op jit(solution)/shard_map/unpack/pallas_call | solution.py:390
  (10 shorter events, 0.1 us)
Async XLA Ops:
  0.6 12.1 %copy-start.2 = (f32[1,2,6,3312]{3,1,2,0:T(2,128)S(1)}, f32[1,2,6,3312]{3,1,2,0:T(2,128)}, u32[]{:S(2)}) copy-start(f32[1,2,6,3312]{3,1,2,0:T(2,128)} %param.11) | copy-start | bytes 476932
  2.5 14.1 %collective-permute-start.1 = (bf16[216,384]{1,0:T(8,128)(2,1)}, bf16[216,384]{1,0:T(8,128)(2,1)S(1)}, u32[]{:S(2)}, u32[]{:S(2)}) collective-permute-start(bf16[216,384]{1,0:T(8,128)(2,1)} %get-tuple-element.25), channel_id=1, source_target_pairs={{0,7},{1,0},{2,1},{3,2},{4,3},{5,4},{6,5},{7,6},{8,15},{9,8},{10,9... | collective-permute-start | bytes 497672 | tf_op jit(solution)/shard_map/ppermute | solution.py:416
  8.1 8.5 %collective-permute-start = (bf16[72,384]{1,0:T(8,128)(2,1)}, bf16[72,384]{1,0:T(8,128)(2,1)S(1)}, u32[]{:S(2)}, u32[]{:S(2)}) collective-permute-start(bf16[72,384]{1,0:T(8,128)(2,1)} %get-tuple-element.24), channel_id=1, source_target_pairs={{0,120},{8,0},{16,8},{24,16},{32,24},{40,32},{48,40},{56,48},{64,5... | collective-permute-start | bytes 165896 | tf_op jit(solution)/shard_map/ppermute | solution.py:414
  9.1 7.6 %collective-permute-start.2 = (bf16[72,384]{1,0:T(8,128)(2,1)}, bf16[72,384]{1,0:T(8,128)(2,1)S(1)}, u32[]{:S(2)}, u32[]{:S(2)}) collective-permute-start(bf16[72,384]{1,0:T(8,128)(2,1)} %get-tuple-element.26), channel_id=1, source_target_pairs={{0,127},{1,120},{2,121},{3,122},{4,123},{5,124},{6,125},{7,126},{8... | collective-permute-start | bytes 165896 | tf_op jit(solution)/shard_map/ppermute | solution.py:422
  12.8 3.9 %copy-start = (bf16[4,6,24,192]{3,2,1,0:T(8,128)(2,1)S(1)}, bf16[4,6,24,192]{3,2,1,0:T(8,128)(2,1)}, u32[]{:S(2)}) copy-start(bf16[4,6,24,192]{3,2,1,0:T(8,128)(2,1)} %air_ref.5) | copy-start | bytes 663556
  12.8 3.9 %copy-start.1 = (bf16[4,6,24,192]{3,2,1,0:T(8,128)(2,1)S(1)}, bf16[4,6,24,192]{3,2,1,0:T(8,128)(2,1)}, u32[]{:S(2)}) copy-start(bf16[4,6,24,192]{3,2,1,0:T(8,128)(2,1)} %up_ref.5) | copy-start | bytes 663556
  12.8 3.9 %copy-start.3 = (bf16[192,576]{1,0:T(8,128)(2,1)S(1)}, bf16[192,576]{1,0:T(8,128)(2,1)}, u32[]{:S(2)}) copy-start(bf16[192,576]{1,0:T(8,128)(2,1)} %wqkv_ref.1) | copy-start | bytes 663556
  12.8 3.9 %copy-start.4 = (bf16[192,192]{1,0:T(8,128)(2,1)S(1)}, bf16[192,192]{1,0:T(8,128)(2,1)}, u32[]{:S(2)}) copy-start(bf16[192,192]{1,0:T(8,128)(2,1)} %wproj_ref.1) | copy-start | bytes 221188
  14.8 1.9 %copy-start.5 = (f32[192]{0:T(256)S(1)}, f32[192]{0:T(256)}, u32[]{:S(2)}) copy-start(f32[192]{0:T(256)} %param.8) | copy-start | bytes 2308
  24.1 17.3 %all-to-all-start = ((bf16[16,96,128]{2,1,0:T(8,128)(2,1)}), bf16[16,96,128]{2,1,0:T(8,128)(2,1)S(1)}, u32[]{:S(2)}, u32[]{:S(2)}) async-start(bf16[16,96,128]{2,1,0:T(8,128)(2,1)} %get-tuple-element.28), calls=%async_computation | async-start | bytes 786432 | tf_op jit(solution)/shard_map/all_to_all | solution.py:447
  31.3 12.7 %collective-permute-start.3 = (bf16[216,384]{1,0:T(8,128)(2,1)S(1)}, bf16[216,384]{1,0:T(8,128)(2,1)S(1)}, u32[]{:S(2)}, u32[]{:S(2)}) collective-permute-start(bf16[216,384]{1,0:T(8,128)(2,1)S(1)} %get-tuple-element.29), channel_id=1, source_target_pairs={{0,1},{1,2},{2,3},{3,4},{4,5},{5,6},{6,7},{7,0},{8,9},{9,10},{10,1... | collective-permute-start | bytes 497672 | tf_op jit(solution)/shard_map/ppermute | solution.py:416
  31.3 10.1 %collective-permute-start.4 = (bf16[72,384]{1,0:T(8,128)(2,1)S(1)}, bf16[72,384]{1,0:T(8,128)(2,1)S(1)}, u32[]{:S(2)}, u32[]{:S(2)}) collective-permute-start(bf16[72,384]{1,0:T(8,128)(2,1)S(1)} %get-tuple-element.30), channel_id=1, source_target_pairs={{0,8},{8,16},{16,24},{24,32},{32,40},{40,48},{48,56},{56,64},{64,7... | collective-permute-start | bytes 165896 | tf_op jit(solution)/shard_map/ppermute | solution.py:414
  34.5 9.5 %collective-permute-start.5 = (bf16[72,384]{1,0:T(8,128)(2,1)S(1)}, bf16[72,384]{1,0:T(8,128)(2,1)S(1)}, u32[]{:S(2)}, u32[]{:S(2)}) collective-permute-start(bf16[72,384]{1,0:T(8,128)(2,1)S(1)} %get-tuple-element.31), channel_id=1, source_target_pairs={{0,9},{1,10},{2,11},{3,12},{4,13},{5,14},{6,15},{7,8},{8,17},{9,18... | collective-permute-start | bytes 165896 | tf_op jit(solution)/shard_map/ppermute | solution.py:422
  44.7 8.9 %all-to-all-start.1 = ((bf16[8,80,128]{2,1,0:T(8,128)(2,1)}), bf16[8,80,128]{2,1,0:T(8,128)(2,1)S(1)}, u32[]{:S(2)}, u32[]{:S(2)}) async-start(bf16[8,80,128]{2,1,0:T(8,128)(2,1)} %broadcast_in_dim.6), calls=%async_computation.1 | async-start | bytes 327680 | tf_op jit(solution)/shard_map/all_to_all | solution.py:427
  54.5 18.1 %all-to-all-start.2 = ((bf16[16,96,128]{2,1,0:T(8,128)(2,1)}), bf16[16,96,128]{2,1,0:T(8,128)(2,1)S(1)}, u32[]{:S(2)}, u32[]{:S(2)}) async-start(bf16[16,96,128]{2,1,0:T(8,128)(2,1)} %broadcast_in_dim.7), calls=%async_computation.2 | async-start | bytes 786432 | tf_op jit(solution)/shard_map/all_to_all | solution.py:427

commit v2 on v1

--- a/solution.py
+++ b/solution.py
@@ -79,17 +79,30 @@
     return state, jnp.concatenate([rows[:, 128:256], rows[:, 320:384]], axis=1)
 
 
-def pack_kernel(air_ref, up_ref, lonh_ref, lath_ref, corh_ref):
+def pack_kernel(air_hbm, up_hbm, lonh_ref, lath_ref, corh_ref, low, high, sems):
+    copies = []
+    for i, src in enumerate((air_hbm, up_hbm)):
+        for lev in range(4):
+            copies.append(
+                pltpu.make_async_copy(src.at[lev, 0:3], low.at[i, lev], sems.at[0, i, lev])
+            )
+            copies.append(
+                pltpu.make_async_copy(
+                    src.at[lev, 3:6, 0:8], high.at[i, lev], sems.at[1, i, lev]
+                )
+            )
+    for copy in copies:
+        copy.start()
+    for copy in copies:
+        copy.wait()
     for lev in range(4):
         for r in range(3):
             at = lev * 3 + r
-            row = joined(air_ref[lev, r].astype(f32), up_ref[lev, r].astype(f32)).astype(bf16)
+            row = joined(low[0, lev, r].astype(f32), low[1, lev, r].astype(f32)).astype(bf16)
             corh_ref[at * 6 : (at + 1) * 6] = row[0:6]
             lath_ref[at * 18 : (at + 1) * 18] = row[6:24]
-            row = joined(
-                air_ref[lev, r + 3][0:6].astype(f32), up_ref[lev, r + 3][0:6].astype(f32)
-            )
-            lonh_ref[at * 6 : (at + 1) * 6] = row.astype(bf16)
+            row = joined(high[0, lev, r].astype(f32), high[1, lev, r].astype(f32))
+            lonh_ref[at * 6 : (at + 1) * 6] = row.astype(bf16)[0:6]
 
 
 HALOS = [
@@ -101,13 +114,23 @@
 
 def pack(air, up):
     vmem = pl.BlockSpec(memory_space=pltpu.VMEM)
+    hbm = pl.BlockSpec(memory_space=pltpu.HBM)
     return pl.pallas_call(
         pack_kernel,
-        in_specs=[vmem] * 2,
+        in_specs=[hbm] * 2,
         out_specs=[vmem] * 3,
         out_shape=HALOS,
+        scratch_shapes=[
+            pltpu.VMEM((2, 4, 3, 24, C), bf16),
+            pltpu.VMEM((2, 4, 3, 8, C), bf16),
+            pltpu.SemaphoreType.DMA((2, 2, 4)),
+        ],
+        compiler_params=pltpu.CompilerParams(vmem_limit_bytes=8 << 20),
         name="pack",
-    )(air, up)
+    )(
+        pltpu.with_memory_space_constraint(air, pltpu.HBM),
+        pltpu.with_memory_space_constraint(up, pltpu.HBM),
+    )
 
 
 def normalised(x):
@@ -224,9 +247,9 @@
             total = jnp.where(lane_head == h, stacked[h * WIN : (h + 1) * WIN], total)
         return total
 
-    def window(w, carry):
+    def window(w):
         a = w // 2
-        rows = pl.ds(pl.multiple_of(w * WIN, 16), WIN)
+        rows = pl.ds(w * WIN, WIN)
         k, v = k_s[rows, :], v_s[rows, :]
         qs = spread(q_s[rows, :])
         scores = dot(k, qs, NT) * scale + bias[a]
@@ -244,9 +267,9 @@
         dsc = dscores.astype(bf16)
         dk_s[rows, :] = (dot(dsc, qs, NN) * scale).astype(bf16)
         dq_s[rows, :] = (gathered(dot(dsc, k, TN)) * scale).astype(bf16)
-        return carry
-
-    lax.fori_loop(0, 4, window, 0)
+
+    for w in range(4):
+        window(w)
 
     mix = mix_s[...]
     mq, mk, mv = (dot(normed, d[...], TN) for d in (dq_s, dk_s, dv_s))
@@ -350,9 +373,58 @@
         out_specs=[vmem] * 2,
         out_shape=[jax.ShapeDtypeStruct(air.shape, bf16)] * 2,
         compiler_params=pltpu.CompilerParams(vmem_limit_bytes=16 << 20),
-        cost_estimate=pl.CostEstimate(flops=10**9, bytes_accessed=4 << 20, transcendentals=0),
+        cost_estimate=pl.CostEstimate(flops=10**10, bytes_accessed=40 << 20, transcendentals=0),
         name="combine",
     )(air, up, own, lonr, latr, corr)
+
+
+def total(ref):
+    parts = [ref[i].astype(f32) for i in range(ref.shape[0])]
+    while len(parts) > 1:
+        parts = [a + b for a, b in zip(parts[::2], parts[1::2])]
+    return parts[0].astype(bf16)
+
+
+def lon_sum_kernel(parts_ref, copies_ref, table_ref):
+    one = total(parts_ref)
+    for i in range(copies_ref.shape[0]):
+        copies_ref[i] = one[:MID]
+    table_ref[...] = one
+
+
+def lat_sum_kernel(parts_ref, table_ref, copies_ref):
+    one = jnp.concatenate([total(parts_ref), table_ref[MID:]], axis=0)
+    row = lax.broadcasted_iota(jnp.int32, (CHUNK, 1), 0)
+    one = jnp.where(row < TROW, one.astype(f32), table_ref[...].astype(f32)).astype(bf16)
+    for i in range(copies_ref.shape[0]):
+        copies_ref[i] = one
+
+
+def lon_sum(parts, lats):
+    vmem = pl.BlockSpec(memory_space=pltpu.VMEM)
+    return pl.pallas_call(
+        lon_sum_kernel,
+        in_specs=[vmem],
+        out_specs=[vmem] * 2,
+        out_shape=[
+            jax.ShapeDtypeStruct((lats, MID, 128), bf16),
+            jax.ShapeDtypeStruct((CHUNK, 128), bf16),
+        ],
+        compiler_params=pltpu.CompilerParams(vmem_limit_bytes=4 << 20),
+        name="lon_sum",
+    )(parts)
+
+
+def lat_sum(parts, table, lons):
+    vmem = pl.BlockSpec(memory_space=pltpu.VMEM)
+    return pl.pallas_call(
+        lat_sum_kernel,
+        in_specs=[vmem] * 2,
+        out_specs=vmem,
+        out_shape=jax.ShapeDtypeStruct((lons, CHUNK, 128), bf16),
+        compiler_params=pltpu.CompilerParams(vmem_limit_bytes=4 << 20),
+        name="lat_sum",
+    )(parts, table)
 
 
 def unpack_kernel(whole_ref, dwqkv_ref, dwproj_ref, dgain_ref, dtable_ref, gw, tr, gt, flat):
@@ -422,15 +494,6 @@
     return lax.ppermute(array, ("lon", "lat"), pairs)
 
 
-def each(array, axis):
-    copies = jnp.broadcast_to(array, (lax.axis_size(axis), *array.shape))
-    return lax.all_to_all(copies, axis, split_axis=0, concat_axis=0, tiled=True)
-
-
-def summed(array):
-    return jnp.sum(array.astype(f32), axis=0).astype(bf16)
-
-
 def on_device(air, up, gain, wqkv, wproj, table):
     lonh, lath, corh = pack(air, up)
     lath = neighbour(lath, 0, -1)
@@ -444,11 +507,11 @@
     latr = neighbour(lato, 0, 1)
     lonr = neighbour(lono, 1, 0)
     corr = neighbour(coro, 1, 1)
-    part = summed(lax.all_to_all(grads, "lon", split_axis=0, concat_axis=0, tiled=True))
-    part, latr, lonr, corr = lax.optimization_barrier((part, latr, lonr, corr))
-    weights = summed(each(part[:MID], "lat"))
-    share = jnp.concatenate([weights[:TROW], part[TROW:]], axis=0)
-    whole = each(share, "lon")
+    parts = lax.all_to_all(grads, "lon", split_axis=0, concat_axis=0, tiled=True)
+    copies, table_part = lon_sum(parts, lax.axis_size("lat"))
+    parts = lax.all_to_all(copies, "lat", split_axis=0, concat_axis=0, tiled=True)
+    copies = lat_sum(parts, table_part, lax.axis_size("lon"))
+    whole = lax.all_to_all(copies, "lon", split_axis=0, concat_axis=0, tiled=True)
     block_out, d_state = combine(air, up, own, lonr, latr, corr)
     d_wqkv, d_wproj, d_gain, d_table = unpack(whole)
     d_table = d_table.reshape(1, HEADS, 2, POS * POS * REL).transpose(0, 2, 1, 3)

time: 74.7 us -> 67.9 us (0.909)
  starting transfers between devices: 32 us -> 28.7 us
  waiting for transfers between devices: 25.8 us -> 24 us
  local copies, waits for them, and re-layouts: 1.53 us -> 0.03 us
    all_to_all x1, waiting for transfers between devices: 6.87 us -> 10.1 us  [on_device(): lax.all_to_all(grads, 'lon', split_axis=0, concat_axis=0, tiled=True)]
    all_to_all x2, starting transfers between devices: 11.4 us -> 8.85 us  [the longest x1 5.46 us: on_device(): lax.all_to_all(copies, 'lon', split_axis=0, concat_axis=0, tiled=True)]
    ppermute x2, waiting for transfers between devices: 2.54 us -> 0.01 us  [neighbour(): return lax.ppermute(array, ('lon', 'lat'), pairs)]
    all_to_all x2, waiting for transfers between devices: 14.6 us -> 12.3 us  [the longest x1 9.08 us: on_device(): lax.all_to_all(copies, 'lon', split_axis=0, concat_axis=0, tiled=True)]
    ppermute x2, starting transfers between devices: 4.16 us -> 1.98 us  [neighbour(): lax.ppermute(array, 'lon', [(i, (i + lon_by) % lons) for i in range(lons)])]
    broadcast_in_dim x2 -> x0, local copies, waits for them, and re-layouts: 1.49 us -> none  [each(): copies = jnp.broadcast_to(array, (lax.axis_size(axis), *array.shape))]
    ppermute x2, starting transfers between devices: 3.66 us -> 5 us  [neighbour(): return lax.ppermute(array, ('lon', 'lat'), pairs)]
    pallas_call x1, Pallas kernels: 7.34 us -> 6.42 us  [run_main(): pl.pallas_call(main_kernel, in_specs=[vmem] * 9, out_specs=[vmem] * 5, ou...]
  transfers between devices with their start and end apart: 9 -> 9, of which waited for: 5 -> 4; matrix products, arithmetic and copies ran while one was open for 0% -> 0% of each run, Pallas kernels for 4% -> 7%
where the time goes in v2:
time: 67.9 us; the launch traced here: 67.5 us
  starting transfers between devices  28.7 us (42%)
  waiting for transfers between devices  24 us (35%)
  Pallas kernels  13.9 us (20%)
  between operations  0.75 us (1%)
    all_to_all x1, waiting for transfers between devices, on_device(): lax.all_to_all(grads, 'lon', split_axis=0, concat_axis=0, tiled=True)  10.1 us
    all_to_all x1, waiting for transfers between devices, on_device(): lax.all_to_all(copies, 'lon', split_axis=0, concat_axis=0, tiled=True)  9.08 us
    all_to_all x1, starting transfers between devices, on_device(): lax.all_to_all(grads, 'lon', split_axis=0, concat_axis=0, tiled=True)  7.23 us
    pallas_call x1, Pallas kernels, run_main(): pl.pallas_call(main_kernel, in_specs=[vmem] * 9, out_specs=[vmem] * 5, ou...  6.42 us
    ppermute x2, starting transfers between devices, neighbour(): lax.ppermute(array, 'lat', [(i, (i + lat_by) % lats) for i in range(lats)])  5.67 us
    all_to_all x1, starting transfers between devices, on_device(): lax.all_to_all(copies, 'lon', split_axis=0, concat_axis=0, tiled=True)  5.46 us
    ppermute x2, starting transfers between devices, neighbour(): return lax.ppermute(array, ('lon', 'lat'), pairs)  5 us
    all_to_all x1, starting transfers between devices, on_device(): lax.all_to_all(copies, 'lat', split_axis=0, concat_axis=0, tiled=True)  3.38 us
  transfers between devices with their start and end apart: 9, of which 4 were waited for; matrix products, arithmetic and copies ran while one was open for 0% of the time, Pallas kernels for 7%

profile of v2, /device:TPU:1, one launch (start us, length us, event | category | flops | bytes accessed | tf_op | source)
XLA Modules:
  0.0 67.5 jit_solution(16678356275762384865)
XLA Ops:
  0.6 0.0 copy-start.2
  0.6 1.3 %pack.1 = (bf16[72,384]{1,0:T(8,128)(2,1)S(1)}, bf16[216,384]{1,0:T(8,128)(2,1)S(1)}, bf16[72,384]{1,0:T(8,128)(2,1)S(1)}) custom-call(bf16[4,6,24,192]{3,2,1,0:T(8,128)(2,1)} %air_ref.3, bf16[4,6,24,192]{3,2,1,0:T(8,128)(2,1)} %up_ref.3), custom_call_target="tpu_custom_call" | custom-call | tf_op jit(solution)/shard_map/pack/pallas_call | solution.py:118
  1.9 5.7 %collective-permute-start.1 = (bf16[216,384]{1,0:T(8,128)(2,1)S(1)}, bf16[216,384]{1,0:T(8,128)(2,1)S(1)}, u32[]{:S(2)}, u32[]{:S(2)}) collective-permute-start(bf16[216,384]{1,0:T(8,128)(2,1)S(1)} %get-tuple-element.23), channel_id=1, source_target_pairs={{0,7},{1,0},{2,1},{3,2},{4,3},{5,4},{6,5},{7,6},{8,15},{9,8},{10,9... | collective-permute-start | bytes 497672 | tf_op jit(solution)/shard_map/ppermute | solution.py:488
  7.6 1.0 %collective-permute-start = (bf16[72,384]{1,0:T(8,128)(2,1)S(1)}, bf16[72,384]{1,0:T(8,128)(2,1)S(1)}, u32[]{:S(2)}, u32[]{:S(2)}) collective-permute-start(bf16[72,384]{1,0:T(8,128)(2,1)S(1)} %get-tuple-element.22), channel_id=1, source_target_pairs={{0,120},{8,0},{16,8},{24,16},{32,24},{40,32},{48,40},{56,48},{64,5... | collective-permute-start | bytes 165896 | tf_op jit(solution)/shard_map/ppermute | solution.py:486
  8.5 3.7 %collective-permute-start.2 = (bf16[72,384]{1,0:T(8,128)(2,1)S(1)}, bf16[72,384]{1,0:T(8,128)(2,1)S(1)}, u32[]{:S(2)}, u32[]{:S(2)}) collective-permute-start(bf16[72,384]{1,0:T(8,128)(2,1)S(1)} %get-tuple-element.24), channel_id=1, source_target_pairs={{0,127},{1,120},{2,121},{3,122},{4,123},{5,124},{6,125},{7,126},{8... | collective-permute-start | bytes 165896 | tf_op jit(solution)/shard_map/ppermute | solution.py:494
  12.2 0.0 copy-done.2
  12.2 0.0 copy-start.4
  12.2 2.0 %prep.1.bias = f32[2,144,864]{2,1,0:T(8,128)S(1)} custom-call(s32[1]{0:T(128)} %bitcast.1.last_ref, f32[6,2,3312]{2,1,0:T(2,128)S(1)} %bitcast.9), custom_call_target="tpu_custom_call" | custom-call | flops 100000000 | bytes 2097152 | tf_op jit(solution)/shard_map/prep/pallas_call | solution.py:195
  14.3 0.0 copy-start.5
  14.3 1.6 %collective-permute-done.lonh_ref = bf16[72,384]{1,0:T(8,128)(2,1)S(1)} collective-permute-done((bf16[72,384]{1,0:T(8,128)(2,1)S(1)}, bf16[72,384]{1,0:T(8,128)(2,1)S(1)}, u32[]{:S(2)}, u32[]{:S(2)}) %collective-permute-start) | collective-permute-done | bytes 55328 | tf_op jit(solution)/shard_map/ppermute | solution.py:486
  15.9 0.0 collective-permute-done.2.corh_ref
  15.9 0.0 collective-permute-done.1.lath_ref
  15.9 0.0 copy-done
  15.9 0.0 copy-done.1
  15.9 0.0 copy-done.3
  15.9 6.4 %sublayer.1 = (bf16[216,384]{1,0:T(8,128)(2,1)S(1)}, bf16[72,384]{1,0:T(8,128)(2,1)S(1)}, bf16[216,384]{1,0:T(8,128)(2,1)S(1)}, bf16[72,384]{1,0:T(8,128)(2,1)S(1)}, bf16[16,96,128]{2,1,0:T(8,128)(2,1)}) custom-call(bf16[4,6,24,192]{3,2,1,0:T(8,128)(2,1)S(1)} %copy-done, bf16[4,6,24,192]{3,2,1,0:T(8,128)(2,1)S(1)} %copy-done.1, ...), custom_call_target="tpu_custom_call" | custom-call | flops 1000000000 | bytes 4194304 | tf_op jit(solution)/shard_map/sublayer/pallas_call | solution.py:329
  22.3 7.2 %all-to-all-start = ((bf16[16,96,128]{2,1,0:T(8,128)(2,1)}), bf16[16,96,128]{2,1,0:T(8,128)(2,1)S(1)}, u32[]{:S(2)}, u32[]{:S(2)}) async-start(bf16[16,96,128]{2,1,0:T(8,128)(2,1)} %get-tuple-element.31), calls=%async_computation | async-start | bytes 786432 | tf_op jit(solution)/shard_map/all_to_all | solution.py:510
  29.6 0.0 collective-permute-start.4
  29.6 10.1 %all-to-all-done.parts_ref = bf16[16,96,128]{2,1,0:T(8,128)(2,1)S(1)} async-done(((bf16[16,96,128]{2,1,0:T(8,128)(2,1)}), bf16[16,96,128]{2,1,0:T(8,128)(2,1)S(1)}, u32[]{:S(2)}, u32[]{:S(2)}) %all-to-all-start) | async-done | bytes 393248 | tf_op jit(solution)/shard_map/all_to_all | solution.py:510
  39.7 0.7 %lon_sum.1 = (bf16[8,80,128]{2,1,0:T(8,128)(2,1)}, bf16[96,128]{1,0:T(8,128)(2,1)S(1)}) custom-call(bf16[16,96,128]{2,1,0:T(8,128)(2,1)S(1)} %all-to-all-done.parts_ref), custom_call_target="tpu_custom_call" | custom-call | tf_op jit(solution)/shard_map/lon_sum/pallas_call | solution.py:405
  40.4 3.4 %all-to-all-start.1 = ((bf16[8,80,128]{2,1,0:T(8,128)(2,1)}), bf16[8,80,128]{2,1,0:T(8,128)(2,1)S(1)}, u32[]{:S(2)}, u32[]{:S(2)}) async-start(bf16[8,80,128]{2,1,0:T(8,128)(2,1)} %get-tuple-element.32), calls=%async_computation.1 | async-start | bytes 327680 | tf_op jit(solution)/shard_map/all_to_all | solution.py:512
  43.8 1.0 %collective-permute-start.3 = (bf16[72,384]{1,0:T(8,128)(2,1)S(1)}, bf16[72,384]{1,0:T(8,128)(2,1)S(1)}, u32[]{:S(2)}, u32[]{:S(2)}) collective-permute-start(bf16[72,384]{1,0:T(8,128)(2,1)S(1)} %get-tuple-element.26), channel_id=1, source_target_pairs={{0,8},{8,16},{16,24},{24,32},{32,40},{40,48},{48,56},{56,64},{64,7... | collective-permute-start | bytes 165896 | tf_op jit(solution)/shard_map/ppermute | solution.py:486
  44.8 1.3 %collective-permute-start.5 = (bf16[72,384]{1,0:T(8,128)(2,1)S(1)}, bf16[72,384]{1,0:T(8,128)(2,1)S(1)}, u32[]{:S(2)}, u32[]{:S(2)}) collective-permute-start(bf16[72,384]{1,0:T(8,128)(2,1)S(1)} %get-tuple-element.28), channel_id=1, source_target_pairs={{0,9},{1,10},{2,11},{3,12},{4,13},{5,14},{6,15},{7,8},{8,17},{9,18... | collective-permute-start | bytes 165896 | tf_op jit(solution)/shard_map/ppermute | solution.py:494
  46.1 3.3 %all-to-all-done.1.parts_ref = bf16[8,80,128]{2,1,0:T(8,128)(2,1)S(1)} async-done(((bf16[8,80,128]{2,1,0:T(8,128)(2,1)}), bf16[8,80,128]{2,1,0:T(8,128)(2,1)S(1)}, u32[]{:S(2)}, u32[]{:S(2)}) %all-to-all-start.1) | async-done | bytes 163872 | tf_op jit(solution)/shard_map/all_to_all | solution.py:512
  49.4 0.8 %lat_sum.1 = bf16[16,96,128]{2,1,0:T(8,128)(2,1)} custom-call(bf16[8,80,128]{2,1,0:T(8,128)(2,1)S(1)} %all-to-all-done.1.parts_ref, bf16[96,128]{1,0:T(8,128)(2,1)S(1)} %get-tuple-element.33.table_ref), custom_call_target="tpu_custom_call" | custom-call | tf_op jit(solution)/shard_map/lat_sum/pallas_call | solution.py:420
  50.2 5.5 %all-to-all-start.2 = ((bf16[16,96,128]{2,1,0:T(8,128)(2,1)}), bf16[16,96,128]{2,1,0:T(8,128)(2,1)S(1)}, u32[]{:S(2)}, u32[]{:S(2)}) async-start(bf16[16,96,128]{2,1,0:T(8,128)(2,1)} %lat_sum.1), calls=%async_computation.2 | async-start | bytes 786432 | tf_op jit(solution)/shard_map/all_to_all | solution.py:514
  55.6 0.0 collective-permute-done.3.lonr_ref
  55.6 0.0 collective-permute-done.5.corr_ref
  55.7 0.0 collective-permute-done.4.latr_ref
  55.7 1.0 %combine.1 = (bf16[4,6,24,192]{3,2,1,0:T(8,128)(2,1)}, bf16[4,6,24,192]{3,2,1,0:T(8,128)(2,1)}) custom-call(bf16[4,6,24,192]{3,2,1,0:T(8,128)(2,1)S(1)} %copy-done, bf16[4,6,24,192]{3,2,1,0:T(8,128)(2,1)S(1)} %copy-done.1, bf16[216,384]{1,0:T(8,128)(2,1)S(1)} %get-tuple-element.25.own_ref, bf16[72,384]{1,0:T(8,128)(2,1)S(1)} %collective-permute-done.3.lonr_ref, ...), custom_call_target="tpu_custom_call" | custom-call | flops 10000000000 | bytes 41943040 | tf_op jit(solution)/shard_map/combine/pallas_call | solution.py:370
  56.7 9.1 %all-to-all-done.2.whole_ref = bf16[16,96,128]{2,1,0:T(8,128)(2,1)S(1)} async-done(((bf16[16,96,128]{2,1,0:T(8,128)(2,1)}), bf16[16,96,128]{2,1,0:T(8,128)(2,1)S(1)}, u32[]{:S(2)}, u32[]{:S(2)}) %all-to-all-start.2) | async-done | bytes 393248 | tf_op jit(solution)/shard_map/all_to_all | solution.py:514
  65.8 1.7 %unpack.1 = (f32[192,576]{1,0:T(8,128)}, f32[192,192]{1,0:T(8,128)}, f32[1,192]{1,0:T(1,128)}, f32[6,2,3312]{2,1,0:T(2,128)}) custom-call(bf16[16,96,128]{2,1,0:T(8,128)(2,1)S(1)} %all-to-all-done.2.whole_ref), custom_call_target="tpu_custom_call" | custom-call | tf_op jit(solution)/shard_map/unpack/pallas_call | solution.py:462
  (5 shorter events, 0.0 us)
Async XLA Ops:
  0.6 11.6 %copy-start.2 = (f32[1,2,6,3312]{3,1,2,0:T(2,128)S(1)}, f32[1,2,6,3312]{3,1,2,0:T(2,128)}, u32[]{:S(2)}) copy-start(f32[1,2,6,3312]{3,1,2,0:T(2,128)} %param.11) | copy-start | bytes 476932
  1.9 14.0 %collective-permute-start.1 = (bf16[216,384]{1,0:T(8,128)(2,1)S(1)}, bf16[216,384]{1,0:T(8,128)(2,1)S(1)}, u32[]{:S(2)}, u32[]{:S(2)}) collective-permute-start(bf16[216,384]{1,0:T(8,128)(2,1)S(1)} %get-tuple-element.23), channel_id=1, source_target_pairs={{0,7},{1,0},{2,1},{3,2},{4,3},{5,4},{6,5},{7,6},{8,15},{9,8},{10,9... | collective-permute-start | bytes 497672 | tf_op jit(solution)/shard_map/ppermute | solution.py:488
  7.6 8.3 %collective-permute-start = (bf16[72,384]{1,0:T(8,128)(2,1)S(1)}, bf16[72,384]{1,0:T(8,128)(2,1)S(1)}, u32[]{:S(2)}, u32[]{:S(2)}) collective-permute-start(bf16[72,384]{1,0:T(8,128)(2,1)S(1)} %get-tuple-element.22), channel_id=1, source_target_pairs={{0,120},{8,0},{16,8},{24,16},{32,24},{40,32},{48,40},{56,48},{64,5... | collective-permute-start | bytes 165896 | tf_op jit(solution)/shard_map/ppermute | solution.py:486
  8.5 7.4 %collective-permute-start.2 = (bf16[72,384]{1,0:T(8,128)(2,1)S(1)}, bf16[72,384]{1,0:T(8,128)(2,1)S(1)}, u32[]{:S(2)}, u32[]{:S(2)}) collective-permute-start(bf16[72,384]{1,0:T(8,128)(2,1)S(1)} %get-tuple-element.24), channel_id=1, source_target_pairs={{0,127},{1,120},{2,121},{3,122},{4,123},{5,124},{6,125},{7,126},{8... | collective-permute-start | bytes 165896 | tf_op jit(solution)/shard_map/ppermute | solution.py:494
  12.2 3.7 %copy-start = (bf16[4,6,24,192]{3,2,1,0:T(8,128)(2,1)S(1)}, bf16[4,6,24,192]{3,2,1,0:T(8,128)(2,1)}, u32[]{:S(2)}) copy-start(bf16[4,6,24,192]{3,2,1,0:T(8,128)(2,1)} %air_ref.3) | copy-start | bytes 663556
  12.2 3.7 %copy-start.1 = (bf16[4,6,24,192]{3,2,1,0:T(8,128)(2,1)S(1)}, bf16[4,6,24,192]{3,2,1,0:T(8,128)(2,1)}, u32[]{:S(2)}) copy-start(bf16[4,6,24,192]{3,2,1,0:T(8,128)(2,1)} %up_ref.3) | copy-start | bytes 663556
  12.2 3.7 %copy-start.3 = (bf16[192,576]{1,0:T(8,128)(2,1)S(1)}, bf16[192,576]{1,0:T(8,128)(2,1)}, u32[]{:S(2)}) copy-start(bf16[192,576]{1,0:T(8,128)(2,1)} %wqkv_ref.1) | copy-start | bytes 663556
  12.2 3.7 %copy-start.4 = (bf16[192,192]{1,0:T(8,128)(2,1)S(1)}, bf16[192,192]{1,0:T(8,128)(2,1)}, u32[]{:S(2)}) copy-start(bf16[192,192]{1,0:T(8,128)(2,1)} %wproj_ref.1) | copy-start | bytes 221188
  14.3 1.7 %copy-start.5 = (f32[192]{0:T(256)S(1)}, f32[192]{0:T(256)}, u32[]{:S(2)}) copy-start(f32[192]{0:T(256)} %param.8) | copy-start | bytes 2308
  22.3 17.3 %all-to-all-start = ((bf16[16,96,128]{2,1,0:T(8,128)(2,1)}), bf16[16,96,128]{2,1,0:T(8,128)(2,1)S(1)}, u32[]{:S(2)}, u32[]{:S(2)}) async-start(bf16[16,96,128]{2,1,0:T(8,128)(2,1)} %get-tuple-element.31), calls=%async_computation | async-start | bytes 786432 | tf_op jit(solution)/shard_map/all_to_all | solution.py:510
  29.6 26.1 %collective-permute-start.4 = (bf16[216,384]{1,0:T(8,128)(2,1)S(1)}, bf16[216,384]{1,0:T(8,128)(2,1)S(1)}, u32[]{:S(2)}, u32[]{:S(2)}) collective-permute-start(bf16[216,384]{1,0:T(8,128)(2,1)S(1)} %get-tuple-element.27), channel_id=1, source_target_pairs={{0,1},{1,2},{2,3},{3,4},{4,5},{5,6},{6,7},{7,0},{8,9},{9,10},{10,1... | collective-permute-start | bytes 497672 | tf_op jit(solution)/shard_map/ppermute | solution.py:488
  40.4 9.0 %all-to-all-start.1 = ((bf16[8,80,128]{2,1,0:T(8,128)(2,1)}), bf16[8,80,128]{2,1,0:T(8,128)(2,1)S(1)}, u32[]{:S(2)}, u32[]{:S(2)}) async-start(bf16[8,80,128]{2,1,0:T(8,128)(2,1)} %get-tuple-element.32), calls=%async_computation.1 | async-start | bytes 327680 | tf_op jit(solution)/shard_map/all_to_all | solution.py:512
  43.8 11.9 %collective-permute-start.3 = (bf16[72,384]{1,0:T(8,128)(2,1)S(1)}, bf16[72,384]{1,0:T(8,128)(2,1)S(1)}, u32[]{:S(2)}, u32[]{:S(2)}) collective-permute-start(bf16[72,384]{1,0:T(8,128)(2,1)S(1)} %get-tuple-element.26), channel_id=1, source_target_pairs={{0,8},{8,16},{16,24},{24,32},{32,40},{40,48},{48,56},{56,64},{64,7... | collective-permute-start | bytes 165896 | tf_op jit(solution)/shard_map/ppermute | solution.py:486
  44.8 10.9 %collective-permute-start.5 = (bf16[72,384]{1,0:T(8,128)(2,1)S(1)}, bf16[72,384]{1,0:T(8,128)(2,1)S(1)}, u32[]{:S(2)}, u32[]{:S(2)}) collective-permute-start(bf16[72,384]{1,0:T(8,128)(2,1)S(1)} %get-tuple-element.28), channel_id=1, source_target_pairs={{0,9},{1,10},{2,11},{3,12},{4,13},{5,14},{6,15},{7,8},{8,17},{9,18... | collective-permute-start | bytes 165896 | tf_op jit(solution)/shard_map/ppermute | solution.py:494
  50.2 15.6 %all-to-all-start.2 = ((bf16[16,96,128]{2,1,0:T(8,128)(2,1)}), bf16[16,96,128]{2,1,0:T(8,128)(2,1)S(1)}, u32[]{:S(2)}, u32[]{:S(2)}) async-start(bf16[16,96,128]{2,1,0:T(8,128)(2,1)} %lat_sum.1), calls=%async_computation.2 | async-start | bytes 786432 | tf_op jit(solution)/shard_map/all_to_all | solution.py:514

commit v3 on v2

--- a/solution.py
+++ b/solution.py
@@ -5,6 +5,7 @@
 from jax import lax
 from jax.experimental import pallas as pl
 from jax.experimental.pallas import tpu as pltpu
+from jax.sharding import Mesh
 from jax.sharding import PartitionSpec as P
 
 HEADS = 6
@@ -19,11 +20,12 @@
 TOK = 576
 SHARES = 16
 WROWS = 72
-GROW = 72
-TROW = 76
-TROWS = 20
-CHUNK = 96
-MID = 80
+CHUNK = 80
+TABLE = 320
+LON = ("x", "yh", "core")
+LAT = ("yl", "z")
+SCATTER = ("yh", "yl", "z")
+REST = ("x", "core")
 LANES = REL * POS
 
 epsilon = 1e-05
@@ -206,7 +208,7 @@
 
 def main_kernel(
     air_ref, up_ref, lonh_ref, lath_ref, corh_ref, gain_ref, wqkv_ref, wproj_ref, bias,
-    own_ref, lono_ref, lato_ref, coro_ref, grad_ref,
+    own_ref, lono_ref, lato_ref, coro_ref, grad_ref, table_ref,
     xt, ut, dbias, q_s, k_s, v_s, dm_s, mix_s, dq_s, dk_s, dv_s, gw, gt, tr, one,
 ):
     for lev, lat, w0, w1 in window_parts():
@@ -296,16 +298,16 @@
                 ]
     tr[0:WIN] = gt[:, 0:128]
     tr[WIN : 2 * WIN] = gt[:, 128:256]
-    tr[2 * WIN :] = jnp.zeros((SHARES * TROWS - 2 * WIN, 128), f32)
+    tr[2 * WIN :] = jnp.zeros((TABLE - 2 * WIN, 128), f32)
     for g in range(6):
         tr[2 * WIN : 2 * WIN + 24, g * 20 : (g + 1) * 20] = gt[g * 24 : (g + 1) * 24, 256:LANES]
 
-    one[GROW:TROW] = jnp.zeros((TROW - GROW, 128), f32)
+    table_ref[...] = tr[...].astype(bf16)
+    one[WROWS:CHUNK] = jnp.zeros((CHUNK - WROWS, 128), f32)
     for i in range(SHARES):
         one[0:WROWS] = gw[i * WROWS : (i + 1) * WROWS]
         if i < 3:
-            one[GROW : GROW + 1] = (dgain[:, :128], high, jnp.zeros((1, 128), f32))[i]
-        one[TROW:CHUNK] = tr[i * TROWS : (i + 1) * TROWS]
+            one[WROWS : WROWS + 1] = (dgain[:, :128], high, jnp.zeros((1, 128), f32))[i]
         grad_ref[i] = one[...].astype(bf16)
 
     hold(xt, dot(mix, wproj_ref[...], NN).astype(bf16).astype(f32))
@@ -329,11 +331,12 @@
     return pl.pallas_call(
         main_kernel,
         in_specs=[vmem] * 9,
-        out_specs=[vmem] * 5,
+        out_specs=[vmem] * 6,
         out_shape=[
             HALOS[1],
             *HALOS,
             jax.ShapeDtypeStruct((SHARES, CHUNK, 128), bf16),
+            jax.ShapeDtypeStruct((TABLE, 128), bf16),
         ],
         scratch_shapes=[
             pltpu.VMEM((2 * TOK, 128), f32),
@@ -344,7 +347,7 @@
         + [
             pltpu.VMEM((SHARES * WROWS, 128), f32),
             pltpu.VMEM((WIN, 384), f32),
-            pltpu.VMEM((SHARES * TROWS, 128), f32),
+            pltpu.VMEM((TABLE, 128), f32),
             pltpu.VMEM((CHUNK, 128), f32),
         ],
         compiler_params=pltpu.CompilerParams(vmem_limit_bytes=40 << 20),
@@ -385,68 +388,68 @@
     return parts[0].astype(bf16)
 
 
-def lon_sum_kernel(parts_ref, copies_ref, table_ref):
+def sum_kernel(*refs):
+    carried = (len(refs) - 2) // 2
+    parts_ref, copies_ref = refs[0], refs[1 + carried]
     one = total(parts_ref)
     for i in range(copies_ref.shape[0]):
-        copies_ref[i] = one[:MID]
-    table_ref[...] = one
-
-
-def lat_sum_kernel(parts_ref, table_ref, copies_ref):
-    one = jnp.concatenate([total(parts_ref), table_ref[MID:]], axis=0)
-    row = lax.broadcasted_iota(jnp.int32, (CHUNK, 1), 0)
-    one = jnp.where(row < TROW, one.astype(f32), table_ref[...].astype(f32)).astype(bf16)
-    for i in range(copies_ref.shape[0]):
         copies_ref[i] = one
 
 
-def lon_sum(parts, lats):
-    vmem = pl.BlockSpec(memory_space=pltpu.VMEM)
-    return pl.pallas_call(
-        lon_sum_kernel,
-        in_specs=[vmem],
-        out_specs=[vmem] * 2,
-        out_shape=[
-            jax.ShapeDtypeStruct((lats, MID, 128), bf16),
-            jax.ShapeDtypeStruct((CHUNK, 128), bf16),
-        ],
+def summed(parts, copies, *carried):
+    vmem = pl.BlockSpec(memory_space=pltpu.VMEM)
+    anywhere = pl.BlockSpec(memory_space=pl.ANY)
+    return pl.pallas_call(
+        sum_kernel,
+        in_specs=[vmem] + [anywhere] * len(carried),
+        out_specs=[vmem] + [anywhere] * len(carried),
+        out_shape=[jax.ShapeDtypeStruct((copies, CHUNK, 128), bf16)]
+        + [jax.ShapeDtypeStruct(array.shape, array.dtype) for array in carried],
+        input_output_aliases={1 + i: 1 + i for i in range(len(carried))},
         compiler_params=pltpu.CompilerParams(vmem_limit_bytes=4 << 20),
-        name="lon_sum",
-    )(parts)
-
-
-def lat_sum(parts, table, lons):
-    vmem = pl.BlockSpec(memory_space=pltpu.VMEM)
-    return pl.pallas_call(
-        lat_sum_kernel,
-        in_specs=[vmem] * 2,
-        out_specs=vmem,
-        out_shape=jax.ShapeDtypeStruct((lons, CHUNK, 128), bf16),
-        compiler_params=pltpu.CompilerParams(vmem_limit_bytes=4 << 20),
-        name="lat_sum",
-    )(parts, table)
-
-
-def unpack_kernel(whole_ref, dwqkv_ref, dwproj_ref, dgain_ref, dtable_ref, gw, tr, gt, flat):
+        name="summed",
+    )(parts, *carried)
+
+
+def unpack_kernel(whole_ref, dwqkv_ref, dwproj_ref, dgain_ref, gw):
     for i in range(SHARES):
         one = whole_ref[i].astype(f32)
         gw[i * WROWS : (i + 1) * WROWS] = one[0:WROWS]
-        tr[i * TROWS : (i + 1) * TROWS] = one[TROW:CHUNK]
         if i == 0:
-            dgain_ref[:, :128] = one[GROW : GROW + 1]
+            dgain_ref[:, :128] = one[WROWS : WROWS + 1]
         if i == 1:
-            dgain_ref[:, 128:] = one[GROW : GROW + 1, :64]
+            dgain_ref[:, 128:] = one[WROWS : WROWS + 1, :64]
     tiles = [gw[t * C : (t + 1) * C] for t in range(6)]
     for t in range(4):
         dwqkv_ref[:, t * 128 : (t + 1) * 128] = tiles[t]
     dwqkv_ref[:, 512:576] = tiles[4][:, :64]
     dwproj_ref[...] = jnp.concatenate([tiles[4][:, 64:], tiles[5]], axis=1)
 
-    gt[:, 0:128] = tr[0:WIN]
-    gt[:, 128:256] = tr[WIN : 2 * WIN]
+
+def unpack(whole):
+    vmem = pl.BlockSpec(memory_space=pltpu.VMEM)
+    return pl.pallas_call(
+        unpack_kernel,
+        in_specs=[vmem],
+        out_specs=[vmem] * 3,
+        out_shape=[
+            jax.ShapeDtypeStruct((C, 3 * C), f32),
+            jax.ShapeDtypeStruct((C, C), f32),
+            jax.ShapeDtypeStruct((1, C), f32),
+        ],
+        scratch_shapes=[pltpu.VMEM((SHARES * WROWS, 128), f32)],
+        compiler_params=pltpu.CompilerParams(vmem_limit_bytes=16 << 20),
+        name="unpack",
+    )(whole)
+
+
+def turn_kernel(tr, dtable_ref, gt, flat):
+    gt[:, 0:128] = tr[0:WIN].astype(f32)
+    gt[:, 128:256] = tr[WIN : 2 * WIN].astype(f32)
     gt[:, 256:384] = jnp.zeros((WIN, 128), f32)
+    last = tr[2 * WIN :].astype(f32)
     for g in range(6):
-        gt[g * 24 : (g + 1) * 24, 256:LANES] = tr[2 * WIN : 2 * WIN + 24, g * 20 : (g + 1) * 20]
+        gt[g * 24 : (g + 1) * 24, 256:LANES] = last[:24, g * 20 : (g + 1) * 20]
     lanes, rows = onehots()
     moved = dot(dot(rows, gt[...].astype(bf16), TN).astype(bf16), lanes, NT)
     for pj in range(POS):
@@ -457,73 +460,75 @@
         dtable_ref[h] = flat[2 * h : 2 * h + 2, 0 : POS * POS * REL]
 
 
-def unpack(whole):
-    vmem = pl.BlockSpec(memory_space=pltpu.VMEM)
-    return pl.pallas_call(
-        unpack_kernel,
+def turned(table):
+    vmem = pl.BlockSpec(memory_space=pltpu.VMEM)
+    return pl.pallas_call(
+        turn_kernel,
         in_specs=[vmem],
-        out_specs=[vmem] * 4,
-        out_shape=[
-            jax.ShapeDtypeStruct((C, 3 * C), f32),
-            jax.ShapeDtypeStruct((C, C), f32),
-            jax.ShapeDtypeStruct((1, C), f32),
-            jax.ShapeDtypeStruct((HEADS, 2, POS * POS * REL), f32),
-        ],
-        scratch_shapes=[
-            pltpu.VMEM((SHARES * WROWS, 128), f32),
-            pltpu.VMEM((SHARES * TROWS, 128), f32),
-            pltpu.VMEM((WIN, 384), f32),
-            pltpu.VMEM((16, 3328), f32),
-        ],
-        compiler_params=pltpu.CompilerParams(vmem_limit_bytes=16 << 20),
-        name="unpack",
-    )(whole)
-
-
-def neighbour(array, lon_by, lat_by):
-    lons, lats = lax.axis_size("lon"), lax.axis_size("lat")
-    if lat_by == 0:
-        return lax.ppermute(array, "lon", [(i, (i + lon_by) % lons) for i in range(lons)])
-    if lon_by == 0:
-        return lax.ppermute(array, "lat", [(i, (i + lat_by) % lats) for i in range(lats)])
-    pairs = [
+        out_specs=vmem,
+        out_shape=jax.ShapeDtypeStruct((HEADS, 2, POS * POS * REL), f32),
+        scratch_shapes=[pltpu.VMEM((WIN, 384), f32), pltpu.VMEM((16, 3328), f32)],
+        compiler_params=pltpu.CompilerParams(vmem_limit_bytes=8 << 20),
+        cost_estimate=pl.CostEstimate(flops=10**9, bytes_accessed=4 << 20, transcendentals=0),
+        name="turn",
+    )(table)
+
+
+def pairs_of(mesh_shape, lon_by, lat_by):
+    lons, lats = (mesh_shape[0], mesh_shape[1])
+    return [
         (i * lats + j, ((i + lon_by) % lons) * lats + (j + lat_by) % lats)
         for i in range(lons)
         for j in range(lats)
     ]
-    return lax.ppermute(array, ("lon", "lat"), pairs)
-
-
-def on_device(air, up, gain, wqkv, wproj, table):
+
+
+def on_device(lons, lats, air, up, gain, wqkv, wproj, table):
+    def neighbour(array, lon_by, lat_by):
+        if lat_by == 0:
+            return lax.ppermute(array, LON, [(i, (i + lon_by) % lons) for i in range(lons)])
+        if lon_by == 0:
+            return lax.ppermute(array, LAT, [(i, (i + lat_by) % lats) for i in range(lats)])
+        return lax.ppermute(array, LON + LAT, pairs_of((lons, lats), lon_by, lat_by))
+
     lonh, lath, corh = pack(air, up)
     lath = neighbour(lath, 0, -1)
     lonh = neighbour(lonh, -1, 0)
     corh = neighbour(corh, -1, -1)
-    last = (lax.axis_index("lat") == lax.axis_size("lat") - 1).astype(jnp.int32).reshape(1)
+    last = (lax.axis_index(LAT) == lats - 1).astype(jnp.int32).reshape(1)
     bias = prep(last, table.transpose(0, 2, 1, 3).reshape(HEADS, 2, POS * POS * REL))
-    own, lono, lato, coro, grads = run_main(
+    own, lono, lato, coro, grads, entries = run_main(
         air, up, lonh, lath, corh, gain.reshape(1, C), wqkv, wproj, bias
     )
+    def paired(entries, step):
+        other = lax.ppermute(entries, LON, [(i, i ^ step) for i in range(lons)])
+        return (entries.astype(f32) + other.astype(f32)).astype(bf16)
+
+    parts = lax.all_to_all(grads, SCATTER, split_axis=0, concat_axis=0, tiled=True)
+    copies, entries, lato, lono, coro = summed(parts, 8, entries, lato, lono, coro)
+    parts = lax.all_to_all(copies, REST, split_axis=0, concat_axis=0, tiled=True)
     latr = neighbour(lato, 0, 1)
     lonr = neighbour(lono, 1, 0)
     corr = neighbour(coro, 1, 1)
-    parts = lax.all_to_all(grads, "lon", split_axis=0, concat_axis=0, tiled=True)
-    copies, table_part = lon_sum(parts, lax.axis_size("lat"))
-    parts = lax.all_to_all(copies, "lat", split_axis=0, concat_axis=0, tiled=True)
-    copies = lat_sum(parts, table_part, lax.axis_size("lon"))
-    whole = lax.all_to_all(copies, "lon", split_axis=0, concat_axis=0, tiled=True)
+    for step in (1, 2, 4):
+        entries = paired(entries, step)
+    (copies,) = summed(parts, SHARES)
+    whole = lax.all_to_all(copies, SCATTER, split_axis=0, concat_axis=0, tiled=True)
+    entries = paired(entries, 8)
+    d_table = turned(entries)
     block_out, d_state = combine(air, up, own, lonr, latr, corr)
-    d_wqkv, d_wproj, d_gain, d_table = unpack(whole)
+    d_wqkv, d_wproj, d_gain = unpack(whole)
     d_table = d_table.reshape(1, HEADS, 2, POS * POS * REL).transpose(0, 2, 1, 3)
     return (block_out, d_state, d_gain.reshape(C), d_wqkv, d_wproj, d_table)
 
 
 def solution(mesh):
-    grid = P(None, "lat", "lon", None)
+    fine = Mesh(mesh.devices.reshape(4, 2, 2, 2, 4), LON + LAT)
+    grid = P(None, LAT, LON, None)
     return jax.shard_map(
-        on_device,
-        mesh=mesh,
-        in_specs=(grid, grid, P(), P(), P(), P("lat", None, None, None)),
-        out_specs=(grid, grid, P(), P(), P(), P("lat", None, None, None)),
+        functools.partial(on_device, mesh.shape["lon"], mesh.shape["lat"]),
+        mesh=fine,
+        in_specs=(grid, grid, P(), P(), P(), P(LAT, None, None, None)),
+        out_specs=(grid, grid, P(), P(), P(), P(LAT, None, None, None)),
         check_vma=False,
     )

time: 67.9 us -> 65.1 us (0.959)
  the two profiles are of different devices: /device:TPU:1 before, /device:TPU:2 now
where the time goes in v3:
time: 65.1 us; the launch traced here: 64.8 us
  starting transfers between devices  24.5 us (38%)
  blocking collectives  15.7 us (24%)
  Pallas kernels  14.2 us (22%)
  waiting for transfers between devices  9.38 us (14%)
  between operations  0.78 us (1%)
    all_to_all x1, blocking collectives, on_device(): lax.all_to_all(grads, SCATTER, split_axis=0, concat_axis=0, tiled=True)  15.7 us
    ppermute x2, starting transfers between devices, neighbour(): lax.ppermute(array, LAT, [(i, (i + lat_by) % lats) for i in range(lats)])  6.17 us
    all_to_all x1, starting transfers between devices, on_device(): lax.all_to_all(copies, SCATTER, split_axis=0, concat_axis=0, tiled=True)  6.11 us
    pallas_call x1, Pallas kernels, run_main(): pl.pallas_call(main_kernel, in_specs=[vmem] * 9, out_specs=[vmem] * 6, ou...  5.99 us
    all_to_all x1, starting transfers between devices, on_device(): lax.all_to_all(copies, REST, split_axis=0, concat_axis=0, tiled=True)  4.84 us
    ppermute x4, waiting for transfers between devices, paired(): other = lax.ppermute(entries, LON, [(i, i ^ step) for i in range(lons)])  4.72 us
    ppermute x4, starting transfers between devices, paired(): other = lax.ppermute(entries, LON, [(i, i ^ step) for i in range(lons)])  3.4 us
    pallas_call x1, Pallas kernels, prep(): pl.pallas_call(prep_kernel, in_specs=[smem, vmem], out_specs=vmem, out_sh...  2.04 us
  transfers between devices with their start and end apart: 12, of which 5 were waited for; matrix products, arithmetic and copies ran while one was open for 0% of the time, Pallas kernels for 8%

profile of v3, /device:TPU:2, one launch (start us, length us, event | category | flops | bytes accessed | tf_op | source)
XLA Modules:
  0.0 64.8 jit_solution(16987470864361328789)
XLA Ops:
  0.6 1.3 %pack.1 = (bf16[72,384]{1,0:T(8,128)(2,1)S(1)}, bf16[216,384]{1,0:T(8,128)(2,1)S(1)}, bf16[72,384]{1,0:T(8,128)(2,1)S(1)}) custom-call(bf16[4,6,24,192]{3,2,1,0:T(8,128)(2,1)} %air_ref.3, bf16[4,6,24,192]{3,2,1,0:T(8,128)(2,1)} %up_ref.3), custom_call_target="tpu_custom_call" | custom-call | tf_op jit(solution)/shard_map/pack/pallas_call | solution.py:120
  1.9 5.1 %collective-permute-start.1 = (bf16[216,384]{1,0:T(8,128)(2,1)S(1)}, bf16[216,384]{1,0:T(8,128)(2,1)S(1)}, u32[]{:S(2)}, u32[]{:S(2)}) collective-permute-start(bf16[216,384]{1,0:T(8,128)(2,1)S(1)} %get-tuple-element.26), channel_id=1, source_target_pairs={{0,7},{1,0},{2,1},{3,2},{4,3},{5,4},{6,5},{7,6},{8,15},{9,8},{10,9... | collective-permute-start | bytes 497672 | tf_op jit(solution)/shard_map/ppermute | solution.py:491
  7.0 2.0 %collective-permute-start = (bf16[72,384]{1,0:T(8,128)(2,1)S(1)}, bf16[72,384]{1,0:T(8,128)(2,1)S(1)}, u32[]{:S(2)}, u32[]{:S(2)}) collective-permute-start(bf16[72,384]{1,0:T(8,128)(2,1)S(1)} %get-tuple-element.25), channel_id=1, source_target_pairs={{0,120},{8,0},{16,8},{24,16},{32,24},{40,32},{48,40},{56,48},{64,5... | collective-permute-start | bytes 165896 | tf_op jit(solution)/shard_map/ppermute | solution.py:489
  9.1 0.0 collective-permute-start.2
  9.1 0.0 copy-start.3
  9.1 0.0 copy-start.4
  9.1 2.0 %prep.1.bias = f32[2,144,864]{2,1,0:T(8,128)S(1)} custom-call(s32[1]{0:T(128)} %bitcast.1.last_ref, f32[6,2,3312]{2,1,0:T(2,128)S(1)} %bitcast.9), custom_call_target="tpu_custom_call" | custom-call | flops 100000000 | bytes 2097152 | tf_op jit(solution)/shard_map/prep/pallas_call | solution.py:197
  11.1 0.0 copy-start.5
  11.2 0.0 collective-permute-done.lonh_ref
  11.2 1.5 %collective-permute-done.2.corh_ref = bf16[72,384]{1,0:T(8,128)(2,1)S(1)} collective-permute-done((bf16[72,384]{1,0:T(8,128)(2,1)S(1)}, bf16[72,384]{1,0:T(8,128)(2,1)S(1)}, u32[]{:S(2)}, u32[]{:S(2)}) %collective-permute-start.2) | collective-permute-done | bytes 55328 | tf_op jit(solution)/shard_map/ppermute | solution.py:492
  12.6 0.0 collective-permute-done.1.lath_ref
  12.7 6.0 %sublayer.1 = (bf16[216,384]{1,0:T(8,128)(2,1)S(1)}, bf16[72,384]{1,0:T(8,128)(2,1)S(1)}, bf16[216,384]{1,0:T(8,128)(2,1)S(1)}, bf16[72,384]{1,0:T(8,128)(2,1)S(...) custom-call(bf16[4,6,24,192]{3,2,1,0:T(8,128)(2,1)S(1)} %copy-done, ...), custom_call_target="tpu_custom_call" | custom-call | flops 1000000000 | bytes 4194304 | tf_op jit(solution)/shard_map/sublayer/pallas_call | solution.py:331
  18.7 15.7 %all_to_all.15.refs_0_ = bf16[16,80,128]{2,1,0:T(8,128)(2,1)S(1)} all-to-all(bf16[16,80,128]{2,1,0:T(8,128)(2,1)S(1)} %get-tuple-element.29), channel_id=1, replica_groups=mesh['x'=4,'yh'=2,'core'=2,'yl'=2,'z'=4] {'yh','yl','z'}, dimensions={0} | all-to-all | bytes 655360 | tf_op jit(solution)/shard_map/all_to_all | solution.py:507
  34.4 0.7 %summed.2 = (bf16[8,80,128]{2,1,0:T(8,128)(2,1)}, bf16[320,128]{1,0:T(8,128)(2,1)S(1)}, bf16[216,384]{1,0:T(8,128)(2,1)S(1)}, bf16[72,384]{1,0:T(8,128)(2,1)S(1)}, bf16[72,384]{1,0:T(8,128)(2,1)S(1)}) custom-call(bf16[16,80,128]{2,1,0:T(8,128)(2,1)S(1)} %all_to_all.15.refs_0_, ...), custom_call_target="tpu_custom_call", output_to_operand_aliasing={{1}: (1, {}), {2}: (2, {}), {3}: (3, {}), {4}: (4, {})} | custom-call | tf_op jit(solution)/shard_map/summed/pallas_call | solution.py:402
  35.1 0.0 collective-permute-start.6
  35.1 1.3 %collective-permute-done.6 = bf16[320,128]{1,0:T(8,128)(2,1)S(1)} collective-permute-done((bf16[320,128]{1,0:T(8,128)(2,1)S(1)}, bf16[320,128]{1,0:T(8,128)(2,1)S(1)}, u32[]{:S(2)}, u32[]{:S(2)}) %collective-permute-start.6) | collective-permute-done | bytes 81952 | tf_op jit(solution)/shard_map/ppermute | solution.py:504
  36.4 1.5 %collective-permute-start.7 = (bf16[320,128]{1,0:T(8,128)(2,1)S(1)}, bf16[320,128]{1,0:T(8,128)(2,1)S(1)}, u32[]{:S(2)}, u32[]{:S(2)}) collective-permute-start(bf16[320,128]{1,0:T(8,128)(2,1)S(1)} %add_convert_fusion.3), channel_id=1, source_target_pairs={{0,16},{8,24},{16,0},{24,8},{32,48},{40,56},{48,32},{56,40},{64,80... | collective-permute-start | bytes 245768 | tf_op jit(solution)/shard_map/ppermute | solution.py:504
  37.9 4.8 %all-to-all-start.1 = ((bf16[8,80,128]{2,1,0:T(8,128)(2,1)}), bf16[8,80,128]{2,1,0:T(8,128)(2,1)S(1)}, u32[]{:S(2)}, u32[]{:S(2)}) async-start(bf16[8,80,128]{2,1,0:T(8,128)(2,1)} %get-tuple-element.39), calls=%async_computation.1 | async-start | bytes 327680 | tf_op jit(solution)/shard_map/all_to_all | solution.py:509
  42.7 0.0 collective-permute-done.7
  42.8 0.4 collective-permute-start.8
  43.2 0.0 collective-permute-start.3
  43.2 2.0 %collective-permute-start.5 = (bf16[72,384]{1,0:T(8,128)(2,1)S(1)}, bf16[72,384]{1,0:T(8,128)(2,1)S(1)}, u32[]{:S(2)}, u32[]{:S(2)}) collective-permute-start(bf16[72,384]{1,0:T(8,128)(2,1)S(1)} %get-tuple-element.36), channel_id=1, source_target_pairs={{0,9},{1,10},{2,11},{3,12},{4,13},{5,14},{6,15},{7,8},{8,17},{9,18... | collective-permute-start | bytes 165896 | tf_op jit(solution)/shard_map/ppermute | solution.py:492
  45.2 1.1 %collective-permute-start.4 = (bf16[216,384]{1,0:T(8,128)(2,1)S(1)}, bf16[216,384]{1,0:T(8,128)(2,1)S(1)}, u32[]{:S(2)}, u32[]{:S(2)}) collective-permute-start(bf16[216,384]{1,0:T(8,128)(2,1)S(1)} %get-tuple-element.35), channel_id=1, source_target_pairs={{0,1},{1,2},{2,3},{3,4},{4,5},{5,6},{6,7},{7,0},{8,9},{9,10},{10,1... | collective-permute-start | bytes 497672 | tf_op jit(solution)/shard_map/ppermute | solution.py:491
  46.2 2.0 %all-to-all-done.1.refs_0_ = bf16[8,80,128]{2,1,0:T(8,128)(2,1)S(1)} async-done(((bf16[8,80,128]{2,1,0:T(8,128)(2,1)}), bf16[8,80,128]{2,1,0:T(8,128)(2,1)S(1)}, u32[]{:S(2)}, u32[]{:S(2)}) %all-to-all-start.1) | async-done | bytes 163872 | tf_op jit(solution)/shard_map/all_to_all | solution.py:509
  48.2 0.8 %summed.3 = bf16[16,80,128]{2,1,0:T(8,128)(2,1)} custom-call(bf16[8,80,128]{2,1,0:T(8,128)(2,1)S(1)} %all-to-all-done.1.refs_0_), custom_call_target="tpu_custom_call" | custom-call | tf_op jit(solution)/shard_map/summed/pallas_call | solution.py:402
  49.0 6.1 %all-to-all-start.2 = ((bf16[16,80,128]{2,1,0:T(8,128)(2,1)}), bf16[16,80,128]{2,1,0:T(8,128)(2,1)S(1)}, u32[]{:S(2)}, u32[]{:S(2)}) async-start(bf16[16,80,128]{2,1,0:T(8,128)(2,1)} %summed.3), calls=%async_computation.2 | async-start | bytes 655360 | tf_op jit(solution)/shard_map/all_to_all | solution.py:516
  55.1 1.5 %collective-permute-start.9 = (bf16[320,128]{1,0:T(8,128)(2,1)S(1)}, bf16[320,128]{1,0:T(8,128)(2,1)S(1)}, u32[]{:S(2)}, u32[]{:S(2)}) collective-permute-start(bf16[320,128]{1,0:T(8,128)(2,1)S(1)} %add_convert_fusion.1), channel_id=1, source_target_pairs={{0,64},{8,72},{16,80},{24,88},{32,96},{40,104},{48,112},{56,120},{... | collective-permute-start | bytes 245768 | tf_op jit(solution)/shard_map/ppermute | solution.py:504
  56.7 1.0 %combine.1 = (bf16[4,6,24,192]{3,2,1,0:T(8,128)(2,1)}, bf16[4,6,24,192]{3,2,1,0:T(8,128)(2,1)}) custom-call(bf16[4,6,24,192]{3,2,1,0:T(8,128)(2,1)S(1)} %copy-done, bf16[4,6,24,192]{3,2,1,0:T(8,128)(2,1)S(1)} %copy-done.1, bf16[216,384]{1,0:T(8,128)(2,1)S(1)} %get-tuple-element.28.own_ref, bf16[72,384]{1,0:T(8,128)(2,1)S(1)} %collective-permute-done.3.lonr_ref, ...), custom_call_target="tpu_custom_call" | custom-call | flops 10000000000 | bytes 41943040 | tf_op jit(solution)/shard_map/combine/pallas_call | solution.py:373
  57.7 3.4 %collective-permute-done.9 = bf16[320,128]{1,0:T(8,128)(2,1)S(1)} collective-permute-done((bf16[320,128]{1,0:T(8,128)(2,1)S(1)}, bf16[320,128]{1,0:T(8,128)(2,1)S(1)}, u32[]{:S(2)}, u32[]{:S(2)}) %collective-permute-start.9) | collective-permute-done | bytes 81952 | tf_op jit(solution)/shard_map/ppermute | solution.py:504
  61.2 1.6 %turn.1 = f32[6,2,3312]{2,1,0:T(2,128)} custom-call(bf16[320,128]{1,0:T(8,128)(2,1)S(1)} %add_convert_fusion.tr), custom_call_target="tpu_custom_call" | custom-call | flops 1000000000 | bytes 4194304 | tf_op jit(solution)/shard_map/turn/pallas_call | solution.py:465
  62.7 1.2 %all-to-all-done.2.whole_ref = bf16[16,80,128]{2,1,0:T(8,128)(2,1)S(1)} async-done(((bf16[16,80,128]{2,1,0:T(8,128)(2,1)}), bf16[16,80,128]{2,1,0:T(8,128)(2,1)S(1)}, u32[]{:S(2)}, u32[]{:S(2)}) %all-to-all-start.2) | async-done | bytes 327712 | tf_op jit(solution)/shard_map/all_to_all | solution.py:516
  63.9 0.9 %unpack.1 = (f32[192,576]{1,0:T(8,128)}, f32[192,192]{1,0:T(8,128)}, f32[1,192]{1,0:T(1,128)}) custom-call(bf16[16,80,128]{2,1,0:T(8,128)(2,1)S(1)} %all-to-all-done.2.whole_ref), custom_call_target="tpu_custom_call" | custom-call | tf_op jit(solution)/shard_map/unpack/pallas_call | solution.py:431
  (17 shorter events, 0.1 us)
Async XLA Ops:
  0.6 8.4 %copy-start.2 = (f32[1,2,6,3312]{3,1,2,0:T(2,128)S(1)}, f32[1,2,6,3312]{3,1,2,0:T(2,128)}, u32[]{:S(2)}) copy-start(f32[1,2,6,3312]{3,1,2,0:T(2,128)} %param.11) | copy-start | bytes 476932
  1.9 10.7 %collective-permute-start.1 = (bf16[216,384]{1,0:T(8,128)(2,1)S(1)}, bf16[216,384]{1,0:T(8,128)(2,1)S(1)}, u32[]{:S(2)}, u32[]{:S(2)}) collective-permute-start(bf16[216,384]{1,0:T(8,128)(2,1)S(1)} %get-tuple-element.26), channel_id=1, source_target_pairs={{0,7},{1,0},{2,1},{3,2},{4,3},{5,4},{6,5},{7,6},{8,15},{9,8},{10,9... | collective-permute-start | bytes 497672 | tf_op jit(solution)/shard_map/ppermute | solution.py:491
  7.0 4.1 %collective-permute-start = (bf16[72,384]{1,0:T(8,128)(2,1)S(1)}, bf16[72,384]{1,0:T(8,128)(2,1)S(1)}, u32[]{:S(2)}, u32[]{:S(2)}) collective-permute-start(bf16[72,384]{1,0:T(8,128)(2,1)S(1)} %get-tuple-element.25), channel_id=1, source_target_pairs={{0,120},{8,0},{16,8},{24,16},{32,24},{40,32},{48,40},{56,48},{64,5... | collective-permute-start | bytes 165896 | tf_op jit(solution)/shard_map/ppermute | solution.py:489
  9.1 3.6 %collective-permute-start.2 = (bf16[72,384]{1,0:T(8,128)(2,1)S(1)}, bf16[72,384]{1,0:T(8,128)(2,1)S(1)}, u32[]{:S(2)}, u32[]{:S(2)}) collective-permute-start(bf16[72,384]{1,0:T(8,128)(2,1)S(1)} %get-tuple-element.27), channel_id=1, source_target_pairs={{0,127},{1,120},{2,121},{3,122},{4,123},{5,124},{6,125},{7,126},{8... | collective-permute-start | bytes 165896 | tf_op jit(solution)/shard_map/ppermute | solution.py:492
  9.1 3.6 %copy-start = (bf16[4,6,24,192]{3,2,1,0:T(8,128)(2,1)S(1)}, bf16[4,6,24,192]{3,2,1,0:T(8,128)(2,1)}, u32[]{:S(2)}) copy-start(bf16[4,6,24,192]{3,2,1,0:T(8,128)(2,1)} %air_ref.3) | copy-start | bytes 663556
  9.1 3.6 %copy-start.1 = (bf16[4,6,24,192]{3,2,1,0:T(8,128)(2,1)S(1)}, bf16[4,6,24,192]{3,2,1,0:T(8,128)(2,1)}, u32[]{:S(2)}) copy-start(bf16[4,6,24,192]{3,2,1,0:T(8,128)(2,1)} %up_ref.3) | copy-start | bytes 663556
  9.1 3.6 %copy-start.3 = (bf16[192,576]{1,0:T(8,128)(2,1)S(1)}, bf16[192,576]{1,0:T(8,128)(2,1)}, u32[]{:S(2)}) copy-start(bf16[192,576]{1,0:T(8,128)(2,1)} %wqkv_ref.1) | copy-start | bytes 663556
  9.1 3.6 %copy-start.4 = (bf16[192,192]{1,0:T(8,128)(2,1)S(1)}, bf16[192,192]{1,0:T(8,128)(2,1)}, u32[]{:S(2)}) copy-start(bf16[192,192]{1,0:T(8,128)(2,1)} %wproj_ref.1) | copy-start | bytes 221188
  11.1 1.5 %copy-start.5 = (f32[192]{0:T(256)S(1)}, f32[192]{0:T(256)}, u32[]{:S(2)}) copy-start(f32[192]{0:T(256)} %param.8) | copy-start | bytes 2308
  35.1 1.3 %collective-permute-start.6 = (bf16[320,128]{1,0:T(8,128)(2,1)S(1)}, bf16[320,128]{1,0:T(8,128)(2,1)S(1)}, u32[]{:S(2)}, u32[]{:S(2)}) collective-permute-start(bf16[320,128]{1,0:T(8,128)(2,1)S(1)} %get-tuple-element.43), channel_id=1, source_target_pairs={{0,8},{8,0},{16,24},{24,16},{32,40},{40,32},{48,56},{56,48},{64,72... | collective-permute-start | bytes 245768 | tf_op jit(solution)/shard_map/ppermute | solution.py:504
  36.4 6.3 %collective-permute-start.7 = (bf16[320,128]{1,0:T(8,128)(2,1)S(1)}, bf16[320,128]{1,0:T(8,128)(2,1)S(1)}, u32[]{:S(2)}, u32[]{:S(2)}) collective-permute-start(bf16[320,128]{1,0:T(8,128)(2,1)S(1)} %add_convert_fusion.3), channel_id=1, source_target_pairs={{0,16},{8,24},{16,0},{24,8},{32,48},{40,56},{48,32},{56,40},{64,80... | collective-permute-start | bytes 245768 | tf_op jit(solution)/shard_map/ppermute | solution.py:504
  37.9 10.3 %all-to-all-start.1 = ((bf16[8,80,128]{2,1,0:T(8,128)(2,1)}), bf16[8,80,128]{2,1,0:T(8,128)(2,1)S(1)}, u32[]{:S(2)}, u32[]{:S(2)}) async-start(bf16[8,80,128]{2,1,0:T(8,128)(2,1)} %get-tuple-element.39), calls=%async_computation.1 | async-start | bytes 327680 | tf_op jit(solution)/shard_map/all_to_all | solution.py:509
  42.8 12.3 %collective-permute-start.8 = (bf16[320,128]{1,0:T(8,128)(2,1)S(1)}, bf16[320,128]{1,0:T(8,128)(2,1)S(1)}, u32[]{:S(2)}, u32[]{:S(2)}) collective-permute-start(bf16[320,128]{1,0:T(8,128)(2,1)S(1)} %add_convert_fusion.2), channel_id=1, source_target_pairs={{0,32},{8,40},{16,48},{24,56},{32,0},{40,8},{48,16},{56,24},{64,96... | collective-permute-start | bytes 245768 | tf_op jit(solution)/shard_map/ppermute | solution.py:504
  43.2 13.5 %collective-permute-start.3 = (bf16[72,384]{1,0:T(8,128)(2,1)S(1)}, bf16[72,384]{1,0:T(8,128)(2,1)S(1)}, u32[]{:S(2)}, u32[]{:S(2)}) collective-permute-start(bf16[72,384]{1,0:T(8,128)(2,1)S(1)} %get-tuple-element.34), channel_id=1, source_target_pairs={{0,8},{8,16},{16,24},{24,32},{32,40},{40,48},{48,56},{56,64},{64,7... | collective-permute-start | bytes 165896 | tf_op jit(solution)/shard_map/ppermute | solution.py:489
  43.2 13.5 %collective-permute-start.5 = (bf16[72,384]{1,0:T(8,128)(2,1)S(1)}, bf16[72,384]{1,0:T(8,128)(2,1)S(1)}, u32[]{:S(2)}, u32[]{:S(2)}) collective-permute-start(bf16[72,384]{1,0:T(8,128)(2,1)S(1)} %get-tuple-element.36), channel_id=1, source_target_pairs={{0,9},{1,10},{2,11},{3,12},{4,13},{5,14},{6,15},{7,8},{8,17},{9,18... | collective-permute-start | bytes 165896 | tf_op jit(solution)/shard_map/ppermute | solution.py:492
  45.2 11.5 %collective-permute-start.4 = (bf16[216,384]{1,0:T(8,128)(2,1)S(1)}, bf16[216,384]{1,0:T(8,128)(2,1)S(1)}, u32[]{:S(2)}, u32[]{:S(2)}) collective-permute-start(bf16[216,384]{1,0:T(8,128)(2,1)S(1)} %get-tuple-element.35), channel_id=1, source_target_pairs={{0,1},{1,2},{2,3},{3,4},{4,5},{5,6},{6,7},{7,0},{8,9},{9,10},{10,1... | collective-permute-start | bytes 497672 | tf_op jit(solution)/shard_map/ppermute | solution.py:491
  49.0 14.9 %all-to-all-start.2 = ((bf16[16,80,128]{2,1,0:T(8,128)(2,1)}), bf16[16,80,128]{2,1,0:T(8,128)(2,1)S(1)}, u32[]{:S(2)}, u32[]{:S(2)}) async-start(bf16[16,80,128]{2,1,0:T(8,128)(2,1)} %summed.3), calls=%async_computation.2 | async-start | bytes 655360 | tf_op jit(solution)/shard_map/all_to_all | solution.py:516
  55.1 6.0 %collective-permute-start.9 = (bf16[320,128]{1,0:T(8,128)(2,1)S(1)}, bf16[320,128]{1,0:T(8,128)(2,1)S(1)}, u32[]{:S(2)}, u32[]{:S(2)}) collective-permute-start(bf16[320,128]{1,0:T(8,128)(2,1)S(1)} %add_convert_fusion.1), channel_id=1, source_target_pairs={{0,64},{8,72},{16,80},{24,88},{32,96},{40,104},{48,112},{56,120},{... | collective-permute-start | bytes 245768 | tf_op jit(solution)/shard_map/ppermute | solution.py:504

commit v4 on v3

--- a/solution.py
+++ b/solution.py
@@ -249,29 +249,37 @@
             total = jnp.where(lane_head == h, stacked[h * WIN : (h + 1) * WIN], total)
         return total
 
-    def window(w):
+    def begin(w):
+        rows = pl.ds(w * WIN, WIN)
+        qs = spread(q_s[rows, :])
+        scores = dot(k_s[rows, :], qs, NT)
+        return rows, qs, scores, dot(v_s[rows, :], spread(dm_s[rows, :]), NT)
+
+    def middle(w, state):
+        rows, qs, scores, dprobs = state
         a = w // 2
-        rows = pl.ds(w * WIN, WIN)
-        k, v = k_s[rows, :], v_s[rows, :]
-        qs = spread(q_s[rows, :])
-        scores = dot(k, qs, NT) * scale + bias[a]
+        scores = scores * scale + bias[a]
         top = jnp.max(scores, axis=0, keepdims=True)
         weights = jnp.exp(scores - top)
         probs = weights * (1.0 / jnp.sum(weights, axis=0, keepdims=True))
-        soft = probs.astype(bf16)
-        mix_s[rows, :] = gathered(dot(soft, v, TN)).astype(bf16)
-        ds = spread(dm_s[rows, :])
-        dprobs = dot(v, ds, NT)
-        dv_s[rows, :] = dot(soft, ds, NN).astype(bf16)
         inner = jnp.sum(probs * dprobs, axis=0, keepdims=True)
         dscores = probs * (dprobs - inner)
         dbias[a] += dscores
-        dsc = dscores.astype(bf16)
+        return rows, qs, probs.astype(bf16), dscores.astype(bf16)
+
+    def end(w, state):
+        rows, qs, soft, dsc = state
+        mix_s[rows, :] = gathered(dot(soft, v_s[rows, :], TN)).astype(bf16)
+        dv_s[rows, :] = dot(soft, spread(dm_s[rows, :]), NN).astype(bf16)
         dk_s[rows, :] = (dot(dsc, qs, NN) * scale).astype(bf16)
-        dq_s[rows, :] = (gathered(dot(dsc, k, TN)) * scale).astype(bf16)
-
+        dq_s[rows, :] = (gathered(dot(dsc, k_s[rows, :], TN)) * scale).astype(bf16)
+
+    ready = begin(0)
     for w in range(4):
-        window(w)
+        done = middle(w, ready)
+        if w < 3:
+            ready = begin(w + 1)
+        end(w, done)
 
     mix = mix_s[...]
     mq, mk, mv = (dot(normed, d[...], TN) for d in (dq_s, dk_s, dv_s))

time: 65.1 us -> 64.4 us (0.989)
  Pallas kernels: 14.2 us -> 13.4 us
    pallas_call x1, Pallas kernels: 5.99 us -> 5.21 us  [run_main(): pl.pallas_call(main_kernel, in_specs=[vmem] * 9, out_specs=[vmem] * 6, ou...]
where the time goes in v4:
time: 64.4 us; the launch traced here: 64 us
  starting transfers between devices  24.5 us (38%)
  blocking collectives  15.8 us (25%)
  Pallas kernels  13.4 us (21%)
  waiting for transfers between devices  9.38 us (15%)
  between operations  0.78 us (1%)
    all_to_all x1, blocking collectives, on_device(): lax.all_to_all(grads, SCATTER, split_axis=0, concat_axis=0, tiled=True)  15.8 us
    ppermute x2, starting transfers between devices, neighbour(): lax.ppermute(array, LAT, [(i, (i + lat_by) % lats) for i in range(lats)])  6.16 us
    all_to_all x1, starting transfers between devices, on_device(): lax.all_to_all(copies, SCATTER, split_axis=0, concat_axis=0, tiled=True)  6.1 us
    pallas_call x1, Pallas kernels, run_main(): pl.pallas_call(main_kernel, in_specs=[vmem] * 9, out_specs=[vmem] * 6, ou...  5.21 us
    all_to_all x1, starting transfers between devices, on_device(): lax.all_to_all(copies, REST, split_axis=0, concat_axis=0, tiled=True)  4.82 us
    ppermute x4, waiting for transfers between devices, paired(): other = lax.ppermute(entries, LON, [(i, i ^ step) for i in range(lons)])  4.72 us
    ppermute x4, starting transfers between devices, paired(): other = lax.ppermute(entries, LON, [(i, i ^ step) for i in range(lons)])  3.42 us
    pallas_call x1, Pallas kernels, prep(): pl.pallas_call(prep_kernel, in_specs=[smem, vmem], out_specs=vmem, out_sh...  2.04 us
  transfers between devices with their start and end apart: 12, of which 5 were waited for; matrix products, arithmetic and copies ran while one was open for 0% of the time, Pallas kernels for 8%

profile of v4, /device:TPU:2, one launch (start us, length us, event | category | flops | bytes accessed | tf_op | source)
XLA Modules:
  0.0 64.0 jit_solution(8222421226807289276)
XLA Ops:
  0.6 1.3 %pack.1 = (bf16[72,384]{1,0:T(8,128)(2,1)S(1)}, bf16[216,384]{1,0:T(8,128)(2,1)S(1)}, bf16[72,384]{1,0:T(8,128)(2,1)S(1)}) custom-call(bf16[4,6,24,192]{3,2,1,0:T(8,128)(2,1)} %air_ref.3, bf16[4,6,24,192]{3,2,1,0:T(8,128)(2,1)} %up_ref.3), custom_call_target="tpu_custom_call" | custom-call | tf_op jit(solution)/shard_map/pack/pallas_call | solution.py:120
  1.9 5.1 %collective-permute-start.1 = (bf16[216,384]{1,0:T(8,128)(2,1)S(1)}, bf16[216,384]{1,0:T(8,128)(2,1)S(1)}, u32[]{:S(2)}, u32[]{:S(2)}) collective-permute-start(bf16[216,384]{1,0:T(8,128)(2,1)S(1)} %get-tuple-element.26), channel_id=1, source_target_pairs={{0,7},{1,0},{2,1},{3,2},{4,3},{5,4},{6,5},{7,6},{8,15},{9,8},{10,9... | collective-permute-start | bytes 497672 | tf_op jit(solution)/shard_map/ppermute | solution.py:499
  7.0 2.0 %collective-permute-start = (bf16[72,384]{1,0:T(8,128)(2,1)S(1)}, bf16[72,384]{1,0:T(8,128)(2,1)S(1)}, u32[]{:S(2)}, u32[]{:S(2)}) collective-permute-start(bf16[72,384]{1,0:T(8,128)(2,1)S(1)} %get-tuple-element.25), channel_id=1, source_target_pairs={{0,120},{8,0},{16,8},{24,16},{32,24},{40,32},{48,40},{56,48},{64,5... | collective-permute-start | bytes 165896 | tf_op jit(solution)/shard_map/ppermute | solution.py:497
  9.1 0.0 collective-permute-start.2
  9.1 0.0 copy-start.3
  9.1 0.0 copy-start.4
  9.1 2.0 %prep.1.bias = f32[2,144,864]{2,1,0:T(8,128)S(1)} custom-call(s32[1]{0:T(128)} %bitcast.1.last_ref, f32[6,2,3312]{2,1,0:T(2,128)S(1)} %bitcast.9), custom_call_target="tpu_custom_call" | custom-call | flops 100000000 | bytes 2097152 | tf_op jit(solution)/shard_map/prep/pallas_call | solution.py:197
  11.1 0.0 copy-start.5
  11.2 0.0 collective-permute-done.lonh_ref
  11.2 1.5 %collective-permute-done.2.corh_ref = bf16[72,384]{1,0:T(8,128)(2,1)S(1)} collective-permute-done((bf16[72,384]{1,0:T(8,128)(2,1)S(1)}, bf16[72,384]{1,0:T(8,128)(2,1)S(1)}, u32[]{:S(2)}, u32[]{:S(2)}) %collective-permute-start.2) | collective-permute-done | bytes 55328 | tf_op jit(solution)/shard_map/ppermute | solution.py:500
  12.6 0.0 collective-permute-done.1.lath_ref
  12.7 5.2 %sublayer.1 = (bf16[216,384]{1,0:T(8,128)(2,1)S(1)}, bf16[72,384]{1,0:T(8,128)(2,1)S(1)}, bf16[216,384]{1,0:T(8,128)(2,1)S(1)}, bf16[72,384]{1,0:T(8,128)(2,1)S(...) custom-call(bf16[4,6,24,192]{3,2,1,0:T(8,128)(2,1)S(1)} %copy-done, ...), custom_call_target="tpu_custom_call" | custom-call | flops 1000000000 | bytes 4194304 | tf_op jit(solution)/shard_map/sublayer/pallas_call | solution.py:339
  17.9 15.8 %all_to_all.15.refs_0_ = bf16[16,80,128]{2,1,0:T(8,128)(2,1)S(1)} all-to-all(bf16[16,80,128]{2,1,0:T(8,128)(2,1)S(1)} %get-tuple-element.29), channel_id=1, replica_groups=mesh['x'=4,'yh'=2,'core'=2,'yl'=2,'z'=4] {'yh','yl','z'}, dimensions={0} | all-to-all | bytes 655360 | tf_op jit(solution)/shard_map/all_to_all | solution.py:515
  33.6 0.7 %summed.2 = (bf16[8,80,128]{2,1,0:T(8,128)(2,1)}, bf16[320,128]{1,0:T(8,128)(2,1)S(1)}, bf16[216,384]{1,0:T(8,128)(2,1)S(1)}, bf16[72,384]{1,0:T(8,128)(2,1)S(1)}, bf16[72,384]{1,0:T(8,128)(2,1)S(1)}) custom-call(bf16[16,80,128]{2,1,0:T(8,128)(2,1)S(1)} %all_to_all.15.refs_0_, ...), custom_call_target="tpu_custom_call", output_to_operand_aliasing={{1}: (1, {}), {2}: (2, {}), {3}: (3, {}), {4}: (4, {})} | custom-call | tf_op jit(solution)/shard_map/summed/pallas_call | solution.py:410
  34.4 0.0 collective-permute-start.6
  34.4 1.3 %collective-permute-done.6 = bf16[320,128]{1,0:T(8,128)(2,1)S(1)} collective-permute-done((bf16[320,128]{1,0:T(8,128)(2,1)S(1)}, bf16[320,128]{1,0:T(8,128)(2,1)S(1)}, u32[]{:S(2)}, u32[]{:S(2)}) %collective-permute-start.6) | collective-permute-done | bytes 81952 | tf_op jit(solution)/shard_map/ppermute | solution.py:512
  35.7 1.5 %collective-permute-start.7 = (bf16[320,128]{1,0:T(8,128)(2,1)S(1)}, bf16[320,128]{1,0:T(8,128)(2,1)S(1)}, u32[]{:S(2)}, u32[]{:S(2)}) collective-permute-start(bf16[320,128]{1,0:T(8,128)(2,1)S(1)} %add_convert_fusion.3), channel_id=1, source_target_pairs={{0,16},{8,24},{16,0},{24,8},{32,48},{40,56},{48,32},{56,40},{64,80... | collective-permute-start | bytes 245768 | tf_op jit(solution)/shard_map/ppermute | solution.py:512
  37.1 4.8 %all-to-all-start.1 = ((bf16[8,80,128]{2,1,0:T(8,128)(2,1)}), bf16[8,80,128]{2,1,0:T(8,128)(2,1)S(1)}, u32[]{:S(2)}, u32[]{:S(2)}) async-start(bf16[8,80,128]{2,1,0:T(8,128)(2,1)} %get-tuple-element.39), calls=%async_computation.1 | async-start | bytes 327680 | tf_op jit(solution)/shard_map/all_to_all | solution.py:517
  41.9 0.0 collective-permute-done.7
  42.0 0.4 collective-permute-start.8
  42.4 0.0 collective-permute-start.3
  42.4 2.0 %collective-permute-start.5 = (bf16[72,384]{1,0:T(8,128)(2,1)S(1)}, bf16[72,384]{1,0:T(8,128)(2,1)S(1)}, u32[]{:S(2)}, u32[]{:S(2)}) collective-permute-start(bf16[72,384]{1,0:T(8,128)(2,1)S(1)} %get-tuple-element.36), channel_id=1, source_target_pairs={{0,9},{1,10},{2,11},{3,12},{4,13},{5,14},{6,15},{7,8},{8,17},{9,18... | collective-permute-start | bytes 165896 | tf_op jit(solution)/shard_map/ppermute | solution.py:500
  44.4 1.0 %collective-permute-start.4 = (bf16[216,384]{1,0:T(8,128)(2,1)S(1)}, bf16[216,384]{1,0:T(8,128)(2,1)S(1)}, u32[]{:S(2)}, u32[]{:S(2)}) collective-permute-start(bf16[216,384]{1,0:T(8,128)(2,1)S(1)} %get-tuple-element.35), channel_id=1, source_target_pairs={{0,1},{1,2},{2,3},{3,4},{4,5},{5,6},{6,7},{7,0},{8,9},{9,10},{10,1... | collective-permute-start | bytes 497672 | tf_op jit(solution)/shard_map/ppermute | solution.py:499
  45.4 2.0 %all-to-all-done.1.refs_0_ = bf16[8,80,128]{2,1,0:T(8,128)(2,1)S(1)} async-done(((bf16[8,80,128]{2,1,0:T(8,128)(2,1)}), bf16[8,80,128]{2,1,0:T(8,128)(2,1)S(1)}, u32[]{:S(2)}, u32[]{:S(2)}) %all-to-all-start.1) | async-done | bytes 163872 | tf_op jit(solution)/shard_map/all_to_all | solution.py:517
  47.4 0.8 %summed.3 = bf16[16,80,128]{2,1,0:T(8,128)(2,1)} custom-call(bf16[8,80,128]{2,1,0:T(8,128)(2,1)S(1)} %all-to-all-done.1.refs_0_), custom_call_target="tpu_custom_call" | custom-call | tf_op jit(solution)/shard_map/summed/pallas_call | solution.py:410
  48.2 6.1 %all-to-all-start.2 = ((bf16[16,80,128]{2,1,0:T(8,128)(2,1)}), bf16[16,80,128]{2,1,0:T(8,128)(2,1)S(1)}, u32[]{:S(2)}, u32[]{:S(2)}) async-start(bf16[16,80,128]{2,1,0:T(8,128)(2,1)} %summed.3), calls=%async_computation.2 | async-start | bytes 655360 | tf_op jit(solution)/shard_map/all_to_all | solution.py:524
  54.4 1.5 %collective-permute-start.9 = (bf16[320,128]{1,0:T(8,128)(2,1)S(1)}, bf16[320,128]{1,0:T(8,128)(2,1)S(1)}, u32[]{:S(2)}, u32[]{:S(2)}) collective-permute-start(bf16[320,128]{1,0:T(8,128)(2,1)S(1)} %add_convert_fusion.1), channel_id=1, source_target_pairs={{0,64},{8,72},{16,80},{24,88},{32,96},{40,104},{48,112},{56,120},{... | collective-permute-start | bytes 245768 | tf_op jit(solution)/shard_map/ppermute | solution.py:512
  55.9 1.0 %combine.1 = (bf16[4,6,24,192]{3,2,1,0:T(8,128)(2,1)}, bf16[4,6,24,192]{3,2,1,0:T(8,128)(2,1)}) custom-call(bf16[4,6,24,192]{3,2,1,0:T(8,128)(2,1)S(1)} %copy-done, bf16[4,6,24,192]{3,2,1,0:T(8,128)(2,1)S(1)} %copy-done.1, bf16[216,384]{1,0:T(8,128)(2,1)S(1)} %get-tuple-element.28.own_ref, bf16[72,384]{1,0:T(8,128)(2,1)S(1)} %collective-permute-done.3.lonr_ref, ...), custom_call_target="tpu_custom_call" | custom-call | flops 10000000000 | bytes 41943040 | tf_op jit(solution)/shard_map/combine/pallas_call | solution.py:381
  56.9 3.4 %collective-permute-done.9 = bf16[320,128]{1,0:T(8,128)(2,1)S(1)} collective-permute-done((bf16[320,128]{1,0:T(8,128)(2,1)S(1)}, bf16[320,128]{1,0:T(8,128)(2,1)S(1)}, u32[]{:S(2)}, u32[]{:S(2)}) %collective-permute-start.9) | collective-permute-done | bytes 81952 | tf_op jit(solution)/shard_map/ppermute | solution.py:512
  60.4 1.6 %turn.1 = f32[6,2,3312]{2,1,0:T(2,128)} custom-call(bf16[320,128]{1,0:T(8,128)(2,1)S(1)} %add_convert_fusion.tr), custom_call_target="tpu_custom_call" | custom-call | flops 1000000000 | bytes 4194304 | tf_op jit(solution)/shard_map/turn/pallas_call | solution.py:473
  62.0 1.2 %all-to-all-done.2.whole_ref = bf16[16,80,128]{2,1,0:T(8,128)(2,1)S(1)} async-done(((bf16[16,80,128]{2,1,0:T(8,128)(2,1)}), bf16[16,80,128]{2,1,0:T(8,128)(2,1)S(1)}, u32[]{:S(2)}, u32[]{:S(2)}) %all-to-all-start.2) | async-done | bytes 327712 | tf_op jit(solution)/shard_map/all_to_all | solution.py:524
  63.1 0.9 %unpack.1 = (f32[192,576]{1,0:T(8,128)}, f32[192,192]{1,0:T(8,128)}, f32[1,192]{1,0:T(1,128)}) custom-call(bf16[16,80,128]{2,1,0:T(8,128)(2,1)S(1)} %all-to-all-done.2.whole_ref), custom_call_target="tpu_custom_call" | custom-call | tf_op jit(solution)/shard_map/unpack/pallas_call | solution.py:439
  (17 shorter events, 0.1 us)
Async XLA Ops:
  0.6 8.4 %copy-start.2 = (f32[1,2,6,3312]{3,1,2,0:T(2,128)S(1)}, f32[1,2,6,3312]{3,1,2,0:T(2,128)}, u32[]{:S(2)}) copy-start(f32[1,2,6,3312]{3,1,2,0:T(2,128)} %param.11) | copy-start | bytes 476932
  1.9 10.7 %collective-permute-start.1 = (bf16[216,384]{1,0:T(8,128)(2,1)S(1)}, bf16[216,384]{1,0:T(8,128)(2,1)S(1)}, u32[]{:S(2)}, u32[]{:S(2)}) collective-permute-start(bf16[216,384]{1,0:T(8,128)(2,1)S(1)} %get-tuple-element.26), channel_id=1, source_target_pairs={{0,7},{1,0},{2,1},{3,2},{4,3},{5,4},{6,5},{7,6},{8,15},{9,8},{10,9... | collective-permute-start | bytes 497672 | tf_op jit(solution)/shard_map/ppermute | solution.py:499
  7.0 4.1 %collective-permute-start = (bf16[72,384]{1,0:T(8,128)(2,1)S(1)}, bf16[72,384]{1,0:T(8,128)(2,1)S(1)}, u32[]{:S(2)}, u32[]{:S(2)}) collective-permute-start(bf16[72,384]{1,0:T(8,128)(2,1)S(1)} %get-tuple-element.25), channel_id=1, source_target_pairs={{0,120},{8,0},{16,8},{24,16},{32,24},{40,32},{48,40},{56,48},{64,5... | collective-permute-start | bytes 165896 | tf_op jit(solution)/shard_map/ppermute | solution.py:497
  9.1 3.6 %collective-permute-start.2 = (bf16[72,384]{1,0:T(8,128)(2,1)S(1)}, bf16[72,384]{1,0:T(8,128)(2,1)S(1)}, u32[]{:S(2)}, u32[]{:S(2)}) collective-permute-start(bf16[72,384]{1,0:T(8,128)(2,1)S(1)} %get-tuple-element.27), channel_id=1, source_target_pairs={{0,127},{1,120},{2,121},{3,122},{4,123},{5,124},{6,125},{7,126},{8... | collective-permute-start | bytes 165896 | tf_op jit(solution)/shard_map/ppermute | solution.py:500
  9.1 3.6 %copy-start = (bf16[4,6,24,192]{3,2,1,0:T(8,128)(2,1)S(1)}, bf16[4,6,24,192]{3,2,1,0:T(8,128)(2,1)}, u32[]{:S(2)}) copy-start(bf16[4,6,24,192]{3,2,1,0:T(8,128)(2,1)} %air_ref.3) | copy-start | bytes 663556
  9.1 3.6 %copy-start.1 = (bf16[4,6,24,192]{3,2,1,0:T(8,128)(2,1)S(1)}, bf16[4,6,24,192]{3,2,1,0:T(8,128)(2,1)}, u32[]{:S(2)}) copy-start(bf16[4,6,24,192]{3,2,1,0:T(8,128)(2,1)} %up_ref.3) | copy-start | bytes 663556
  9.1 3.6 %copy-start.3 = (bf16[192,576]{1,0:T(8,128)(2,1)S(1)}, bf16[192,576]{1,0:T(8,128)(2,1)}, u32[]{:S(2)}) copy-start(bf16[192,576]{1,0:T(8,128)(2,1)} %wqkv_ref.1) | copy-start | bytes 663556
  9.1 3.6 %copy-start.4 = (bf16[192,192]{1,0:T(8,128)(2,1)S(1)}, bf16[192,192]{1,0:T(8,128)(2,1)}, u32[]{:S(2)}) copy-start(bf16[192,192]{1,0:T(8,128)(2,1)} %wproj_ref.1) | copy-start | bytes 221188
  11.1 1.5 %copy-start.5 = (f32[192]{0:T(256)S(1)}, f32[192]{0:T(256)}, u32[]{:S(2)}) copy-start(f32[192]{0:T(256)} %param.8) | copy-start | bytes 2308
  34.4 1.3 %collective-permute-start.6 = (bf16[320,128]{1,0:T(8,128)(2,1)S(1)}, bf16[320,128]{1,0:T(8,128)(2,1)S(1)}, u32[]{:S(2)}, u32[]{:S(2)}) collective-permute-start(bf16[320,128]{1,0:T(8,128)(2,1)S(1)} %get-tuple-element.43), channel_id=1, source_target_pairs={{0,8},{8,0},{16,24},{24,16},{32,40},{40,32},{48,56},{56,48},{64,72... | collective-permute-start | bytes 245768 | tf_op jit(solution)/shard_map/ppermute | solution.py:512
  35.7 6.3 %collective-permute-start.7 = (bf16[320,128]{1,0:T(8,128)(2,1)S(1)}, bf16[320,128]{1,0:T(8,128)(2,1)S(1)}, u32[]{:S(2)}, u32[]{:S(2)}) collective-permute-start(bf16[320,128]{1,0:T(8,128)(2,1)S(1)} %add_convert_fusion.3), channel_id=1, source_target_pairs={{0,16},{8,24},{16,0},{24,8},{32,48},{40,56},{48,32},{56,40},{64,80... | collective-permute-start | bytes 245768 | tf_op jit(solution)/shard_map/ppermute | solution.py:512
  37.1 10.3 %all-to-all-start.1 = ((bf16[8,80,128]{2,1,0:T(8,128)(2,1)}), bf16[8,80,128]{2,1,0:T(8,128)(2,1)S(1)}, u32[]{:S(2)}, u32[]{:S(2)}) async-start(bf16[8,80,128]{2,1,0:T(8,128)(2,1)} %get-tuple-element.39), calls=%async_computation.1 | async-start | bytes 327680 | tf_op jit(solution)/shard_map/all_to_all | solution.py:517
  42.0 12.3 %collective-permute-start.8 = (bf16[320,128]{1,0:T(8,128)(2,1)S(1)}, bf16[320,128]{1,0:T(8,128)(2,1)S(1)}, u32[]{:S(2)}, u32[]{:S(2)}) collective-permute-start(bf16[320,128]{1,0:T(8,128)(2,1)S(1)} %add_convert_fusion.2), channel_id=1, source_target_pairs={{0,32},{8,40},{16,48},{24,56},{32,0},{40,8},{48,16},{56,24},{64,96... | collective-permute-start | bytes 245768 | tf_op jit(solution)/shard_map/ppermute | solution.py:512
  42.4 13.5 %collective-permute-start.3 = (bf16[72,384]{1,0:T(8,128)(2,1)S(1)}, bf16[72,384]{1,0:T(8,128)(2,1)S(1)}, u32[]{:S(2)}, u32[]{:S(2)}) collective-permute-start(bf16[72,384]{1,0:T(8,128)(2,1)S(1)} %get-tuple-element.34), channel_id=1, source_target_pairs={{0,8},{8,16},{16,24},{24,32},{32,40},{40,48},{48,56},{56,64},{64,7... | collective-permute-start | bytes 165896 | tf_op jit(solution)/shard_map/ppermute | solution.py:497
  42.4 13.5 %collective-permute-start.5 = (bf16[72,384]{1,0:T(8,128)(2,1)S(1)}, bf16[72,384]{1,0:T(8,128)(2,1)S(1)}, u32[]{:S(2)}, u32[]{:S(2)}) collective-permute-start(bf16[72,384]{1,0:T(8,128)(2,1)S(1)} %get-tuple-element.36), channel_id=1, source_target_pairs={{0,9},{1,10},{2,11},{3,12},{4,13},{5,14},{6,15},{7,8},{8,17},{9,18... | collective-permute-start | bytes 165896 | tf_op jit(solution)/shard_map/ppermute | solution.py:500
  44.4 11.5 %collective-permute-start.4 = (bf16[216,384]{1,0:T(8,128)(2,1)S(1)}, bf16[216,384]{1,0:T(8,128)(2,1)S(1)}, u32[]{:S(2)}, u32[]{:S(2)}) collective-permute-start(bf16[216,384]{1,0:T(8,128)(2,1)S(1)} %get-tuple-element.35), channel_id=1, source_target_pairs={{0,1},{1,2},{2,3},{3,4},{4,5},{5,6},{6,7},{7,0},{8,9},{9,10},{10,1... | collective-permute-start | bytes 497672 | tf_op jit(solution)/shard_map/ppermute | solution.py:499
  48.2 14.9 %all-to-all-start.2 = ((bf16[16,80,128]{2,1,0:T(8,128)(2,1)}), bf16[16,80,128]{2,1,0:T(8,128)(2,1)S(1)}, u32[]{:S(2)}, u32[]{:S(2)}) async-start(bf16[16,80,128]{2,1,0:T(8,128)(2,1)} %summed.3), calls=%async_computation.2 | async-start | bytes 655360 | tf_op jit(solution)/shard_map/all_to_all | solution.py:524
  54.4 6.0 %collective-permute-start.9 = (bf16[320,128]{1,0:T(8,128)(2,1)S(1)}, bf16[320,128]{1,0:T(8,128)(2,1)S(1)}, u32[]{:S(2)}, u32[]{:S(2)}) collective-permute-start(bf16[320,128]{1,0:T(8,128)(2,1)S(1)} %add_convert_fusion.1), channel_id=1, source_target_pairs={{0,64},{8,72},{16,80},{24,88},{32,96},{40,104},{48,112},{56,120},{... | collective-permute-start | bytes 245768 | tf_op jit(solution)/shard_map/ppermute | solution.py:512

commit v5 on v4

--- a/solution.py
+++ b/solution.py
@@ -64,12 +64,12 @@
 
 
 def whole_rows(src):
-    return jnp.concatenate([src[:TOK], src[TOK:][:, :64]], axis=1)
+    return jnp.concatenate([src[:TOK], src[TOK : 2 * TOK][:, :64]], axis=1)
 
 
 def hold(dst, rows):
     dst[:TOK] = rows[:, :128]
-    dst[TOK:, :64] = rows[:, 128:]
+    dst[TOK : 2 * TOK, :64] = rows[:, 128:]
 
 
 def joined(state, up):
@@ -108,9 +108,9 @@
 
 
 HALOS = [
-    jax.ShapeDtypeStruct((72, 2 * C), bf16),
-    jax.ShapeDtypeStruct((216, 2 * C), bf16),
-    jax.ShapeDtypeStruct((72, 2 * C), bf16),
+    jax.ShapeDtypeStruct((80, 2 * C), bf16),
+    jax.ShapeDtypeStruct((224, 2 * C), bf16),
+    jax.ShapeDtypeStruct((80, 2 * C), bf16),
 ]
 
 
@@ -347,8 +347,8 @@
             jax.ShapeDtypeStruct((TABLE, 128), bf16),
         ],
         scratch_shapes=[
-            pltpu.VMEM((2 * TOK, 128), f32),
-            pltpu.VMEM((2 * TOK, 128), f32),
+            pltpu.VMEM((2 * TOK + 128, 128), f32),
+            pltpu.VMEM((2 * TOK + 128, 128), f32),
             pltpu.VMEM((2, WIN, HEADS * WIN), f32),
         ]
         + [tok(bf16)] * 8

time: 64.4 us -> 64.6 us (level)
  no operation moved by 1% of the time
where the time goes in v5:
time: 64.6 us; the launch traced here: 64.2 us
  starting transfers between devices  24.7 us (38%)
  blocking collectives  15.8 us (24%)
  Pallas kernels  13.4 us (21%)
  waiting for transfers between devices  9.38 us (15%)
  between operations  0.78 us (1%)
    all_to_all x1, blocking collectives, on_device(): lax.all_to_all(grads, SCATTER, split_axis=0, concat_axis=0, tiled=True)  15.8 us
    all_to_all x1, starting transfers between devices, on_device(): lax.all_to_all(copies, SCATTER, split_axis=0, concat_axis=0, tiled=True)  6.25 us
    ppermute x2, starting transfers between devices, neighbour(): lax.ppermute(array, LAT, [(i, (i + lat_by) % lats) for i in range(lats)])  6.02 us
    pallas_call x1, Pallas kernels, run_main(): pl.pallas_call(main_kernel, in_specs=[vmem] * 9, out_specs=[vmem] * 6, ou...  5.22 us
    all_to_all x1, starting transfers between devices, on_device(): lax.all_to_all(copies, REST, split_axis=0, concat_axis=0, tiled=True)  4.83 us
    ppermute x4, waiting for transfers between devices, paired(): other = lax.ppermute(entries, LON, [(i, i ^ step) for i in range(lons)])  4.73 us
    ppermute x4, starting transfers between devices, paired(): other = lax.ppermute(entries, LON, [(i, i ^ step) for i in range(lons)])  3.41 us
    ppermute x2, starting transfers between devices, neighbour(): lax.ppermute(array, LON + LAT, pairs_of((lons, lats), lon_by, lat_by))  2.14 us
  transfers between devices with their start and end apart: 12, of which 5 were waited for; matrix products, arithmetic and copies ran while one was open for 0% of the time, Pallas kernels for 8%

profile of v5, /device:TPU:2, one launch (start us, length us, event | category | flops | bytes accessed | tf_op | source)
XLA Modules:
  0.0 64.2 jit_solution(8665186532886576863)
XLA Ops:
  0.6 1.3 %pack.1 = (bf16[80,384]{1,0:T(8,128)(2,1)S(1)}, bf16[224,384]{1,0:T(8,128)(2,1)S(1)}, bf16[80,384]{1,0:T(8,128)(2,1)S(1)}) custom-call(bf16[4,6,24,192]{3,2,1,0:T(8,128)(2,1)} %air_ref.3, bf16[4,6,24,192]{3,2,1,0:T(8,128)(2,1)} %up_ref.3), custom_call_target="tpu_custom_call" | custom-call | tf_op jit(solution)/shard_map/pack/pallas_call | solution.py:120
  1.9 5.1 %collective-permute-start.1 = (bf16[224,384]{1,0:T(8,128)(2,1)S(1)}, bf16[224,384]{1,0:T(8,128)(2,1)S(1)}, u32[]{:S(2)}, u32[]{:S(2)}) collective-permute-start(bf16[224,384]{1,0:T(8,128)(2,1)S(1)} %get-tuple-element.26), channel_id=1, source_target_pairs={{0,7},{1,0},{2,1},{3,2},{4,3},{5,4},{6,5},{7,6},{8,15},{9,8},{10,9... | collective-permute-start | bytes 516104 | tf_op jit(solution)/shard_map/ppermute | solution.py:499
  7.0 2.0 %collective-permute-start = (bf16[80,384]{1,0:T(8,128)(2,1)S(1)}, bf16[80,384]{1,0:T(8,128)(2,1)S(1)}, u32[]{:S(2)}, u32[]{:S(2)}) collective-permute-start(bf16[80,384]{1,0:T(8,128)(2,1)S(1)} %get-tuple-element.25), channel_id=1, source_target_pairs={{0,120},{8,0},{16,8},{24,16},{32,24},{40,32},{48,40},{56,48},{64,5... | collective-permute-start | bytes 184328 | tf_op jit(solution)/shard_map/ppermute | solution.py:497
  9.1 0.0 collective-permute-start.2
  9.1 0.0 copy-start.3
  9.1 0.0 copy-start.4
  9.1 2.0 %prep.1.bias = f32[2,144,864]{2,1,0:T(8,128)S(1)} custom-call(s32[1]{0:T(128)} %bitcast.1.last_ref, f32[6,2,3312]{2,1,0:T(2,128)S(1)} %bitcast.9), custom_call_target="tpu_custom_call" | custom-call | flops 100000000 | bytes 2097152 | tf_op jit(solution)/shard_map/prep/pallas_call | solution.py:197
  11.1 0.0 copy-start.5
  11.2 0.0 collective-permute-done.lonh_ref
  11.2 1.5 %collective-permute-done.2.corh_ref = bf16[80,384]{1,0:T(8,128)(2,1)S(1)} collective-permute-done((bf16[80,384]{1,0:T(8,128)(2,1)S(1)}, bf16[80,384]{1,0:T(8,128)(2,1)S(1)}, u32[]{:S(2)}, u32[]{:S(2)}) %collective-permute-start.2) | collective-permute-done | bytes 61472 | tf_op jit(solution)/shard_map/ppermute | solution.py:500
  12.7 5.2 %sublayer.1 = (bf16[224,384]{1,0:T(8,128)(2,1)S(1)}, bf16[80,384]{1,0:T(8,128)(2,1)S(1)}, bf16[224,384]{1,0:T(8,128)(2,1)S(1)}, bf16[80,384]{1,0:T(8,128)(2,1)S(...) custom-call(bf16[4,6,24,192]{3,2,1,0:T(8,128)(2,1)S(1)} %copy-done, ...), custom_call_target="tpu_custom_call" | custom-call | flops 1000000000 | bytes 4194304 | tf_op jit(solution)/shard_map/sublayer/pallas_call | solution.py:339
  18.0 15.8 %all_to_all.15.refs_0_ = bf16[16,80,128]{2,1,0:T(8,128)(2,1)S(1)} all-to-all(bf16[16,80,128]{2,1,0:T(8,128)(2,1)S(1)} %get-tuple-element.29), channel_id=1, replica_groups=mesh['x'=4,'yh'=2,'core'=2,'yl'=2,'z'=4] {'yh','yl','z'}, dimensions={0} | all-to-all | bytes 655360 | tf_op jit(solution)/shard_map/all_to_all | solution.py:515
  33.8 0.7 %summed.2 = (bf16[8,80,128]{2,1,0:T(8,128)(2,1)}, bf16[320,128]{1,0:T(8,128)(2,1)S(1)}, bf16[224,384]{1,0:T(8,128)(2,1)S(1)}, bf16[80,384]{1,0:T(8,128)(2,1)S(1)}, bf16[80,384]{1,0:T(8,128)(2,1)S(1)}) custom-call(bf16[16,80,128]{2,1,0:T(8,128)(2,1)S(1)} %all_to_all.15.refs_0_, ...), custom_call_target="tpu_custom_call", output_to_operand_aliasing={{1}: (1, {}), {2}: (2, {}), {3}: (3, {}), {4}: (4, {})} | custom-call | tf_op jit(solution)/shard_map/summed/pallas_call | solution.py:410
  34.5 1.3 %collective-permute-done.6 = bf16[320,128]{1,0:T(8,128)(2,1)S(1)} collective-permute-done((bf16[320,128]{1,0:T(8,128)(2,1)S(1)}, bf16[320,128]{1,0:T(8,128)(2,1)S(1)}, u32[]{:S(2)}, u32[]{:S(2)}) %collective-permute-start.6) | collective-permute-done | bytes 81952 | tf_op jit(solution)/shard_map/ppermute | solution.py:512
  35.8 1.4 %collective-permute-start.7 = (bf16[320,128]{1,0:T(8,128)(2,1)S(1)}, bf16[320,128]{1,0:T(8,128)(2,1)S(1)}, u32[]{:S(2)}, u32[]{:S(2)}) collective-permute-start(bf16[320,128]{1,0:T(8,128)(2,1)S(1)} %add_convert_fusion.3), channel_id=1, source_target_pairs={{0,16},{8,24},{16,0},{24,8},{32,48},{40,56},{48,32},{56,40},{64,80... | collective-permute-start | bytes 245768 | tf_op jit(solution)/shard_map/ppermute | solution.py:512
  37.2 4.8 %all-to-all-start.1 = ((bf16[8,80,128]{2,1,0:T(8,128)(2,1)}), bf16[8,80,128]{2,1,0:T(8,128)(2,1)S(1)}, u32[]{:S(2)}, u32[]{:S(2)}) async-start(bf16[8,80,128]{2,1,0:T(8,128)(2,1)} %get-tuple-element.39), calls=%async_computation.1 | async-start | bytes 327680 | tf_op jit(solution)/shard_map/all_to_all | solution.py:517
  42.0 0.5 collective-permute-start.8
  42.5 2.1 %collective-permute-start.5 = (bf16[80,384]{1,0:T(8,128)(2,1)S(1)}, bf16[80,384]{1,0:T(8,128)(2,1)S(1)}, u32[]{:S(2)}, u32[]{:S(2)}) collective-permute-start(bf16[80,384]{1,0:T(8,128)(2,1)S(1)} %get-tuple-element.36), channel_id=1, source_target_pairs={{0,9},{1,10},{2,11},{3,12},{4,13},{5,14},{6,15},{7,8},{8,17},{9,18... | collective-permute-start | bytes 184328 | tf_op jit(solution)/shard_map/ppermute | solution.py:500
  44.7 0.9 %collective-permute-start.4 = (bf16[224,384]{1,0:T(8,128)(2,1)S(1)}, bf16[224,384]{1,0:T(8,128)(2,1)S(1)}, u32[]{:S(2)}, u32[]{:S(2)}) collective-permute-start(bf16[224,384]{1,0:T(8,128)(2,1)S(1)} %get-tuple-element.35), channel_id=1, source_target_pairs={{0,1},{1,2},{2,3},{3,4},{4,5},{5,6},{6,7},{7,0},{8,9},{9,10},{10,1... | collective-permute-start | bytes 516104 | tf_op jit(solution)/shard_map/ppermute | solution.py:499
  45.6 1.9 %all-to-all-done.1.refs_0_ = bf16[8,80,128]{2,1,0:T(8,128)(2,1)S(1)} async-done(((bf16[8,80,128]{2,1,0:T(8,128)(2,1)}), bf16[8,80,128]{2,1,0:T(8,128)(2,1)S(1)}, u32[]{:S(2)}, u32[]{:S(2)}) %all-to-all-start.1) | async-done | bytes 163872 | tf_op jit(solution)/shard_map/all_to_all | solution.py:517
  47.5 0.8 %summed.3 = bf16[16,80,128]{2,1,0:T(8,128)(2,1)} custom-call(bf16[8,80,128]{2,1,0:T(8,128)(2,1)S(1)} %all-to-all-done.1.refs_0_), custom_call_target="tpu_custom_call" | custom-call | tf_op jit(solution)/shard_map/summed/pallas_call | solution.py:410
  48.3 6.3 %all-to-all-start.2 = ((bf16[16,80,128]{2,1,0:T(8,128)(2,1)}), bf16[16,80,128]{2,1,0:T(8,128)(2,1)S(1)}, u32[]{:S(2)}, u32[]{:S(2)}) async-start(bf16[16,80,128]{2,1,0:T(8,128)(2,1)} %summed.3), calls=%async_computation.2 | async-start | bytes 655360 | tf_op jit(solution)/shard_map/all_to_all | solution.py:524
  54.5 0.0 collective-permute-done.8
  54.6 1.5 %collective-permute-start.9 = (bf16[320,128]{1,0:T(8,128)(2,1)S(1)}, bf16[320,128]{1,0:T(8,128)(2,1)S(1)}, u32[]{:S(2)}, u32[]{:S(2)}) collective-permute-start(bf16[320,128]{1,0:T(8,128)(2,1)S(1)} %add_convert_fusion.1), channel_id=1, source_target_pairs={{0,64},{8,72},{16,80},{24,88},{32,96},{40,104},{48,112},{56,120},{... | collective-permute-start | bytes 245768 | tf_op jit(solution)/shard_map/ppermute | solution.py:512
  56.1 0.0 collective-permute-done.3.lonr_ref
  56.1 0.0 collective-permute-done.5.corr_ref
  56.1 0.0 collective-permute-done.4.latr_ref
  56.1 1.0 %combine.1 = (bf16[4,6,24,192]{3,2,1,0:T(8,128)(2,1)}, bf16[4,6,24,192]{3,2,1,0:T(8,128)(2,1)}) custom-call(bf16[4,6,24,192]{3,2,1,0:T(8,128)(2,1)S(1)} %copy-done, bf16[4,6,24,192]{3,2,1,0:T(8,128)(2,1)S(1)} %copy-done.1, bf16[224,384]{1,0:T(8,128)(2,1)S(1)} %get-tuple-element.28.own_ref, bf16[80,384]{1,0:T(8,128)(2,1)S(1)} %collective-permute-done.3.lonr_ref, ...), custom_call_target="tpu_custom_call" | custom-call | flops 10000000000 | bytes 41943040 | tf_op jit(solution)/shard_map/combine/pallas_call | solution.py:381
  57.1 3.4 %collective-permute-done.9 = bf16[320,128]{1,0:T(8,128)(2,1)S(1)} collective-permute-done((bf16[320,128]{1,0:T(8,128)(2,1)S(1)}, bf16[320,128]{1,0:T(8,128)(2,1)S(1)}, u32[]{:S(2)}, u32[]{:S(2)}) %collective-permute-start.9) | collective-permute-done | bytes 81952 | tf_op jit(solution)/shard_map/ppermute | solution.py:512
  60.6 1.6 %turn.1 = f32[6,2,3312]{2,1,0:T(2,128)} custom-call(bf16[320,128]{1,0:T(8,128)(2,1)S(1)} %add_convert_fusion.tr), custom_call_target="tpu_custom_call" | custom-call | flops 1000000000 | bytes 4194304 | tf_op jit(solution)/shard_map/turn/pallas_call | solution.py:473
  62.2 1.2 %all-to-all-done.2.whole_ref = bf16[16,80,128]{2,1,0:T(8,128)(2,1)S(1)} async-done(((bf16[16,80,128]{2,1,0:T(8,128)(2,1)}), bf16[16,80,128]{2,1,0:T(8,128)(2,1)S(1)}, u32[]{:S(2)}, u32[]{:S(2)}) %all-to-all-start.2) | async-done | bytes 327712 | tf_op jit(solution)/shard_map/all_to_all | solution.py:524
  63.3 0.9 %unpack.1 = (f32[192,576]{1,0:T(8,128)}, f32[192,192]{1,0:T(8,128)}, f32[1,192]{1,0:T(1,128)}) custom-call(bf16[16,80,128]{2,1,0:T(8,128)(2,1)S(1)} %all-to-all-done.2.whole_ref), custom_call_target="tpu_custom_call" | custom-call | tf_op jit(solution)/shard_map/unpack/pallas_call | solution.py:439
  (17 shorter events, 0.1 us)
Async XLA Ops:
  0.6 8.4 %copy-start.2 = (f32[1,2,6,3312]{3,1,2,0:T(2,128)S(1)}, f32[1,2,6,3312]{3,1,2,0:T(2,128)}, u32[]{:S(2)}) copy-start(f32[1,2,6,3312]{3,1,2,0:T(2,128)} %param.11) | copy-start | bytes 476932
  1.9 10.8 %collective-permute-start.1 = (bf16[224,384]{1,0:T(8,128)(2,1)S(1)}, bf16[224,384]{1,0:T(8,128)(2,1)S(1)}, u32[]{:S(2)}, u32[]{:S(2)}) collective-permute-start(bf16[224,384]{1,0:T(8,128)(2,1)S(1)} %get-tuple-element.26), channel_id=1, source_target_pairs={{0,7},{1,0},{2,1},{3,2},{4,3},{5,4},{6,5},{7,6},{8,15},{9,8},{10,9... | collective-permute-start | bytes 516104 | tf_op jit(solution)/shard_map/ppermute | solution.py:499
  7.0 4.1 %collective-permute-start = (bf16[80,384]{1,0:T(8,128)(2,1)S(1)}, bf16[80,384]{1,0:T(8,128)(2,1)S(1)}, u32[]{:S(2)}, u32[]{:S(2)}) collective-permute-start(bf16[80,384]{1,0:T(8,128)(2,1)S(1)} %get-tuple-element.25), channel_id=1, source_target_pairs={{0,120},{8,0},{16,8},{24,16},{32,24},{40,32},{48,40},{56,48},{64,5... | collective-permute-start | bytes 184328 | tf_op jit(solution)/shard_map/ppermute | solution.py:497
  9.1 3.6 %collective-permute-start.2 = (bf16[80,384]{1,0:T(8,128)(2,1)S(1)}, bf16[80,384]{1,0:T(8,128)(2,1)S(1)}, u32[]{:S(2)}, u32[]{:S(2)}) collective-permute-start(bf16[80,384]{1,0:T(8,128)(2,1)S(1)} %get-tuple-element.27), channel_id=1, source_target_pairs={{0,127},{1,120},{2,121},{3,122},{4,123},{5,124},{6,125},{7,126},{8... | collective-permute-start | bytes 184328 | tf_op jit(solution)/shard_map/ppermute | solution.py:500
  9.1 3.6 %copy-start = (bf16[4,6,24,192]{3,2,1,0:T(8,128)(2,1)S(1)}, bf16[4,6,24,192]{3,2,1,0:T(8,128)(2,1)}, u32[]{:S(2)}) copy-start(bf16[4,6,24,192]{3,2,1,0:T(8,128)(2,1)} %air_ref.3) | copy-start | bytes 663556
  9.1 3.6 %copy-start.1 = (bf16[4,6,24,192]{3,2,1,0:T(8,128)(2,1)S(1)}, bf16[4,6,24,192]{3,2,1,0:T(8,128)(2,1)}, u32[]{:S(2)}) copy-start(bf16[4,6,24,192]{3,2,1,0:T(8,128)(2,1)} %up_ref.3) | copy-start | bytes 663556
  9.1 3.6 %copy-start.3 = (bf16[192,576]{1,0:T(8,128)(2,1)S(1)}, bf16[192,576]{1,0:T(8,128)(2,1)}, u32[]{:S(2)}) copy-start(bf16[192,576]{1,0:T(8,128)(2,1)} %wqkv_ref.1) | copy-start | bytes 663556
  9.1 3.6 %copy-start.4 = (bf16[192,192]{1,0:T(8,128)(2,1)S(1)}, bf16[192,192]{1,0:T(8,128)(2,1)}, u32[]{:S(2)}) copy-start(bf16[192,192]{1,0:T(8,128)(2,1)} %wproj_ref.1) | copy-start | bytes 221188
  11.1 1.6 %copy-start.5 = (f32[192]{0:T(256)S(1)}, f32[192]{0:T(256)}, u32[]{:S(2)}) copy-start(f32[192]{0:T(256)} %param.8) | copy-start | bytes 2308
  34.5 1.3 %collective-permute-start.6 = (bf16[320,128]{1,0:T(8,128)(2,1)S(1)}, bf16[320,128]{1,0:T(8,128)(2,1)S(1)}, u32[]{:S(2)}, u32[]{:S(2)}) collective-permute-start(bf16[320,128]{1,0:T(8,128)(2,1)S(1)} %get-tuple-element.43), channel_id=1, source_target_pairs={{0,8},{8,0},{16,24},{24,16},{32,40},{40,32},{48,56},{56,48},{64,72... | collective-permute-start | bytes 245768 | tf_op jit(solution)/shard_map/ppermute | solution.py:512
  35.8 6.2 %collective-permute-start.7 = (bf16[320,128]{1,0:T(8,128)(2,1)S(1)}, bf16[320,128]{1,0:T(8,128)(2,1)S(1)}, u32[]{:S(2)}, u32[]{:S(2)}) collective-permute-start(bf16[320,128]{1,0:T(8,128)(2,1)S(1)} %add_convert_fusion.3), channel_id=1, source_target_pairs={{0,16},{8,24},{16,0},{24,8},{32,48},{40,56},{48,32},{56,40},{64,80... | collective-permute-start | bytes 245768 | tf_op jit(solution)/shard_map/ppermute | solution.py:512
  37.2 10.3 %all-to-all-start.1 = ((bf16[8,80,128]{2,1,0:T(8,128)(2,1)}), bf16[8,80,128]{2,1,0:T(8,128)(2,1)S(1)}, u32[]{:S(2)}, u32[]{:S(2)}) async-start(bf16[8,80,128]{2,1,0:T(8,128)(2,1)} %get-tuple-element.39), calls=%async_computation.1 | async-start | bytes 327680 | tf_op jit(solution)/shard_map/all_to_all | solution.py:517
  42.0 12.5 %collective-permute-start.8 = (bf16[320,128]{1,0:T(8,128)(2,1)S(1)}, bf16[320,128]{1,0:T(8,128)(2,1)S(1)}, u32[]{:S(2)}, u32[]{:S(2)}) collective-permute-start(bf16[320,128]{1,0:T(8,128)(2,1)S(1)} %add_convert_fusion.2), channel_id=1, source_target_pairs={{0,32},{8,40},{16,48},{24,56},{32,0},{40,8},{48,16},{56,24},{64,96... | collective-permute-start | bytes 245768 | tf_op jit(solution)/shard_map/ppermute | solution.py:512
  42.5 13.6 %collective-permute-start.3 = (bf16[80,384]{1,0:T(8,128)(2,1)S(1)}, bf16[80,384]{1,0:T(8,128)(2,1)S(1)}, u32[]{:S(2)}, u32[]{:S(2)}) collective-permute-start(bf16[80,384]{1,0:T(8,128)(2,1)S(1)} %get-tuple-element.34), channel_id=1, source_target_pairs={{0,8},{8,16},{16,24},{24,32},{32,40},{40,48},{48,56},{56,64},{64,7... | collective-permute-start | bytes 184328 | tf_op jit(solution)/shard_map/ppermute | solution.py:497
  42.5 13.6 %collective-permute-start.5 = (bf16[80,384]{1,0:T(8,128)(2,1)S(1)}, bf16[80,384]{1,0:T(8,128)(2,1)S(1)}, u32[]{:S(2)}, u32[]{:S(2)}) collective-permute-start(bf16[80,384]{1,0:T(8,128)(2,1)S(1)} %get-tuple-element.36), channel_id=1, source_target_pairs={{0,9},{1,10},{2,11},{3,12},{4,13},{5,14},{6,15},{7,8},{8,17},{9,18... | collective-permute-start | bytes 184328 | tf_op jit(solution)/shard_map/ppermute | solution.py:500
  44.7 11.4 %collective-permute-start.4 = (bf16[224,384]{1,0:T(8,128)(2,1)S(1)}, bf16[224,384]{1,0:T(8,128)(2,1)S(1)}, u32[]{:S(2)}, u32[]{:S(2)}) collective-permute-start(bf16[224,384]{1,0:T(8,128)(2,1)S(1)} %get-tuple-element.35), channel_id=1, source_target_pairs={{0,1},{1,2},{2,3},{3,4},{4,5},{5,6},{6,7},{7,0},{8,9},{9,10},{10,1... | collective-permute-start | bytes 516104 | tf_op jit(solution)/shard_map/ppermute | solution.py:499
  48.3 15.1 %all-to-all-start.2 = ((bf16[16,80,128]{2,1,0:T(8,128)(2,1)}), bf16[16,80,128]{2,1,0:T(8,128)(2,1)S(1)}, u32[]{:S(2)}, u32[]{:S(2)}) async-start(bf16[16,80,128]{2,1,0:T(8,128)(2,1)} %summed.3), calls=%async_computation.2 | async-start | bytes 655360 | tf_op jit(solution)/shard_map/all_to_all | solution.py:524
  54.6 6.0 %collective-permute-start.9 = (bf16[320,128]{1,0:T(8,128)(2,1)S(1)}, bf16[320,128]{1,0:T(8,128)(2,1)S(1)}, u32[]{:S(2)}, u32[]{:S(2)}) collective-permute-start(bf16[320,128]{1,0:T(8,128)(2,1)S(1)} %add_convert_fusion.1), channel_id=1, source_target_pairs={{0,64},{8,72},{16,80},{24,88},{32,96},{40,104},{48,112},{56,120},{... | collective-permute-start | bytes 245768 | tf_op jit(solution)/shard_map/ppermute | solution.py:512
